TPU v7x, 512 devices: a whole 4x4x16 slice. The times are simulated.
512 devices in a mesh: ctx: 64 (over y, z), tp: 8 (over x, core).
Axes of the slice: x: 4, y: 4, z: 16, core: 2. Of those that a mesh axis runs over, the one named last changes fastest.
Arguments:
- inputs: bfloat16 [3, 16384, 8192], P(None, 'ctx', 'tp'), may hold values from -6 to 6
- cotangent: bfloat16 [16384, 8192], P('ctx', 'tp'), may hold values from -140 to 140
- short_filter: float32 [3, 7, 8192], P(None, None, 'tp'), may hold values from -2 to 2
- residue: float32 [16, 8192], P(None, 'tp'), may hold values from -0.22 to 0.22
- decay_rate: float32 [16, 8192], P(None, 'tp'), may hold values from 6.1035156e-06 to 0.04
Outputs:
- grad_inputs: bfloat16 [3, 16384, 8192], P(None, 'ctx', 'tp')
- grad_short: float32 [3, 7, 8192], P(None, None, 'tp')
All inputs are finite; a program needn't handle non-finite values.
Results may differ from a plain program's by a relative error of at most 0.0057.
Values may be sent and summed in bfloat16 or wider, within the bound.
No kernel may reach another device: no remote copies, remote signals or barrier semaphores. Data moves between devices by JAX's collectives and lax.ppermute only.
A program may use at most 128 MiB of HBM per device.

v0:
```python
import functools
import math

import jax
import jax.numpy as jnp
from jax import lax
from jax.experimental import pallas as pl
from jax.experimental.pallas import tpu as pltpu
from jax.sharding import PartitionSpec as P

LANES = 128
SUBS = 8
HALO = 8
F32 = jnp.float32
BF16 = jnp.bfloat16


def sub_index():
    return lax.broadcasted_iota(jnp.int32, (SUBS, LANES), 0)


def step_major(row_count, inverse):
    kept = lax.broadcasted_iota(jnp.int32, (row_count, row_count), 1 if inverse else 0)
    time = lax.broadcasted_iota(jnp.int32, (row_count, row_count), 0 if inverse else 1)
    source = (kept & (SUBS - 1)) * (row_count // SUBS) + (kept >> 3)
    return jnp.where(source == time, 1.0, 0.0).astype(BF16)


def spread(row):
    return jnp.broadcast_to(row, (SUBS, LANES))


def lanes_of(group):
    return pl.ds(group * LANES, LANES)


def load_steps(perm, x_ref, prev_ref, held, part, row_count, lead):
    steps = row_count // SUBS
    held[part, pl.ds(lead * SUBS, row_count), :] = jnp.dot(
        perm, x_ref[part], preferred_element_type=F32
    )
    early = prev_ref[part].astype(F32)
    for group in range(held.shape[2] // LANES):
        for step in range(lead):
            late = held[part, pl.ds((steps + step) * SUBS, SUBS), lanes_of(group)]
            row = HALO - lead + step
            first = early[row : row + 1, group * LANES : (group + 1) * LANES]
            held[part, pl.ds(step * SUBS, SUBS), lanes_of(group)] = jnp.where(
                sub_index() == 0, spread(first), pltpu.roll(late, 1, 0)
            )


def mix_kernel(
    x_ref, prev_ref, cot_ref, filt_ref, rate_ref,
    kv_ref, gated_ref, gradm_ref, state_ref,
    held, cot_held, perm_ref,
):
    row_count = cot_ref.shape[0]
    taps = filt_ref.shape[1]
    modes = rate_ref.shape[0]
    lead = taps - 1
    steps = row_count // SUBS
    groups = cot_ref.shape[1] // LANES

    @pl.when(pl.program_id(0) == 0)
    def _():
        perm_ref[...] = step_major(row_count, False)

    perm = perm_ref[...]
    for part in range(3):
        load_steps(perm, x_ref, prev_ref, held, part, row_count, lead)
    cot_held[...] = jnp.dot(perm, cot_ref[...], preferred_element_type=F32)
    chunk = 4 * SUBS
    for group in range(groups):
        lanes = lanes_of(group)
        taps_of = [
            [filt_ref[part, pl.ds(k, 1), lanes] for k in range(taps)] for part in range(3)
        ]

        def mix_chunk(index, carry):
            base = pl.multiple_of(index * chunk, chunk)
            mixed = []
            for part in range(3):
                total = taps_of[part][0] * held[part, pl.ds(base + lead * SUBS, chunk), lanes]
                for k in range(1, taps):
                    total += (
                        taps_of[part][k]
                        * held[part, pl.ds(base + (lead - k) * SUBS, chunk), lanes]
                    )
                mixed.append(total)
            rows = pl.ds(base, chunk)
            kv_ref[0, rows, lanes] = mixed[1]
            kv_ref[1, rows, lanes] = mixed[2]
            gated_ref[rows, lanes] = (mixed[1] * mixed[2]).astype(BF16).astype(F32)
            gradm_ref[rows, lanes] = (
                (cot_held[rows, lanes] * mixed[0]).astype(BF16).astype(F32)
            )
            return carry

        lax.fori_loop(0, row_count // chunk, mix_chunk, 0)
        decay = [spread(jnp.exp(-rate_ref[pl.ds(n, 1), lanes])) for n in range(modes)]

        def gather_step(step, carry):
            ends, starts = carry
            ahead = gated_ref[pl.ds(pl.multiple_of(step * SUBS, SUBS), SUBS), lanes]
            behind = gradm_ref[
                pl.ds(pl.multiple_of((steps - 1 - step) * SUBS, SUBS), SUBS), lanes
            ]
            return (
                [e * d + ahead for e, d in zip(ends, decay)],
                [s * d + behind for s, d in zip(starts, decay)],
            )

        zero = jnp.zeros((SUBS, LANES), F32)
        ends, starts = lax.fori_loop(
            0, steps, gather_step, ([zero] * modes, [zero] * modes), unroll=4
        )
        place = pl.ds(pl.program_id(0) * groups + group, 1)
        seg = sub_index().astype(F32) * steps
        for n in range(modes):
            rate = spread(rate_ref[pl.ds(n, 1), lanes])
            to_start = jnp.exp(-rate * seg)
            to_end = jnp.exp(-rate * (steps * (SUBS - 1) - seg))
            state_ref[n, place, :] = jnp.sum(ends[n] * to_end, axis=0, keepdims=True)
            state_ref[modes + n, place, :] = jnp.sum(
                starts[n] * to_start, axis=0, keepdims=True
            )


def chain_kernel(row_count, half, first_ref, arrived_ref, rate_ref, out_ref):
    blocks = arrived_ref.shape[0]
    step_decay = jnp.exp(-rate_ref[...] * row_count)

    def run(order):
        def body(index, carry):
            block = order(index)
            out_ref[pl.ds(block, 1)] = carry[None]
            return carry * step_decay + arrived_ref[pl.ds(block, 1)][0]

        lax.fori_loop(0, blocks, body, jnp.zeros(rate_ref.shape, F32), unroll=8)

    @pl.when(first_ref[0] < half)
    def _():
        run(lambda index: index)

    @pl.when(first_ref[0] >= half)
    def _():
        run(lambda index: blocks - 1 - index)


def local_kernel(
    gated_ref, gradm_ref, residue_ref, rate_ref, ahead_ref, behind_ref, seg_ref
):
    row_count = gated_ref.shape[0]
    modes = rate_ref.shape[0]
    steps = row_count // SUBS
    for group in range(gated_ref.shape[1] // LANES):
        lanes = lanes_of(group)
        weight = [spread(residue_ref[pl.ds(n, 1), lanes]) for n in range(modes)]
        rates = [rate_ref[pl.ds(n, 1), lanes] for n in range(modes)]
        decay = [spread(jnp.exp(-r)) for r in rates]
        zero = jnp.zeros((SUBS, LANES), F32)
        for source, target, backward in (
            (gated_ref, ahead_ref, False),
            (gradm_ref, behind_ref, True),
        ):

            def scan_step(step, states):
                at = steps - 1 - step if backward else step
                rows = pl.ds(pl.multiple_of(at * SUBS, SUBS), SUBS)
                value = source[rows, lanes]
                states = [s * d + value for s, d in zip(states, decay)]
                terms = [s * w for s, w in zip(states, weight)]
                while len(terms) > 1:
                    terms = [a + b for a, b in zip(terms[::2], terms[1::2])]
                target[rows, lanes] = terms[0]
                return states

            states = lax.fori_loop(0, steps, scan_step, [zero] * modes, unroll=4)
            sub = sub_index()
            for n in range(modes):
                span = spread(jnp.exp(-rates[n] * steps))
                total = states[n]
                for shift in (1, 2, 4):
                    if backward:
                        moved = jnp.where(
                            sub < SUBS - shift, pltpu.roll(total, SUBS - shift, 0), 0.0
                        )
                    else:
                        moved = jnp.where(sub >= shift, pltpu.roll(total, shift, 0), 0.0)
                    total = total + span * moved
                    span = span * span
                if backward:
                    enters = jnp.where(sub < SUBS - 1, pltpu.roll(total, SUBS - 1, 0), 0.0)
                else:
                    enters = jnp.where(sub >= 1, pltpu.roll(total, 1, 0), 0.0)
                seg_ref[int(backward), n, :, lanes] = enters


def grad_kernel(
    x_ref, prev_ref, cot_ref, kv_ref, ahead_ref, behind_ref, seg_ref, enter_ref,
    residue_ref, rate_ref,
    mix_ref, short_ref,
    held, cot_held, perm_ref,
):
    row_count = cot_ref.shape[0]
    modes = rate_ref.shape[0]
    taps = short_ref.shape[1]
    lead = taps - 1
    steps = row_count // SUBS
    groups = cot_ref.shape[1] // LANES

    @pl.when(pl.program_id(0) == 0)
    def _():
        perm_ref[...] = step_major(row_count, False)

    perm = perm_ref[...]
    for part in range(3):
        load_steps(perm, x_ref, prev_ref, held, part, row_count, lead)
    cot_held[...] = jnp.dot(perm, cot_ref[...], preferred_element_type=F32)
    for group in range(groups):
        lanes = lanes_of(group)
        place = pl.ds(pl.program_id(0) * groups + group, 1)
        rates = [spread(rate_ref[pl.ds(n, 1), lanes]) for n in range(modes)]
        decay = [jnp.exp(-r) for r in rates]
        seg = sub_index().astype(F32) * steps
        for backward in (False, True):
            gap = steps * (SUBS - 1) - seg if backward else seg
            carried = []
            for n in range(modes):
                outer = spread(enter_ref[int(backward) * modes + n, place, :])
                inner = seg_ref[int(backward), n, :, lanes]
                total = inner + jnp.exp(-rates[n] * gap) * outer
                carried.append(
                    total * decay[n] * spread(residue_ref[pl.ds(n, 1), lanes])
                )
            parts = (1, 2) if backward else (0,)

            def grad_pair(index, carry):
                carried, sums = carry
                pair = steps // 2 - 1 - index if backward else index
                base = pl.multiple_of(pair * 2 * SUBS, 2 * SUBS)
                long_rows = [None, None]
                source = behind_ref if backward else ahead_ref
                for which in (1, 0) if backward else (0, 1):
                    terms = list(carried)
                    while len(terms) > 1:
                        terms = [a + b for a, b in zip(terms[::2], terms[1::2])]
                    long_rows[which] = (
                        source[pl.ds(base + which * SUBS, SUBS), lanes] + terms[0]
                    )
                    carried = [c * d for c, d in zip(carried, decay)]
                long_pair = jnp.concatenate(long_rows, axis=0)
                rows = pl.ds(base, 2 * SUBS)
                new_sums = []
                for part, old in zip(parts, sums):
                    if part == 0:
                        factor = cot_held[rows, lanes]
                    else:
                        factor = kv_ref[2 - part, rows, lanes]
                    grad = (long_pair * factor).astype(BF16)
                    mix_ref[part, rows, lanes] = grad
                    wide = grad.astype(F32)
                    taken = []
                    for k in range(taps):
                        term = wide * held[part, pl.ds(base + (lead - k) * SUBS, 2 * SUBS), lanes]
                        taken.append(old[k] + (term[:SUBS] + term[SUBS:]))
                    new_sums.append(taken)
                return carried, new_sums

            zero = jnp.zeros((SUBS, LANES), F32)
            _, sums = lax.fori_loop(
                0, steps // 2, grad_pair, (carried, [[zero] * taps for _ in parts]), unroll=2
            )
            for part, taken in zip(parts, sums):
                for k in range(taps):
                    short_ref[part, k, place, :] = jnp.sum(taken[k], axis=0, keepdims=True)


def back_kernel(mix_ref, next_ref, filt_ref, out_ref, held, made, perm_ref):
    row_count = mix_ref.shape[1]
    taps = filt_ref.shape[1]
    steps = row_count // SUBS

    @pl.when(pl.program_id(0) == 0)
    def _():
        perm_ref[...] = step_major(row_count, True)

    perm = perm_ref[...]
    chunk = 4 * SUBS
    for part in range(3):
        held[pl.ds(0, row_count), :] = mix_ref[part].astype(F32)
        late = next_ref[part].astype(F32)
        for group in range(held.shape[1] // LANES):
            lanes = lanes_of(group)
            for step in range(taps - 1):
                first = held[pl.ds(step * SUBS, SUBS), lanes]
                row = late[step : step + 1, group * LANES : (group + 1) * LANES]
                held[pl.ds((steps + step) * SUBS, SUBS), lanes] = jnp.where(
                    sub_index() == SUBS - 1, spread(row), pltpu.roll(first, SUBS - 1, 0)
                )
            weights = [filt_ref[part, pl.ds(k, 1), lanes] for k in range(taps)]

            def back_chunk(index, carry):
                base = pl.multiple_of(index * chunk, chunk)
                total = weights[0] * held[pl.ds(base, chunk), lanes]
                for k in range(1, taps):
                    total += weights[k] * held[pl.ds(base + k * SUBS, chunk), lanes]
                made[pl.ds(base, chunk), lanes] = total.astype(BF16)
                return carry

            lax.fori_loop(0, row_count // chunk, back_chunk, 0)
        out_ref[part] = jnp.dot(perm, made[...], preferred_element_type=F32).astype(BF16)


def passed_along(shard, by):
    length = lax.axis_size("ctx")
    pairs = [(i, i + by) for i in range(length) if 0 <= i + by < length]
    return lax.ppermute(shard, "ctx", pairs)


def exchange(blocks, axis):
    return lax.all_to_all(blocks, axis, split_axis=0, concat_axis=0, tiled=True)


def cost(flops, bytes_accessed):
    return pl.CostEstimate(flops=flops, bytes_accessed=bytes_accessed, transcendentals=0)


def per_device(inputs, cotangent, short_filter, residue, decay_rate):
    _, row_count, channels = inputs.shape
    taps = short_filter.shape[1]
    modes = residue.shape[0]
    blocks = lax.axis_size("ctx")
    groups = channels // LANES
    wide = min(channels, 2 * LANES)
    grid = (channels // wide,)
    lead = taps - 1

    def columns(*lead_dims):
        zeros = (0,) * len(lead_dims)
        return pl.BlockSpec((*lead_dims, wide), lambda c: (*zeros, c))

    def whole(*dims):
        zeros = (0,) * len(dims)
        return pl.BlockSpec(dims, lambda c: zeros)

    def shaped(dtype, *dims):
        return jax.ShapeDtypeStruct(dims, dtype)

    params = pltpu.CompilerParams(vmem_limit_bytes=32 << 20)
    work = row_count * channels
    step_scratch = [
        pltpu.VMEM((3, row_count + lead * SUBS, wide), F32),
        pltpu.VMEM((row_count, wide), F32),
        pltpu.VMEM((row_count, row_count), BF16),
    ]

    prev = passed_along(inputs[:, row_count - HALO :, :], 1)
    kv, gated, gradm, states = pl.pallas_call(
        mix_kernel,
        grid=grid,
        in_specs=[
            columns(3, row_count),
            columns(3, HALO),
            columns(row_count),
            columns(3, taps),
            columns(modes),
        ],
        out_specs=[
            columns(2, row_count),
            columns(row_count),
            columns(row_count),
            whole(2 * modes, groups, LANES),
        ],
        out_shape=[
            shaped(F32, 2, row_count, channels),
            shaped(F32, row_count, channels),
            shaped(F32, row_count, channels),
            shaped(F32, 2 * modes, groups, LANES),
        ],
        scratch_shapes=step_scratch,
        compiler_params=params,
        cost_estimate=cost(work * 110, work * 24),
        name="mix",
    )(inputs, prev, cotangent, short_filter, decay_rate)

    state_rows = 2 * modes * groups // blocks
    first = lax.axis_index("ctx") * state_rows
    half = modes * groups
    arrived = exchange(states.reshape(blocks, state_rows, LANES), "ctx")
    rate_rows = jnp.tile(decay_rate.reshape(half, LANES), (2, 1))
    entering = pl.pallas_call(
        functools.partial(chain_kernel, row_count, half),
        in_specs=[
            pl.BlockSpec(memory_space=pltpu.SMEM),
            pl.BlockSpec(memory_space=pltpu.VMEM),
            pl.BlockSpec(memory_space=pltpu.VMEM),
        ],
        out_specs=pl.BlockSpec(memory_space=pltpu.VMEM),
        out_shape=shaped(F32, blocks, state_rows, LANES),
        compiler_params=pltpu.CompilerParams(vmem_limit_bytes=4 << 20),
        cost_estimate=cost(blocks * state_rows * LANES * 2, blocks * state_rows * LANES * 8),
        name="chain",
    )(first[None], arrived, lax.dynamic_slice_in_dim(rate_rows, first, state_rows, 0))
    entering = exchange(entering, "ctx").reshape(2 * modes, groups, LANES)

    ahead, behind, seg_states = pl.pallas_call(
        local_kernel,
        grid=grid,
        in_specs=[columns(row_count), columns(row_count), columns(modes), columns(modes)],
        out_specs=[columns(row_count), columns(row_count), columns(2, modes, SUBS)],
        out_shape=[
            shaped(F32, row_count, channels),
            shaped(F32, row_count, channels),
            shaped(F32, 2, modes, SUBS, channels),
        ],
        compiler_params=params,
        cost_estimate=cost(work * 128, work * 18),
        name="local",
    )(gated, gradm, residue, decay_rate)

    grad_mix, short_part = pl.pallas_call(
        grad_kernel,
        grid=grid,
        in_specs=[
            columns(3, row_count),
            columns(3, HALO),
            columns(row_count),
            columns(2, row_count),
            columns(row_count),
            columns(row_count),
            columns(2, modes, SUBS),
            whole(2 * modes, groups, LANES),
            columns(modes),
            columns(modes),
        ],
        out_specs=[columns(3, row_count), whole(3, taps, groups, LANES)],
        out_shape=[
            shaped(BF16, 3, row_count, channels),
            shaped(F32, 3, taps, groups, LANES),
        ],
        scratch_shapes=step_scratch,
        compiler_params=params,
        cost_estimate=cost(work * 110, work * 30),
        name="grad",
    )(
        inputs, prev, cotangent, kv, ahead, behind, seg_states, entering, residue, decay_rate
    )

    short_rows = 3 * taps * groups
    share = -(-short_rows // blocks)
    padded = jnp.pad(
        short_part.reshape(short_rows, LANES), ((0, share * blocks - short_rows), (0, 0))
    )
    gathered = exchange(padded.reshape(blocks, share, LANES), "ctx")
    own_sum = jnp.sum(gathered, axis=0)
    all_sums = exchange(jnp.broadcast_to(own_sum[None], (blocks, share, LANES)), "ctx")
    all_sums = all_sums.reshape(share * blocks, LANES)
    squares = jnp.sum(all_sums * all_sums)
    tp_count = lax.axis_size("tp")
    squares = jnp.sum(exchange(jnp.broadcast_to(squares, (tp_count, LANES)), "tp")[:, 0])
    clip_limit = math.sqrt(3 * channels * tp_count * taps)
    factor = jnp.minimum(1.0, clip_limit / (jnp.sqrt(squares) + 1e-06))
    grad_short = (all_sums[:short_rows] * factor).reshape(3, taps, channels)

    late = passed_along(grad_mix[:, : lead * SUBS : SUBS, :], -1)
    late = jnp.pad(late, ((0, 0), (0, HALO - lead), (0, 0)))
    grad_inputs = pl.pallas_call(
        back_kernel,
        grid=grid,
        in_specs=[columns(3, row_count), columns(3, HALO), columns(3, taps)],
        out_specs=columns(3, row_count),
        out_shape=shaped(BF16, 3, row_count, channels),
        scratch_shapes=[
            pltpu.VMEM((row_count + lead * SUBS, wide), F32),
            pltpu.VMEM((row_count, wide), BF16),
            pltpu.VMEM((row_count, row_count), BF16),
        ],
        compiler_params=params,
        cost_estimate=cost(work * 48, work * 12),
        name="back",
    )(grad_mix, late, short_filter)
    return (grad_inputs, grad_short)


def solution(mesh):
    return jax.shard_map(
        per_device,
        mesh=mesh,
        in_specs=(
            P(None, "ctx", "tp"),
            P("ctx", "tp"),
            P(None, None, "tp"),
            P(None, "tp"),
            P(None, "tp"),
        ),
        out_specs=(P(None, "ctx", "tp"), P(None, None, "tp")),
        check_vma=False,
    )
```

profile of v0, /device:TPU:1, one launch (start us, length us, event | category | flops | bytes accessed | tf_op | source)
XLA Modules:
  0.0 158.7 jit_solution(16182792251198630915)
XLA Ops:
  0.6 0.0 copy-start.9
  0.6 0.8 slice.13
  1.5 4.4 %collective-permute-start = (bf16[3,8,1024]{2,1,0:T(8,128)(2,1)S(1)}, bf16[3,8,1024]{2,1,0:T(8,128)(2,1)S(1)}, u32[]{:S(2)}, u32[]{:S(2)}) collective-permute-start(bf16[3,8,1024]{2,1,0:T(8,128)(2,1)S(1)} %slice.13), channel_id=1, source_target_pairs={{0,8},{8,16},{16,24},{24,32},{32,40},{40,48},{48,56},{56,64},{64,7... | collective-permute-start | bytes 147464 | tf_op jit(solution)/shard_map/ppermute | solution.py:319
  5.8 1.2 collective-permute-done.prev_ref
  7.0 0.0 copy-start
  7.0 1.4 copy-done
  8.4 0.0 copy-start.4
  8.4 1.0 copy-done.4
  9.5 0.0 copy-start.8
  9.5 0.8 copy-done.8
  10.3 0.0 copy-start.18
  10.3 0.9 copy-done.18
  11.2 0.0 copy-start.20
  11.2 8.3 %mix.1 = (f32[2,256,1024]{2,1,0:T(8,128)S(1)}, f32[256,1024]{1,0:T(8,128)S(1)}, f32[256,1024]{1,0:T(8,128)S(1)}, f32[32,8,128]{2,1,0:T(8,128)}) custom-call(bf16[3,256,1024]{2,1,0:T(8,128)(2,1)S(1)} %copy-done, bf16[3,8,1024]{2,1,0:T(8,128)(2,1)S(1)} %collective-permute-done.prev_ref, bf16[256,1024]{1,0:T(8,128)(2,1)S(1)} %copy-done.4, ...), custom_call_target="tpu_custom_call" | custom-call | flops 28835840 | bytes 6291456 | tf_op jit(solution)/shard_map/mix/pallas_call | solution.py:360
  19.5 0.0 copy-start.2
  19.5 1.3 copy-done.2
  20.8 0.0 copy-start.10
  20.8 1.0 copy-done.10
  21.8 19.8 %all-to-all-start = ((f32[64,4,128]{2,1,0:T(4,128)}), f32[64,4,128]{2,1,0:T(4,128)S(1)}, u32[]{:S(2)}, u32[]{:S(2)}) async-start(f32[64,4,128]{2,1,0:T(4,128)} %bitcast.1), calls=%async_computation | async-start | bytes 262144 | tf_op jit(solution)/shard_map/all_to_all | solution.py:323
  41.6 0.0 copy-start.1
  41.6 0.0 copy-start.5
  41.6 0.0 copy-done.9
  41.7 13.9 %all-to-all-done.arrived_ref = f32[64,4,128]{2,1,0:T(4,128)S(1)} async-done(((f32[64,4,128]{2,1,0:T(4,128)}), f32[64,4,128]{2,1,0:T(4,128)S(1)}, u32[]{:S(2)}, u32[]{:S(2)}) %all-to-all-start) | async-done | bytes 131104 | tf_op jit(solution)/shard_map/all_to_all | solution.py:323
  55.6 0.8 chain.1
  56.4 5.6 %all-to-all-start.1 = ((f32[64,4,128]{2,1,0:T(4,128)}), f32[64,4,128]{2,1,0:T(4,128)S(1)}, u32[]{:S(2)}, u32[]{:S(2)}) async-start(f32[64,4,128]{2,1,0:T(4,128)} %chain.1), calls=%async_computation.1 | async-start | bytes 262144 | tf_op jit(solution)/shard_map/all_to_all | solution.py:323
  62.0 0.0 copy-done.20
  62.0 0.0 copy-start.11
  62.0 1.2 copy-done.11
  63.3 6.4 %local.1 = (f32[256,1024]{1,0:T(8,128)S(1)}, f32[256,1024]{1,0:T(8,128)S(1)}, f32[2,16,8,1024]{3,2,1,0:T(8,128)S(1)}) custom-call(f32[256,1024]{1,0:T(8,128)S(1)} %get-tuple-element.12.gated_ref, f32[256,1024]{1,0:T(8,128)S(1)} %copy-done.11, f32[16,1024]{1,0:T(8,128)S(1)} %copy-done.20, f32[16,1024]{1,0:T(8,128)S(1)} %copy-done.9), custom_call_target="tpu_custom_call" | custom-call | flops 33554432 | bytes 4718592 | tf_op jit(solution)/shard_map/local/pallas_call | solution.py:408
  69.6 0.0 copy-start.12
  69.7 1.0 copy-done.12
  70.6 0.0 copy-start.14
  70.6 1.0 copy-done.14
  71.6 0.0 copy-start.16
  71.6 1.0 copy-done.16
  72.6 3.4 %all-to-all-done.1 = f32[64,4,128]{2,1,0:T(4,128)S(1)} async-done(((f32[64,4,128]{2,1,0:T(4,128)}), f32[64,4,128]{2,1,0:T(4,128)S(1)}, u32[]{:S(2)}, u32[]{:S(2)}) %all-to-all-start.1) | async-done | bytes 131104 | tf_op jit(solution)/shard_map/all_to_all | solution.py:323
  76.0 0.0 copy-done.1
  76.0 0.0 copy-done.5
  76.0 0.0 copy-start.3
  76.0 1.6 %copy-done.3 = f32[2,256,1024]{2,1,0:T(8,128)S(1)} copy-done((f32[2,256,1024]{2,1,0:T(8,128)S(1)}, f32[2,256,1024]{2,1,0:T(8,128)}, u32[]{:S(2)}) %copy-start.3) | copy-done | bytes 2097176
  77.6 1.2 copy-done.13
  78.8 1.2 copy-done.15
  80.0 1.2 copy-done.17
  81.2 8.5 %grad.1 = (bf16[3,256,1024]{2,1,0:T(8,128)(2,1)S(1)}, f32[3,7,8,128]{3,2,1,0:T(8,128)S(1)}) custom-call(bf16[3,256,1024]{2,1,0:T(8,128)(2,1)S(1)} %copy-done.1, bf16[3,8,1024]{2,1,0:T(8,128)(2,1)S(1)} %collective-permute-done.prev_ref, bf16[256,1024]{1,0:T(8,128)(2,1)S(1)} %copy-done.5, f32[2,256,1024]{2,1,0:T(8,128)S(1)} %copy-done.3, ...), custom_call_target="tpu_custom_call" | custom-call | flops 28835840 | bytes 7864320 | tf_op jit(solution)/shard_map/grad/pallas_call | solution.py:423
  89.7 0.0 copy-start.6
  89.8 1.1 copy-done.6
  91.0 24.9 %all_to_all.29 = f32[64,3,128]{2,1,0:T(4,128)S(1)} all-to-all(f32[64,3,128]{2,1,0:T(4,128)S(1)} %reshape.32), channel_id=1, replica_groups=mesh['ctx'=64,'tp'=8] {'ctx'}, dimensions={0} | all-to-all | bytes 196608 | tf_op jit(solution)/shard_map/all_to_all | solution.py:323
  115.9 0.1 reduce_sum.27
  116.0 0.7 broadcast_in_dim.13
  116.6 5.5 %all-to-all-start.3 = ((f32[64,3,128]{2,1,0:T(4,128)}), f32[64,3,128]{2,1,0:T(4,128)S(1)}, u32[]{:S(2)}, u32[]{:S(2)}) async-start(f32[64,3,128]{2,1,0:T(4,128)} %broadcast_in_dim.13), calls=%async_computation.3 | async-start | bytes 262144 | tf_op jit(solution)/shard_map/all_to_all | solution.py:323
  122.1 1.0 slice.14
  123.2 1.3 collective-permute-start.1
  124.5 11.6 %all-to-all-done.3 = f32[64,3,128]{2,1,0:T(4,128)S(1)} async-done(((f32[64,3,128]{2,1,0:T(4,128)}), f32[64,3,128]{2,1,0:T(4,128)S(1)}, u32[]{:S(2)}, u32[]{:S(2)}) %all-to-all-start.3) | async-done | bytes 98336 | tf_op jit(solution)/shard_map/all_to_all | solution.py:323
  136.1 0.7 multiply_reduce_fusion
  136.8 1.3 broadcast_in_dim.14
  138.1 10.5 %all-to-all-start.4 = ((f32[8,1,128]{2,1,0:T(1,128)}), f32[8,1,128]{2,1,0:T(1,128)S(1)}, u32[]{:S(2)}, u32[]{:S(2)}) async-start(f32[8,1,128]{2,1,0:T(1,128)} %broadcast_in_dim.14), calls=%async_computation.4 | async-start | bytes 8192 | tf_op jit(solution)/shard_map/all_to_all | solution.py:323
  148.6 0.0 collective-permute-done.1
  148.6 0.0 copy-done.19
  148.6 0.0 copy-start.7
  148.6 1.4 copy-done.7
  150.0 6.7 %back.1 = bf16[3,256,1024]{2,1,0:T(8,128)(2,1)} custom-call(bf16[3,256,1024]{2,1,0:T(8,128)(2,1)S(1)} %copy-done.7, bf16[3,8,1024]{2,1,0:T(8,128)(2,1)S(1)} %pad.8.next_ref, f32[3,7,1024]{2,1,0:T(8,128)S(1)} %copy-done.19), custom_call_target="tpu_custom_call" | custom-call | flops 12582912 | bytes 3145728 | tf_op jit(solution)/shard_map/back/pallas_call | solution.py:469
  156.7 0.0 all-to-all-done.4
  156.7 0.6 slice_reduce_fusion
  158.0 0.7 mul.21
  (11 shorter events, 0.1 us)
Async XLA Ops:
  0.6 41.0 %copy-start.9 = (f32[16,1024]{1,0:T(8,128)S(1)}, f32[16,1024]{1,0:T(8,128)}, u32[]{:S(2)}) copy-start(f32[16,1024]{1,0:T(8,128)} %rate_ref.5) | copy-start | bytes 196612
  1.5 5.5 %collective-permute-start = (bf16[3,8,1024]{2,1,0:T(8,128)(2,1)S(1)}, bf16[3,8,1024]{2,1,0:T(8,128)(2,1)S(1)}, u32[]{:S(2)}, u32[]{:S(2)}) collective-permute-start(bf16[3,8,1024]{2,1,0:T(8,128)(2,1)S(1)} %slice.13), channel_id=1, source_target_pairs={{0,8},{8,16},{16,24},{24,32},{32,40},{40,48},{48,56},{56,64},{64,7... | collective-permute-start | bytes 147464 | tf_op jit(solution)/shard_map/ppermute | solution.py:319
  7.0 1.4 copy-start
  8.4 1.0 copy-start.4
  9.5 0.8 copy-start.8
  10.3 0.9 copy-start.18
  11.2 50.8 %copy-start.20 = (f32[16,1024]{1,0:T(8,128)S(1)}, f32[16,1024]{1,0:T(8,128)}, u32[]{:S(2)}) copy-start(f32[16,1024]{1,0:T(8,128)} %residue_ref.3) | copy-start | bytes 196612
  19.5 1.3 copy-start.2
  20.8 1.0 copy-start.10
  21.8 33.8 %all-to-all-start = ((f32[64,4,128]{2,1,0:T(4,128)}), f32[64,4,128]{2,1,0:T(4,128)S(1)}, u32[]{:S(2)}, u32[]{:S(2)}) async-start(f32[64,4,128]{2,1,0:T(4,128)} %bitcast.1), calls=%async_computation | async-start | bytes 262144 | tf_op jit(solution)/shard_map/all_to_all | solution.py:323
  41.6 34.4 %copy-start.1 = (bf16[3,256,1024]{2,1,0:T(8,128)(2,1)S(1)}, bf16[3,256,1024]{2,1,0:T(8,128)(2,1)}, u32[]{:S(2)}) copy-start(bf16[3,256,1024]{2,1,0:T(8,128)(2,1)} %x_ref.3) | copy-start | bytes 4718596
  41.6 34.4 %copy-start.5 = (bf16[256,1024]{1,0:T(8,128)(2,1)S(1)}, bf16[256,1024]{1,0:T(8,128)(2,1)}, u32[]{:S(2)}) copy-start(bf16[256,1024]{1,0:T(8,128)(2,1)} %cot_ref.3) | copy-start | bytes 1572868
  56.4 19.5 %all-to-all-start.1 = ((f32[64,4,128]{2,1,0:T(4,128)}), f32[64,4,128]{2,1,0:T(4,128)S(1)}, u32[]{:S(2)}, u32[]{:S(2)}) async-start(f32[64,4,128]{2,1,0:T(4,128)} %chain.1), calls=%async_computation.1 | async-start | bytes 262144 | tf_op jit(solution)/shard_map/all_to_all | solution.py:323
  62.0 1.2 copy-start.11
  69.6 1.0 copy-start.12
  70.6 1.0 copy-start.14
  71.6 1.0 copy-start.16
  76.0 1.6 %copy-start.3 = (f32[2,256,1024]{2,1,0:T(8,128)S(1)}, f32[2,256,1024]{2,1,0:T(8,128)}, u32[]{:S(2)}) copy-start(f32[2,256,1024]{2,1,0:T(8,128)} %copy-done.2) | copy-start | bytes 6291460
  77.6 1.2 copy-start.13
  78.8 1.2 copy-start.15
  80.0 1.2 copy-start.17
  89.7 1.1 copy-start.6
  90.9 57.7 %copy-start.19 = (f32[3,7,1024]{2,1,0:T(8,128)S(1)}, f32[3,7,1024]{2,1,0:T(8,128)}, u32[]{:S(2)}) copy-start(f32[3,7,1024]{2,1,0:T(8,128)} %filt_ref.3) | copy-start | bytes 258052
  116.6 19.4 %all-to-all-start.3 = ((f32[64,3,128]{2,1,0:T(4,128)}), f32[64,3,128]{2,1,0:T(4,128)S(1)}, u32[]{:S(2)}, u32[]{:S(2)}) async-start(f32[64,3,128]{2,1,0:T(4,128)} %broadcast_in_dim.13), calls=%async_computation.3 | async-start | bytes 262144 | tf_op jit(solution)/shard_map/all_to_all | solution.py:323
  123.2 25.4 %collective-permute-start.1 = (bf16[3,6,1024]{2,1,0:T(8,128)(2,1)S(1)}, bf16[3,6,1024]{2,1,0:T(8,128)(2,1)S(1)}, u32[]{:S(2)}, u32[]{:S(2)}) collective-permute-start(bf16[3,6,1024]{2,1,0:T(8,128)(2,1)S(1)} %slice.14), channel_id=1, source_target_pairs={{8,0},{16,8},{24,16},{32,24},{40,32},{48,40},{56,48},{64,56},{72,6... | collective-permute-start | bytes 110600 | tf_op jit(solution)/shard_map/ppermute | solution.py:319
  138.1 18.6 %all-to-all-start.4 = ((f32[8,1,128]{2,1,0:T(1,128)}), f32[8,1,128]{2,1,0:T(1,128)S(1)}, u32[]{:S(2)}, u32[]{:S(2)}) async-start(f32[8,1,128]{2,1,0:T(1,128)} %broadcast_in_dim.14), calls=%async_computation.4 | async-start | bytes 8192 | tf_op jit(solution)/shard_map/all_to_all | solution.py:323
  148.6 1.4 copy-start.7
where the time goes:
time: 160 us; the launch traced here: 159 us
  starting transfers between devices  47 us (29%)
  Pallas kernels  30.6 us (19%)
  waiting for transfers between devices  30.1 us (19%)
  blocking collectives  24.9 us (16%)
  local copies, waits for them, and re-layouts  23.1 us (14%)
    all_to_all x4, starting transfers between devices, exchange(): return lax.all_to_all(blocks, axis, split_axis=0, concat_axis=0, tiled=True)  41.3 us
    all_to_all x4, waiting for transfers between devices, exchange(): return lax.all_to_all(blocks, axis, split_axis=0, concat_axis=0, tiled=True)  28.9 us
    all_to_all x1, blocking collectives, exchange(): return lax.all_to_all(blocks, axis, split_axis=0, concat_axis=0, tiled=True)  24.9 us
    unnamed x42, local copies, waits for them, and re-layouts  18.4 us
    pallas_call x1, Pallas kernels, per_device(): pl.pallas_call(grad_kernel, grid=grid, in_specs=[columns(3, row_count), c...  8.49 us
    pallas_call x1, Pallas kernels, per_device(): pl.pallas_call(mix_kernel, grid=grid, in_specs=[columns(3, row_count), co...  8.31 us
    pallas_call x1, Pallas kernels, per_device(): pl.pallas_call(back_kernel, grid=grid, in_specs=[columns(3, row_count), c...  6.67 us
    pallas_call x1, Pallas kernels, per_device(): pl.pallas_call(local_kernel, grid=grid, in_specs=[columns(row_count), col...  6.37 us
  transfers between devices with their start and end apart: 6, of which 4 were waited for; matrix products, arithmetic and copies ran while one was open for 2% of the time, Pallas kernels for 8%

commit v1 on v0

--- a/solution.py
+++ b/solution.py
@@ -11,6 +11,8 @@
 LANES = 128
 SUBS = 8
 HALO = 8
+CHUNK = 8
+TAPS = 7
 F32 = jnp.float32
 BF16 = jnp.bfloat16
 
@@ -32,6 +34,21 @@
 
 def lanes_of(group):
     return pl.ds(group * LANES, LANES)
+
+
+def kept(value):
+    return value.astype(BF16).astype(F32)
+
+
+def added(terms):
+    while len(terms) > 1:
+        odd = terms[-1:] if len(terms) % 2 else []
+        terms = [a + b for a, b in zip(terms[::2], terms[1::2])] + odd
+    return terms[0]
+
+
+def tapped(weights, rows):
+    return added([w * r for w, r in zip(weights, rows)])
 
 
 def load_steps(perm, x_ref, prev_ref, held, part, row_count, lead):
@@ -70,34 +87,35 @@
     for part in range(3):
         load_steps(perm, x_ref, prev_ref, held, part, row_count, lead)
     cot_held[...] = jnp.dot(perm, cot_ref[...], preferred_element_type=F32)
-    chunk = 4 * SUBS
     for group in range(groups):
         lanes = lanes_of(group)
-        taps_of = [
-            [filt_ref[part, pl.ds(k, 1), lanes] for k in range(taps)] for part in range(3)
+        weights = [
+            [spread(filt_ref[part, pl.ds(k, 1), lanes]) for k in range(taps)] for part in range(3)
         ]
 
         def mix_chunk(index, carry):
-            base = pl.multiple_of(index * chunk, chunk)
-            mixed = []
-            for part in range(3):
-                total = taps_of[part][0] * held[part, pl.ds(base + lead * SUBS, chunk), lanes]
-                for k in range(1, taps):
-                    total += (
-                        taps_of[part][k]
-                        * held[part, pl.ds(base + (lead - k) * SUBS, chunk), lanes]
-                    )
-                mixed.append(total)
-            rows = pl.ds(base, chunk)
-            kv_ref[0, rows, lanes] = mixed[1]
-            kv_ref[1, rows, lanes] = mixed[2]
-            gated_ref[rows, lanes] = (mixed[1] * mixed[2]).astype(BF16).astype(F32)
-            gradm_ref[rows, lanes] = (
-                (cot_held[rows, lanes] * mixed[0]).astype(BF16).astype(F32)
-            )
+            base = pl.multiple_of(index * (CHUNK * SUBS), CHUNK * SUBS)
+
+            def short(part):
+                window = [
+                    held[part, pl.ds(base + at * SUBS, SUBS), lanes] for at in range(CHUNK + lead)
+                ]
+                return [tapped(weights[part], window[at : at + taps][::-1]) for at in range(CHUNK)]
+
+            key_rows = short(1)
+            value_rows = short(2)
+            for at in range(CHUNK):
+                rows = pl.ds(base + at * SUBS, SUBS)
+                kv_ref[0, rows, lanes] = key_rows[at]
+                kv_ref[1, rows, lanes] = value_rows[at]
+                gated_ref[rows, lanes] = kept(key_rows[at] * value_rows[at])
+            query_rows = short(0)
+            for at in range(CHUNK):
+                rows = pl.ds(base + at * SUBS, SUBS)
+                gradm_ref[rows, lanes] = kept(cot_held[rows, lanes] * query_rows[at])
             return carry
 
-        lax.fori_loop(0, row_count // chunk, mix_chunk, 0)
+        lax.fori_loop(0, steps // CHUNK, mix_chunk, 0)
         decay = [spread(jnp.exp(-rate_ref[pl.ds(n, 1), lanes])) for n in range(modes)]
 
         def gather_step(step, carry):
@@ -113,7 +131,7 @@
 
         zero = jnp.zeros((SUBS, LANES), F32)
         ends, starts = lax.fori_loop(
-            0, steps, gather_step, ([zero] * modes, [zero] * modes), unroll=4
+            0, steps, gather_step, ([zero] * modes, [zero] * modes), unroll=8
         )
         place = pl.ds(pl.program_id(0) * groups + group, 1)
         seg = sub_index().astype(F32) * steps
@@ -170,13 +188,10 @@
                 rows = pl.ds(pl.multiple_of(at * SUBS, SUBS), SUBS)
                 value = source[rows, lanes]
                 states = [s * d + value for s, d in zip(states, decay)]
-                terms = [s * w for s, w in zip(states, weight)]
-                while len(terms) > 1:
-                    terms = [a + b for a, b in zip(terms[::2], terms[1::2])]
-                target[rows, lanes] = terms[0]
+                target[rows, lanes] = tapped(weight, states)
                 return states
 
-            states = lax.fori_loop(0, steps, scan_step, [zero] * modes, unroll=4)
+            states = lax.fori_loop(0, steps, scan_step, [zero] * modes, unroll=8)
             sub = sub_index()
             for n in range(modes):
                 span = spread(jnp.exp(-rates[n] * steps))
@@ -205,7 +220,7 @@
 ):
     row_count = cot_ref.shape[0]
     modes = rate_ref.shape[0]
-    taps = short_ref.shape[1]
+    taps = TAPS
     lead = taps - 1
     steps = row_count // SUBS
     groups = cot_ref.shape[1] // LANES
@@ -213,6 +228,7 @@
     @pl.when(pl.program_id(0) == 0)
     def _():
         perm_ref[...] = step_major(row_count, False)
+        short_ref[...] = jnp.zeros(short_ref.shape, F32)
 
     perm = perm_ref[...]
     for part in range(3):
@@ -236,45 +252,45 @@
                 )
             parts = (1, 2) if backward else (0,)
 
-            def grad_pair(index, carry):
+            def grad_chunk(index, carry):
                 carried, sums = carry
-                pair = steps // 2 - 1 - index if backward else index
-                base = pl.multiple_of(pair * 2 * SUBS, 2 * SUBS)
-                long_rows = [None, None]
+                place_of = steps // CHUNK - 1 - index if backward else index
+                base = pl.multiple_of(place_of * (CHUNK * SUBS), CHUNK * SUBS)
                 source = behind_ref if backward else ahead_ref
-                for which in (1, 0) if backward else (0, 1):
-                    terms = list(carried)
-                    while len(terms) > 1:
-                        terms = [a + b for a, b in zip(terms[::2], terms[1::2])]
-                    long_rows[which] = (
-                        source[pl.ds(base + which * SUBS, SUBS), lanes] + terms[0]
-                    )
+                long_rows = [None] * CHUNK
+                for at in range(CHUNK)[:: -1 if backward else 1]:
+                    long_rows[at] = source[pl.ds(base + at * SUBS, SUBS), lanes] + added(carried)
                     carried = [c * d for c, d in zip(carried, decay)]
-                long_pair = jnp.concatenate(long_rows, axis=0)
-                rows = pl.ds(base, 2 * SUBS)
                 new_sums = []
                 for part, old in zip(parts, sums):
-                    if part == 0:
-                        factor = cot_held[rows, lanes]
-                    else:
-                        factor = kv_ref[2 - part, rows, lanes]
-                    grad = (long_pair * factor).astype(BF16)
-                    mix_ref[part, rows, lanes] = grad
-                    wide = grad.astype(F32)
-                    taken = []
-                    for k in range(taps):
-                        term = wide * held[part, pl.ds(base + (lead - k) * SUBS, 2 * SUBS), lanes]
-                        taken.append(old[k] + (term[:SUBS] + term[SUBS:]))
-                    new_sums.append(taken)
+                    wide = []
+                    for pair in range(CHUNK // 2):
+                        rows = pl.ds(base + pair * 2 * SUBS, 2 * SUBS)
+                        factor = cot_held[rows, lanes] if part == 0 else kv_ref[2 - part, rows, lanes]
+                        grad = jnp.concatenate(long_rows[2 * pair : 2 * pair + 2], axis=0) * factor
+                        grad = grad.astype(BF16)
+                        mix_ref[part, rows, lanes] = grad
+                        grad = grad.astype(F32)
+                        wide += [grad[:SUBS], grad[SUBS:]]
+                    window = [
+                        held[part, pl.ds(base + at * SUBS, SUBS), lanes]
+                        for at in range(CHUNK + lead)
+                    ]
+                    new_sums.append(
+                        [
+                            old[k] + tapped(wide, window[lead - k : lead - k + CHUNK])
+                            for k in range(taps)
+                        ]
+                    )
                 return carried, new_sums
 
             zero = jnp.zeros((SUBS, LANES), F32)
             _, sums = lax.fori_loop(
-                0, steps // 2, grad_pair, (carried, [[zero] * taps for _ in parts]), unroll=2
+                0, steps // CHUNK, grad_chunk, (carried, [[zero] * taps for _ in parts])
             )
             for part, taken in zip(parts, sums):
                 for k in range(taps):
-                    short_ref[part, k, place, :] = jnp.sum(taken[k], axis=0, keepdims=True)
+                    short_ref[part * taps + k, place, :] = jnp.sum(taken[k], axis=0, keepdims=True)
 
 
 def back_kernel(mix_ref, next_ref, filt_ref, out_ref, held, made, perm_ref):
@@ -287,7 +303,6 @@
         perm_ref[...] = step_major(row_count, True)
 
     perm = perm_ref[...]
-    chunk = 4 * SUBS
     for part in range(3):
         held[pl.ds(0, row_count), :] = mix_ref[part].astype(F32)
         late = next_ref[part].astype(F32)
@@ -299,18 +314,41 @@
                 held[pl.ds((steps + step) * SUBS, SUBS), lanes] = jnp.where(
                     sub_index() == SUBS - 1, spread(row), pltpu.roll(first, SUBS - 1, 0)
                 )
-            weights = [filt_ref[part, pl.ds(k, 1), lanes] for k in range(taps)]
+            weights = [spread(filt_ref[part, pl.ds(k, 1), lanes]) for k in range(taps)]
 
             def back_chunk(index, carry):
-                base = pl.multiple_of(index * chunk, chunk)
-                total = weights[0] * held[pl.ds(base, chunk), lanes]
-                for k in range(1, taps):
-                    total += weights[k] * held[pl.ds(base + k * SUBS, chunk), lanes]
-                made[pl.ds(base, chunk), lanes] = total.astype(BF16)
+                base = pl.multiple_of(index * (CHUNK * SUBS), CHUNK * SUBS)
+                window = [
+                    held[pl.ds(base + at * SUBS, SUBS), lanes] for at in range(CHUNK + taps - 1)
+                ]
+                rows = [tapped(weights, window[at : at + taps]) for at in range(CHUNK)]
+                made[pl.ds(base, CHUNK * SUBS), lanes] = jnp.concatenate(rows, axis=0).astype(BF16)
                 return carry
 
-            lax.fori_loop(0, row_count // chunk, back_chunk, 0)
+            lax.fori_loop(0, steps // CHUNK, back_chunk, 0)
         out_ref[part] = jnp.dot(perm, made[...], preferred_element_type=F32).astype(BF16)
+
+
+def fold_kernel(part_ref, out_ref):
+    total = jnp.sum(part_ref[...], axis=0, keepdims=True)
+    out_ref[...] = jnp.broadcast_to(total, out_ref.shape)
+
+
+def square_kernel(sums_ref, out_ref):
+    value = sums_ref[...]
+    total = jnp.sum(jnp.sum(value * value, axis=0))
+    out_ref[...] = jnp.full(out_ref.shape, total, F32)
+
+
+def scale_kernel(clip_limit, sums_ref, squares_ref, out_ref):
+    squares = jnp.sum(squares_ref[...], axis=0, keepdims=True)
+    factor = jnp.minimum(1.0, clip_limit / (jnp.sqrt(squares) + 1e-06))
+    taps = out_ref.shape[1]
+    for part in range(3):
+        for k in range(taps):
+            rows = sums_ref[part * taps + k] * factor
+            for group in range(rows.shape[0]):
+                out_ref[part, pl.ds(k, 1), lanes_of(group)] = rows[group : group + 1]
 
 
 def passed_along(shard, by):
@@ -348,7 +386,9 @@
     def shaped(dtype, *dims):
         return jax.ShapeDtypeStruct(dims, dtype)
 
-    params = pltpu.CompilerParams(vmem_limit_bytes=32 << 20)
+    params = pltpu.CompilerParams(vmem_limit_bytes=60 << 20)
+    small = pltpu.CompilerParams(vmem_limit_bytes=4 << 20)
+    in_vmem = pl.BlockSpec(memory_space=pltpu.VMEM)
     work = row_count * channels
     step_scratch = [
         pltpu.VMEM((3, row_count + lead * SUBS, wide), F32),
@@ -389,22 +429,6 @@
     first = lax.axis_index("ctx") * state_rows
     half = modes * groups
     arrived = exchange(states.reshape(blocks, state_rows, LANES), "ctx")
-    rate_rows = jnp.tile(decay_rate.reshape(half, LANES), (2, 1))
-    entering = pl.pallas_call(
-        functools.partial(chain_kernel, row_count, half),
-        in_specs=[
-            pl.BlockSpec(memory_space=pltpu.SMEM),
-            pl.BlockSpec(memory_space=pltpu.VMEM),
-            pl.BlockSpec(memory_space=pltpu.VMEM),
-        ],
-        out_specs=pl.BlockSpec(memory_space=pltpu.VMEM),
-        out_shape=shaped(F32, blocks, state_rows, LANES),
-        compiler_params=pltpu.CompilerParams(vmem_limit_bytes=4 << 20),
-        cost_estimate=cost(blocks * state_rows * LANES * 2, blocks * state_rows * LANES * 8),
-        name="chain",
-    )(first[None], arrived, lax.dynamic_slice_in_dim(rate_rows, first, state_rows, 0))
-    entering = exchange(entering, "ctx").reshape(2 * modes, groups, LANES)
-
     ahead, behind, seg_states = pl.pallas_call(
         local_kernel,
         grid=grid,
@@ -419,7 +443,29 @@
         cost_estimate=cost(work * 128, work * 18),
         name="local",
     )(gated, gradm, residue, decay_rate)
-
+    arrived, ahead, behind, seg_states = lax.optimization_barrier(
+        (arrived, ahead, behind, seg_states)
+    )
+
+    rate_rows = jnp.tile(decay_rate.reshape(half, LANES), (2, 1))
+    entering = pl.pallas_call(
+        functools.partial(chain_kernel, row_count, half),
+        in_specs=[
+            pl.BlockSpec(memory_space=pltpu.SMEM),
+            in_vmem,
+            in_vmem,
+        ],
+        out_specs=in_vmem,
+        out_shape=shaped(F32, blocks, state_rows, LANES),
+        compiler_params=small,
+        cost_estimate=cost(blocks * state_rows * LANES * 2, blocks * state_rows * LANES * 8),
+        name="chain",
+    )(first[None], arrived, lax.dynamic_slice_in_dim(rate_rows, first, state_rows, 0))
+    entering = exchange(entering, "ctx").reshape(2 * modes, groups, LANES)
+
+    share = -(-3 * taps * groups // blocks)
+    share += share % 2
+    short_rows = share * blocks // groups
     grad_mix, short_part = pl.pallas_call(
         grad_kernel,
         grid=grid,
@@ -435,10 +481,10 @@
             columns(modes),
             columns(modes),
         ],
-        out_specs=[columns(3, row_count), whole(3, taps, groups, LANES)],
+        out_specs=[columns(3, row_count), whole(short_rows, groups, LANES)],
         out_shape=[
             shaped(BF16, 3, row_count, channels),
-            shaped(F32, 3, taps, groups, LANES),
+            shaped(F32, short_rows, groups, LANES),
         ],
         scratch_shapes=step_scratch,
         compiler_params=params,
@@ -448,24 +494,19 @@
         inputs, prev, cotangent, kv, ahead, behind, seg_states, entering, residue, decay_rate
     )
 
-    short_rows = 3 * taps * groups
-    share = -(-short_rows // blocks)
-    padded = jnp.pad(
-        short_part.reshape(short_rows, LANES), ((0, share * blocks - short_rows), (0, 0))
-    )
-    gathered = exchange(padded.reshape(blocks, share, LANES), "ctx")
-    own_sum = jnp.sum(gathered, axis=0)
-    all_sums = exchange(jnp.broadcast_to(own_sum[None], (blocks, share, LANES)), "ctx")
-    all_sums = all_sums.reshape(share * blocks, LANES)
-    squares = jnp.sum(all_sums * all_sums)
-    tp_count = lax.axis_size("tp")
-    squares = jnp.sum(exchange(jnp.broadcast_to(squares, (tp_count, LANES)), "tp")[:, 0])
-    clip_limit = math.sqrt(3 * channels * tp_count * taps)
-    factor = jnp.minimum(1.0, clip_limit / (jnp.sqrt(squares) + 1e-06))
-    grad_short = (all_sums[:short_rows] * factor).reshape(3, taps, channels)
-
+    gathered = exchange(short_part.reshape(blocks, share, LANES), "ctx")
     late = passed_along(grad_mix[:, : lead * SUBS : SUBS, :], -1)
     late = jnp.pad(late, ((0, 0), (0, HALO - lead), (0, 0)))
+    gathered, late = lax.optimization_barrier((gathered, late))
+    own_sum = pl.pallas_call(
+        fold_kernel,
+        in_specs=[in_vmem],
+        out_specs=in_vmem,
+        out_shape=shaped(F32, blocks, share, LANES),
+        compiler_params=small,
+        name="fold",
+    )(gathered)
+    all_sums = exchange(own_sum, "ctx")
     grad_inputs = pl.pallas_call(
         back_kernel,
         grid=grid,
@@ -481,6 +522,27 @@
         cost_estimate=cost(work * 48, work * 12),
         name="back",
     )(grad_mix, late, short_filter)
+    all_sums, grad_inputs = lax.optimization_barrier((all_sums, grad_inputs))
+    all_sums = all_sums.reshape(short_rows, groups, LANES)
+    tp_count = lax.axis_size("tp")
+    squares = pl.pallas_call(
+        square_kernel,
+        in_specs=[in_vmem],
+        out_specs=in_vmem,
+        out_shape=shaped(F32, tp_count, LANES),
+        compiler_params=small,
+        name="square",
+    )(all_sums)
+    squares = exchange(squares, "tp")
+    clip_limit = math.sqrt(3 * channels * tp_count * taps)
+    grad_short = pl.pallas_call(
+        functools.partial(scale_kernel, clip_limit),
+        in_specs=[in_vmem, in_vmem],
+        out_specs=in_vmem,
+        out_shape=shaped(F32, 3, taps, channels),
+        compiler_params=small,
+        name="scale",
+    )(all_sums, squares)
     return (grad_inputs, grad_short)
 
 

time: 160 us -> 140 us (0.88)
  local copies, waits for them, and re-layouts: 23.1 us -> 3.18 us
  blocking collectives: 24.9 us -> 35 us
  starting transfers between devices: 47 us -> 40.4 us
  waiting for transfers between devices: 30.1 us -> 25.8 us
  Pallas kernels: 30.6 us -> 33.9 us
    unnamed x42 -> x4, local copies, waits for them, and re-layouts: 18.4 us -> 0.63 us
    all_to_all x1 -> x2, blocking collectives: 24.9 us -> 35 us  [exchange(): return lax.all_to_all(blocks, axis, split_axis=0, concat_axis=0, tiled=True)]
    all_to_all x4 -> x3, waiting for transfers between devices: 28.9 us -> 20.6 us  [exchange(): return lax.all_to_all(blocks, axis, split_axis=0, concat_axis=0, tiled=True)]
    all_to_all x4 -> x3, starting transfers between devices: 41.3 us -> 34.8 us  [exchange(): return lax.all_to_all(blocks, axis, split_axis=0, concat_axis=0, tiled=True)]
    ppermute x2, waiting for transfers between devices: 1.16 us -> 5.21 us  [passed_along(): return lax.ppermute(shard, 'ctx', pairs)]
    broadcast_in_dim x2 -> x0, local copies, waits for them, and re-layouts: 1.94 us -> none  [the longest x1 1.28 us: per_device(): jnp.broadcast_to(squares, (tp_count, LANES))]
  transfers between devices with their start and end apart: 6 -> 5, of which waited for: 4 -> 5; matrix products, arithmetic and copies ran while one was open for 2% -> 1% of each run, Pallas kernels for 8% -> 10%
where the time goes in v1:
time: 140 us; the launch traced here: 139 us
  starting transfers between devices  40.4 us (29%)
  blocking collectives  35 us (25%)
  Pallas kernels  33.9 us (24%)
  waiting for transfers between devices  25.8 us (18%)
  local copies, waits for them, and re-layouts  3.18 us (2%)
    all_to_all x2, blocking collectives, exchange(): return lax.all_to_all(blocks, axis, split_axis=0, concat_axis=0, tiled=True)  35 us
    all_to_all x3, starting transfers between devices, exchange(): return lax.all_to_all(blocks, axis, split_axis=0, concat_axis=0, tiled=True)  34.8 us
    all_to_all x3, waiting for transfers between devices, exchange(): return lax.all_to_all(blocks, axis, split_axis=0, concat_axis=0, tiled=True)  20.6 us
    pallas_call x1, Pallas kernels, per_device(): pl.pallas_call(grad_kernel, grid=grid, in_specs=[columns(3, row_count), c...  9.58 us
    pallas_call x1, Pallas kernels, per_device(): pl.pallas_call(mix_kernel, grid=grid, in_specs=[columns(3, row_count), co...  8.31 us
    pallas_call x1, Pallas kernels, per_device(): pl.pallas_call(local_kernel, grid=grid, in_specs=[columns(row_count), col...  7.5 us
    pallas_call x1, Pallas kernels, per_device(): pl.pallas_call(back_kernel, grid=grid, in_specs=[columns(3, row_count), c...  6.76 us
    ppermute x2, starting transfers between devices, passed_along(): return lax.ppermute(shard, 'ctx', pairs)  5.65 us
  transfers between devices with their start and end apart: 5, of which 5 were waited for; matrix products, arithmetic and copies ran while one was open for 1% of the time, Pallas kernels for 10%

profile of v1, /device:TPU:1, one launch (start us, length us, event | category | flops | bytes accessed | tf_op | source)
XLA Modules:
  0.0 139.0 jit_solution(9491296939375445177)
XLA Ops:
  0.6 0.0 copy-start
  0.6 0.8 slice.6
  1.5 4.4 %collective-permute-start = (bf16[3,8,1024]{2,1,0:T(8,128)(2,1)S(1)}, bf16[3,8,1024]{2,1,0:T(8,128)(2,1)S(1)}, u32[]{:S(2)}, u32[]{:S(2)}) collective-permute-start(bf16[3,8,1024]{2,1,0:T(8,128)(2,1)S(1)} %slice.6), channel_id=1, source_target_pairs={{0,8},{8,16},{16,24},{24,32},{32,40},{40,48},{48,56},{56,64},{64,7... | collective-permute-start | bytes 147464 | tf_op jit(solution)/shard_map/ppermute | solution.py:357
  5.8 1.2 collective-permute-done.prev_ref
  7.0 0.0 copy-start.1
  7.0 0.6 copy-done.1
  7.6 8.3 %mix.1 = (f32[2,256,1024]{2,1,0:T(8,128)}, f32[256,1024]{1,0:T(8,128)}, f32[256,1024]{1,0:T(8,128)}, f32[32,8,128]{2,1,0:T(8,128)}) custom-call(bf16[3,256,1024]{2,1,0:T(8,128)(2,1)} %x_ref.3, bf16[3,8,1024]{2,1,0:T(8,128)(2,1)} %copy-done.1, bf16[256,1024]{1,0:T(8,128)(2,1)} %cot_ref.3, f32[3,7,1024]{2,1,0:T(8,128)} %filt_ref.3, f32[16,1024]{1,0:T(8,128)} %rate_ref.5), custom_call_target="tpu_custom_call" | custom-call | flops 28835840 | bytes 6291456 | tf_op jit(solution)/shard_map/mix/pallas_call | solution.py:400
  15.9 19.8 %all-to-all-start = ((f32[64,4,128]{2,1,0:T(4,128)}), f32[64,4,128]{2,1,0:T(4,128)S(1)}, u32[]{:S(2)}, u32[]{:S(2)}) async-start(f32[64,4,128]{2,1,0:T(4,128)} %bitcast.16), calls=%async_computation | async-start | bytes 262144 | tf_op jit(solution)/shard_map/all_to_all | solution.py:361
  35.7 0.0 copy-done
  35.8 7.5 %local.1 = (f32[256,1024]{1,0:T(8,128)}, f32[256,1024]{1,0:T(8,128)}, f32[2,16,8,1024]{3,2,1,0:T(8,128)}) custom-call(f32[256,1024]{1,0:T(8,128)} %get-tuple-element.21.gated_ref, f32[256,1024]{1,0:T(8,128)} %get-tuple-element.22.gradm_ref, f32[16,1024]{1,0:T(8,128)} %residue_ref.3, f32[16,1024]{1,0:T(8,128)} %rate_ref.5), custom_call_target="tpu_custom_call" | custom-call | flops 33554432 | bytes 4718592 | tf_op jit(solution)/shard_map/local/pallas_call | solution.py:432
  43.3 6.5 %all-to-all-done.arrived_ref = f32[64,4,128]{2,1,0:T(4,128)S(1)} async-done(((f32[64,4,128]{2,1,0:T(4,128)}), f32[64,4,128]{2,1,0:T(4,128)S(1)}, u32[]{:S(2)}, u32[]{:S(2)}) %all-to-all-start) | async-done | bytes 131104 | tf_op jit(solution)/shard_map/all_to_all | solution.py:361
  49.8 0.1 chain.1
  49.9 22.0 %all_to_all.31 = f32[64,4,128]{2,1,0:T(4,128)} all-to-all(f32[64,4,128]{2,1,0:T(4,128)S(1)} %chain.1), channel_id=1, replica_groups=mesh['ctx'=64,'tp'=8] {'ctx'}, dimensions={0} | all-to-all | bytes 262144 | tf_op jit(solution)/shard_map/all_to_all | solution.py:361
  71.9 9.6 %grad.1 = (bf16[3,256,1024]{2,1,0:T(8,128)(2,1)}, f32[32,8,128]{2,1,0:T(8,128)}) custom-call(bf16[3,256,1024]{2,1,0:T(8,128)(2,1)} %x_ref.3, bf16[3,8,1024]{2,1,0:T(8,128)(2,1)} %copy-done.1, bf16[256,1024]{1,0:T(8,128)(2,1)} %cot_ref.3, f32[2,256,1024]{2,1,0:T(8,128)} %get-tuple-element.19.kv_ref, f32[256,1024]{1,0:T(8,128)} %get-tuple-element.26.ahead_ref, ...), custom_call_target="tpu_custom_call" | custom-call | flops 28835840 | bytes 7864320 | tf_op jit(solution)/shard_map/grad/pallas_call | solution.py:469
  81.5 5.5 %all-to-all-start.2 = ((f32[64,4,128]{2,1,0:T(4,128)}), f32[64,4,128]{2,1,0:T(4,128)S(1)}, u32[]{:S(2)}, u32[]{:S(2)}) async-start(f32[64,4,128]{2,1,0:T(4,128)} %bitcast.17), calls=%async_computation.2 | async-start | bytes 262144 | tf_op jit(solution)/shard_map/all_to_all | solution.py:361
  87.0 1.0 slice.7
  88.0 1.3 collective-permute-start.1
  89.3 4.1 %collective-permute-done.1 = bf16[3,6,1024]{2,1,0:T(8,128)(2,1)S(1)} collective-permute-done((bf16[3,6,1024]{2,1,0:T(8,128)(2,1)S(1)}, bf16[3,6,1024]{2,1,0:T(8,128)(2,1)S(1)}, u32[]{:S(2)}, u32[]{:S(2)}) %collective-permute-start.1) | collective-permute-done | bytes 36896 | tf_op jit(solution)/shard_map/ppermute | solution.py:357
  93.4 0.6 pad.4.next_ref
  94.0 6.9 %all-to-all-done.2.part_ref = f32[64,4,128]{2,1,0:T(4,128)S(1)} async-done(((f32[64,4,128]{2,1,0:T(4,128)}), f32[64,4,128]{2,1,0:T(4,128)S(1)}, u32[]{:S(2)}, u32[]{:S(2)}) %all-to-all-start.2) | async-done | bytes 131104 | tf_op jit(solution)/shard_map/all_to_all | solution.py:361
  100.9 0.7 fold.1
  101.7 9.5 %all-to-all-start.3 = ((f32[64,4,128]{2,1,0:T(4,128)}), f32[64,4,128]{2,1,0:T(4,128)S(1)}, u32[]{:S(2)}, u32[]{:S(2)}) async-start(f32[64,4,128]{2,1,0:T(4,128)} %fold.1), calls=%async_computation.3 | async-start | bytes 262144 | tf_op jit(solution)/shard_map/all_to_all | solution.py:361
  111.2 6.8 %back.1 = bf16[3,256,1024]{2,1,0:T(8,128)(2,1)} custom-call(bf16[3,256,1024]{2,1,0:T(8,128)(2,1)} %get-tuple-element.31.mix_ref, bf16[3,8,1024]{2,1,0:T(8,128)(2,1)} %pad.4.next_ref, f32[3,7,1024]{2,1,0:T(8,128)} %filt_ref.3), custom_call_target="tpu_custom_call" | custom-call | flops 12582912 | bytes 3145728 | tf_op jit(solution)/shard_map/back/pallas_call | solution.py:510
  117.9 7.2 %all-to-all-done.3 = f32[64,4,128]{2,1,0:T(4,128)S(1)} async-done(((f32[64,4,128]{2,1,0:T(4,128)}), f32[64,4,128]{2,1,0:T(4,128)S(1)}, u32[]{:S(2)}, u32[]{:S(2)}) %all-to-all-start.3) | async-done | bytes 131104 | tf_op jit(solution)/shard_map/all_to_all | solution.py:361
  125.1 0.1 square.1
  125.3 13.0 %all_to_all.32 = f32[8,1,128]{2,1,0:T(1,128)S(1)} all-to-all(f32[8,1,128]{2,1,0:T(1,128)S(1)} %bitcast.13), channel_id=1, replica_groups=mesh['ctx'=64,'tp'=8] {'tp'}, dimensions={0} | all-to-all | bytes 8192 | tf_op jit(solution)/shard_map/all_to_all | solution.py:361
  138.2 0.7 scale.1
  (3 shorter events, 0.0 us)
Async XLA Ops:
  0.6 35.1 %copy-start = (f32[16,1024]{1,0:T(8,128)S(1)}, f32[16,1024]{1,0:T(8,128)}, u32[]{:S(2)}) copy-start(f32[16,1024]{1,0:T(8,128)} %rate_ref.5) | copy-start | bytes 196612
  1.5 5.5 %collective-permute-start = (bf16[3,8,1024]{2,1,0:T(8,128)(2,1)S(1)}, bf16[3,8,1024]{2,1,0:T(8,128)(2,1)S(1)}, u32[]{:S(2)}, u32[]{:S(2)}) collective-permute-start(bf16[3,8,1024]{2,1,0:T(8,128)(2,1)S(1)} %slice.6), channel_id=1, source_target_pairs={{0,8},{8,16},{16,24},{24,32},{32,40},{40,48},{48,56},{56,64},{64,7... | collective-permute-start | bytes 147464 | tf_op jit(solution)/shard_map/ppermute | solution.py:357
  7.0 0.6 copy-start.1
  15.9 33.8 %all-to-all-start = ((f32[64,4,128]{2,1,0:T(4,128)}), f32[64,4,128]{2,1,0:T(4,128)S(1)}, u32[]{:S(2)}, u32[]{:S(2)}) async-start(f32[64,4,128]{2,1,0:T(4,128)} %bitcast.16), calls=%async_computation | async-start | bytes 262144 | tf_op jit(solution)/shard_map/all_to_all | solution.py:361
  81.5 19.4 %all-to-all-start.2 = ((f32[64,4,128]{2,1,0:T(4,128)}), f32[64,4,128]{2,1,0:T(4,128)S(1)}, u32[]{:S(2)}, u32[]{:S(2)}) async-start(f32[64,4,128]{2,1,0:T(4,128)} %bitcast.17), calls=%async_computation.2 | async-start | bytes 262144 | tf_op jit(solution)/shard_map/all_to_all | solution.py:361
  88.0 5.4 %collective-permute-start.1 = (bf16[3,6,1024]{2,1,0:T(8,128)(2,1)S(1)}, bf16[3,6,1024]{2,1,0:T(8,128)(2,1)S(1)}, u32[]{:S(2)}, u32[]{:S(2)}) collective-permute-start(bf16[3,6,1024]{2,1,0:T(8,128)(2,1)S(1)} %slice.7), channel_id=1, source_target_pairs={{8,0},{16,8},{24,16},{32,24},{40,32},{48,40},{56,48},{64,56},{72,6... | collective-permute-start | bytes 110600 | tf_op jit(solution)/shard_map/ppermute | solution.py:357
  101.7 23.4 %all-to-all-start.3 = ((f32[64,4,128]{2,1,0:T(4,128)}), f32[64,4,128]{2,1,0:T(4,128)S(1)}, u32[]{:S(2)}, u32[]{:S(2)}) async-start(f32[64,4,128]{2,1,0:T(4,128)} %fold.1), calls=%async_computation.3 | async-start | bytes 262144 | tf_op jit(solution)/shard_map/all_to_all | solution.py:361

commit v2 on v1

v2 whole, which is shorter than its diff:
```python
import functools
import math

import jax
import jax.numpy as jnp
from jax import lax
from jax.experimental import pallas as pl
from jax.experimental.pallas import tpu as pltpu
from jax.sharding import PartitionSpec as P

LANES = 128
SUBS = 8
HALO = 8
CHUNK = 16
F32 = jnp.float32
BF16 = jnp.bfloat16


def sub_index():
    return lax.broadcasted_iota(jnp.int32, (SUBS, LANES), 0)


def step_major(row_count, inverse):
    kept = lax.broadcasted_iota(jnp.int32, (row_count, row_count), 1 if inverse else 0)
    time = lax.broadcasted_iota(jnp.int32, (row_count, row_count), 0 if inverse else 1)
    source = (kept & (SUBS - 1)) * (row_count // SUBS) + (kept >> 3)
    return jnp.where(source == time, 1.0, 0.0).astype(BF16)


def spread(row):
    return jnp.broadcast_to(row, (SUBS, LANES))


def step_rows(first, count=1):
    return pl.ds(pl.multiple_of(first * SUBS, SUBS), count * SUBS)


def kept(value):
    return value.astype(BF16).astype(F32)


def added(terms):
    while len(terms) > 1:
        odd = terms[-1:] if len(terms) % 2 else []
        terms = [a + b for a, b in zip(terms[::2], terms[1::2])] + odd
    return terms[0]


def tapped(weights, rows):
    return added([w * r for w, r in zip(weights, rows)])


def each_group(groups, body):
    def step(group, carry):
        body(group)
        return carry

    lax.fori_loop(0, groups, step, 0)


def slabs(sems, pairs):
    def of(group):
        return [
            pltpu.make_async_copy(source.at[group], target.at[group], sems.at[index, group])
            for index, (source, target) in enumerate(pairs)
        ]

    return of


def start_all(copies):
    for copy in copies:
        copy.start()


def wait_all(copies):
    for copy in copies:
        copy.wait()


def earlier_rows(held, first_row, early, group, part, lanes, lead):
    steps = (held.shape[2] - first_row) // SUBS
    made = []
    for step in range(lead):
        late = held[group, part, pl.ds(first_row + (steps - lead + step) * SUBS, SUBS), :]
        first = early[part, pl.ds(HALO - lead + step, 1), lanes]
        made.append(jnp.where(sub_index() == 0, spread(first), pltpu.roll(late, 1, 0)))
    return made


def short_weights(filt_ref, lanes):
    return [
        [spread(filt_ref[part, pl.ds(k, 1), lanes]) for k in range(filt_ref.shape[1])]
        for part in range(3)
    ]


def short_chunk(weights, window):
    taps = len(weights)
    return [tapped(weights, window[at : at + taps][::-1]) for at in range(CHUNK)]


def load_rows(x_ref, cot_ref, held, cot_held, wide, sems):
    row_count, channels = cot_ref.shape
    copies = [
        pltpu.make_async_copy(x_ref.at[part] if part < 3 else cot_ref, wide.at[part], sems.at[part])
        for part in range(4)
    ]
    start_all(copies)
    perm = step_major(row_count, False)
    lead_rows = held.shape[2] - row_count
    for part, copy in enumerate(copies):
        copy.wait()
        rows = jnp.dot(perm, wide[part], preferred_element_type=F32)
        for group in range(channels // LANES):
            slab = rows[:, group * LANES : (group + 1) * LANES]
            if part < 3:
                held[group, part, pl.ds(lead_rows, row_count), :] = slab
            else:
                cot_held[group] = slab


def load_kernel(
    x_ref, cot_ref, filt_ref, rate_ref, residue_ref,
    held_ref, cot_held_ref, filt_out, rate_out, residue_out,
    wide, sems, small_sems,
):
    sources = [filt_ref, rate_ref, residue_ref]
    targets = [filt_out, rate_out, residue_out]
    copies = [
        pltpu.make_async_copy(source, target, small_sems.at[index])
        for index, (source, target) in enumerate(zip(sources, targets))
    ]
    start_all(copies)
    load_rows(x_ref, cot_ref, held_ref, cot_held_ref, wide, sems)
    wait_all(copies)


def stage_kernel(
    x_ref, cot_ref, prev_ref, filt_ref, held_out, cot_out, kv_out,
    held, cot_held, kv, early, wide, sems, out_sems,
):
    groups, row_count, _ = cot_out.shape
    lead = filt_ref.shape[1] - 1
    load_rows(x_ref, cot_ref, held, cot_held, wide, sems)
    early[...] = prev_ref[...].astype(F32)
    leaving = slabs(out_sems, [(held, held_out), (cot_held, cot_out), (kv, kv_out)])

    def one_group(group):
        lanes = pl.ds(pl.multiple_of(group * LANES, LANES), LANES)
        for part in range(3):
            rows = earlier_rows(held, lead * SUBS, early, group, part, lanes, lead)
            for step in range(lead):
                held[group, part, step_rows(step), :] = rows[step]
        weights = short_weights(filt_ref, lanes)

        def stage_chunk(index, carry):
            base = index * CHUNK
            for part in (1, 2):
                window = [held[group, part, step_rows(base + at), :] for at in range(CHUNK + lead)]
                rows = short_chunk(weights[part], window)
                for at in range(CHUNK):
                    kv[group, part - 1, step_rows(base + at), :] = rows[at]
            return carry

        lax.fori_loop(0, row_count // SUBS // CHUNK, stage_chunk, 0)
        start_all(leaving(group))

    each_group(groups, one_group)
    each_group(groups, lambda group: wait_all(leaving(group)))


def mix_kernel(
    held, prev_ref, cot_ref, filt_ref, rate_ref, gated, gradm, state_ref, early
):
    groups, row_count, _ = cot_ref.shape
    taps = filt_ref.shape[1]
    modes = rate_ref.shape[0]
    lead = taps - 1
    steps = row_count // SUBS
    early[...] = prev_ref[...].astype(F32)

    def one_group(group):
        lanes = pl.ds(pl.multiple_of(group * LANES, LANES), LANES)
        weights = short_weights(filt_ref, lanes)

        def mix_rows(base, window_of):
            key_rows = short_chunk(weights[1], window_of(1))
            value_rows = short_chunk(weights[2], window_of(2))
            for at in range(CHUNK):
                gated[group, step_rows(base + at), :] = kept(key_rows[at] * value_rows[at])
            query_rows = short_chunk(weights[0], window_of(0))
            for at in range(CHUNK):
                rows = step_rows(base + at)
                gradm[group, rows, :] = kept(cot_ref[group, rows, :] * query_rows[at])

        def inner(base, count):
            return lambda part: [
                held[group, part, step_rows(base + at), :] for at in range(count)
            ]

        def mix_chunk(index, carry):
            base = index * CHUNK
            mix_rows(base, inner(base - lead, CHUNK + lead))
            return carry

        mix_rows(
            0,
            lambda part: earlier_rows(held, 0, early, group, part, lanes, lead)
            + inner(0, CHUNK)(part),
        )
        lax.fori_loop(1, steps // CHUNK, mix_chunk, 0)
        decay = [spread(jnp.exp(-rate_ref[pl.ds(n, 1), lanes])) for n in range(modes)]

        def gather_step(step, carry):
            ends, starts = carry
            ahead = gated[group, step_rows(step), :]
            behind = gradm[group, step_rows(steps - 1 - step), :]
            return (
                [e * d + ahead for e, d in zip(ends, decay)],
                [s * d + behind for s, d in zip(starts, decay)],
            )

        zero = jnp.zeros((SUBS, LANES), F32)
        ends, starts = lax.fori_loop(
            0, steps, gather_step, ([zero] * modes, [zero] * modes), unroll=32
        )
        place = pl.ds(group, 1)
        seg = sub_index().astype(F32) * steps
        for n in range(modes):
            rate = spread(rate_ref[pl.ds(n, 1), lanes])
            to_start = jnp.exp(-rate * seg)
            to_end = jnp.exp(-rate * (steps * (SUBS - 1) - seg))
            state_ref[n, place, :] = jnp.sum(ends[n] * to_end, axis=0, keepdims=True)
            state_ref[modes + n, place, :] = jnp.sum(
                starts[n] * to_start, axis=0, keepdims=True
            )

    each_group(groups, one_group)


def chain_kernel(row_count, half, first_ref, arrived_ref, rate_ref, residue_ref, out_ref):
    blocks = arrived_ref.shape[0]
    step_decay = jnp.exp(-rate_ref[...] * row_count)
    weight = residue_ref[...] * jnp.exp(-rate_ref[...])

    def run(order):
        def body(index, carry):
            block = order(index)
            out_ref[pl.ds(block, 1)] = (carry * weight)[None]
            return carry * step_decay + arrived_ref[pl.ds(block, 1)][0]

        lax.fori_loop(0, blocks, body, jnp.zeros(rate_ref.shape, F32), unroll=32)

    @pl.when(first_ref[0] < half)
    def _():
        run(lambda index: index)

    @pl.when(first_ref[0] >= half)
    def _():
        run(lambda index: blocks - 1 - index)


def local_kernel(
    gated, gradm, residue_ref, rate_ref,
    ahead, behind, seg_out,
    seg_states, sems,
):
    groups, row_count, _ = gated.shape
    modes = rate_ref.shape[0]
    steps = row_count // SUBS
    leaving = slabs(sems, [(seg_states, seg_out)])

    def one_group(group):
        lanes = pl.ds(pl.multiple_of(group * LANES, LANES), LANES)
        weight = [spread(residue_ref[pl.ds(n, 1), lanes]) for n in range(modes)]
        rates = [rate_ref[pl.ds(n, 1), lanes] for n in range(modes)]
        decay = [spread(jnp.exp(-r)) for r in rates]
        zero = jnp.zeros((SUBS, LANES), F32)
        for source, target, backward in ((gated, ahead, False), (gradm, behind, True)):

            def scan_chunk(index, states):
                base = (steps // CHUNK - 1 - index if backward else index) * CHUNK
                values = [source[group, step_rows(base + at), :] for at in range(CHUNK)]
                made = [None] * CHUNK
                for at in range(CHUNK)[:: -1 if backward else 1]:
                    states = [s * d + values[at] for s, d in zip(states, decay)]
                    made[at] = tapped(weight, states)
                for at in range(CHUNK):
                    target[group, step_rows(base + at), :] = made[at]
                return states

            states = lax.fori_loop(0, steps // CHUNK, scan_chunk, [zero] * modes)
            sub = sub_index()
            for n in range(modes):
                span = spread(jnp.exp(-rates[n] * steps))
                total = states[n]
                for shift in (1, 2, 4):
                    if backward:
                        moved = jnp.where(
                            sub < SUBS - shift, pltpu.roll(total, SUBS - shift, 0), 0.0
                        )
                    else:
                        moved = jnp.where(sub >= shift, pltpu.roll(total, shift, 0), 0.0)
                    total = total + span * moved
                    span = span * span
                if backward:
                    enters = jnp.where(sub < SUBS - 1, pltpu.roll(total, SUBS - 1, 0), 0.0)
                else:
                    enters = jnp.where(sub >= 1, pltpu.roll(total, 1, 0), 0.0)
                seg_states[group, int(backward), n] = enters * weight[n] * decay[n]
        start_all(leaving(group))

    each_group(groups, one_group)
    each_group(groups, lambda group: wait_all(leaving(group)))


def grad_kernel(
    held_ref, cot_ref, kv_ref, seg_ref, ahead, behind, enter_ref, rate_ref,
    query_mix, key_mix, value_mix, head_ref, short_ref,
    held, cot, kv, seg_states, sems,
):
    groups, row_count, _ = cot.shape
    arriving = slabs(
        sems, [(seg_ref, seg_states), (cot_ref, cot), (held_ref, held), (kv_ref, kv)]
    )
    each_group(groups, lambda group: start_all(arriving(group)))
    modes = rate_ref.shape[0]
    steps = row_count // SUBS
    lead = held.shape[2] // SUBS - steps
    taps = lead + 1
    mix = (query_mix, key_mix, value_mix)
    short_ref[...] = jnp.zeros(short_ref.shape, F32)
    head_ref[...] = jnp.zeros(head_ref.shape, BF16)

    def one_group(group):
        lanes = pl.ds(pl.multiple_of(group * LANES, LANES), LANES)
        place = pl.ds(group, 1)
        rates = [spread(rate_ref[pl.ds(n, 1), lanes]) for n in range(modes)]
        decay = [jnp.exp(-r) for r in rates]
        seg = sub_index().astype(F32) * steps
        wait_all(arriving(group))
        for backward in (False, True):
            gap = steps * (SUBS - 1) - seg if backward else seg
            carried = []
            for n in range(modes):
                outer = spread(enter_ref[int(backward) * modes + n, place, :])
                inner = seg_states[group, int(backward), n]
                carried.append(inner + jnp.exp(-rates[n] * gap) * outer)
            parts = (1, 2) if backward else (0,)
            def grad_chunk(index, carry):
                carried, sums = carry
                base = (steps // CHUNK - 1 - index if backward else index) * CHUNK
                source = behind if backward else ahead
                long_rows = [None] * CHUNK
                for at in range(CHUNK)[:: -1 if backward else 1]:
                    long_rows[at] = source[group, step_rows(base + at), :] + added(carried)
                    carried = [c * d for c, d in zip(carried, decay)]
                new_sums = []
                for part, old in zip(parts, sums):
                    grads = []
                    for at in range(CHUNK):
                        rows = step_rows(base + at)
                        factor = cot[group, rows, :] if part == 0 else kv[group, 2 - part, rows, :]
                        grads.append(kept(long_rows[at] * factor))
                        mix[part][group, rows, :] = grads[at]
                    window = [
                        held[group, part, step_rows(base + at), :] for at in range(CHUNK + lead)
                    ]
                    new_sums.append(
                        [
                            old[k] + tapped(grads, window[lead - k : lead - k + CHUNK])
                            for k in range(taps)
                        ]
                    )
                return carried, new_sums

            zero = jnp.zeros((SUBS, LANES), F32)
            _, sums = lax.fori_loop(
                0, steps // CHUNK, grad_chunk, (carried, [[zero] * taps for _ in parts])
            )
            for part, taken in zip(parts, sums):
                for k in range(taps):
                    short_ref[part * taps + k, place, :] = jnp.sum(taken[k], axis=0, keepdims=True)
                first = [mix[part][group, pl.ds(step * SUBS, 1), :] for step in range(lead)]
                first += [jnp.zeros((1, LANES), F32)] * (HALO - lead)
                head_ref[part, :, lanes] = jnp.concatenate(first, axis=0).astype(BF16)

    each_group(groups, one_group)


def back_kernel(
    query_mix, key_mix, value_mix, next_ref, filt_ref, out_ref, late, made, wide, sems
):
    mix = (query_mix, key_mix, value_mix)
    taps = filt_ref.shape[1]
    row_count, channels = made.shape
    groups = channels // LANES
    steps = row_count // SUBS
    perm = step_major(row_count, True)
    late[...] = next_ref[...].astype(F32)
    copies = []
    for part in range(3):

        def one_group(group):
            lanes = pl.ds(pl.multiple_of(group * LANES, LANES), LANES)
            weights = [spread(filt_ref[part, pl.ds(k, 1), lanes]) for k in range(taps)]

            def back_rows(base, window):
                rows = [tapped(weights, window[at : at + taps]) for at in range(CHUNK)]
                made[step_rows(base, CHUNK), lanes] = jnp.concatenate(rows, axis=0).astype(BF16)

            def back_chunk(index, carry):
                base = index * CHUNK
                back_rows(
                    base,
                    [mix[part][group, step_rows(base + at), :] for at in range(CHUNK + taps - 1)],
                )
                return carry

            last = steps - CHUNK
            lax.fori_loop(0, last // CHUNK, back_chunk, 0)
            window = [mix[part][group, step_rows(last + at), :] for at in range(CHUNK)]
            for step in range(taps - 1):
                first = mix[part][group, step_rows(step), :]
                row = late[part, pl.ds(step, 1), lanes]
                window.append(
                    jnp.where(sub_index() == SUBS - 1, spread(row), pltpu.roll(first, SUBS - 1, 0))
                )
            back_rows(last, window)

        each_group(groups, one_group)
        wide[part] = jnp.dot(perm, made[...], preferred_element_type=F32).astype(BF16)
        copies.append(pltpu.make_async_copy(wide.at[part], out_ref.at[part], sems.at[part]))
        copies[-1].start()
    wait_all(copies)


def fold_kernel(part_ref, out_ref):
    total = jnp.sum(part_ref[...], axis=0, keepdims=True)
    out_ref[...] = jnp.broadcast_to(total, out_ref.shape)


def square_kernel(sums_ref, out_ref):
    value = sums_ref[...]
    total = jnp.sum(jnp.sum(value * value, axis=0))
    out_ref[...] = jnp.full(out_ref.shape, total, F32)


def scale_kernel(clip_limit, sums_ref, squares_ref, out_ref):
    squares = jnp.sum(squares_ref[...], axis=0, keepdims=True)
    factor = jnp.minimum(1.0, clip_limit / (jnp.sqrt(squares) + 1e-06))
    taps = out_ref.shape[1]
    for part in range(3):
        for k in range(taps):
            rows = sums_ref[part * taps + k] * factor
            for group in range(rows.shape[0]):
                out_ref[part, pl.ds(k, 1), pl.ds(group * LANES, LANES)] = rows[group : group + 1]


def passed_along(shard, by):
    length = lax.axis_size("ctx")
    pairs = [(i, i + by) for i in range(length) if 0 <= i + by < length]
    return lax.ppermute(shard, "ctx", pairs)


def exchange(blocks, axis):
    return lax.all_to_all(blocks, axis, split_axis=0, concat_axis=0, tiled=True)


def cost(flops, bytes_accessed):
    return pl.CostEstimate(flops=flops, bytes_accessed=bytes_accessed, transcendentals=0)


def per_device(inputs, cotangent, short_filter, residue, decay_rate):
    _, row_count, channels = inputs.shape
    taps = short_filter.shape[1]
    modes = residue.shape[0]
    blocks = lax.axis_size("ctx")
    groups = channels // LANES
    lead = taps - 1
    long_rows = row_count + lead * SUBS

    def shaped(dtype, *dims):
        return jax.ShapeDtypeStruct(dims, dtype)

    def near(dtype, *dims):
        return pltpu.VMEM(dims, dtype)

    def far(dtype, *dims):
        return pltpu.HBM(dims, dtype)

    def from_near(*values):
        return [pltpu.with_memory_space_constraint(v, pltpu.VMEM) for v in values]

    def from_far(*values):
        return [pltpu.with_memory_space_constraint(v, pltpu.HBM) for v in values]

    small = pltpu.CompilerParams(vmem_limit_bytes=4 << 20)
    params = pltpu.CompilerParams(vmem_limit_bytes=24 << 20)
    at_vmem = pl.BlockSpec(memory_space=pltpu.VMEM)
    at_hbm = pl.BlockSpec(memory_space=pltpu.HBM)
    sems = pltpu.SemaphoreType.DMA
    work = row_count * channels
    held_dims = (groups, 3, long_rows, LANES)
    part_dims = (groups, 3, row_count, LANES)
    row_dims = (groups, row_count, LANES)
    kv_dims = (groups, 2, row_count, LANES)
    seg_dims = (groups, 2, modes, SUBS, LANES)

    held, cot_held, filt, rate, weight = pl.pallas_call(
        load_kernel,
        in_specs=[at_hbm] * 5,
        out_specs=[at_vmem] * 5,
        out_shape=[
            near(F32, *part_dims),
            near(F32, *row_dims),
            near(F32, 3, taps, channels),
            near(F32, modes, channels),
            near(F32, modes, channels),
        ],
        scratch_shapes=[pltpu.VMEM((4, row_count, channels), BF16), sems((4,)), sems((3,))],
        compiler_params=params,
        cost_estimate=cost(work * 2000, work * 8),
        name="load",
    )(*from_far(inputs, cotangent, short_filter, decay_rate, residue))
    prev = passed_along(inputs[:, row_count - HALO :, :], 1)
    prev, held, cot_held = lax.optimization_barrier((prev, held, cot_held))
    gated, gradm, states = pl.pallas_call(
        mix_kernel,
        in_specs=[at_vmem] * 5,
        out_specs=[at_vmem] * 3,
        out_shape=[
            near(F32, *row_dims),
            near(F32, *row_dims),
            shaped(F32, 2 * modes, groups, LANES),
        ],
        scratch_shapes=[pltpu.VMEM((3, HALO, channels), F32)],
        compiler_params=params,
        cost_estimate=cost(work * 110, work * 24),
        name="mix",
    )(*from_near(held), prev, *from_near(cot_held, filt, rate))

    state_rows = 2 * modes * groups // blocks
    first = lax.axis_index("ctx") * state_rows
    half = modes * groups
    arrived = exchange(states.reshape(blocks, state_rows, LANES), "ctx")
    held, cot_held, kv = pl.pallas_call(
        stage_kernel,
        in_specs=[at_hbm] * 2 + [at_vmem] * 2,
        out_specs=[at_hbm] * 3,
        out_shape=[far(F32, *held_dims), far(F32, *row_dims), far(F32, *kv_dims)],
        scratch_shapes=[
            pltpu.VMEM(held_dims, F32),
            pltpu.VMEM(row_dims, F32),
            pltpu.VMEM(kv_dims, F32),
            pltpu.VMEM((3, HALO, channels), F32),
            pltpu.VMEM((4, row_count, channels), BF16),
            sems((4,)),
            sems((3, groups)),
        ],
        compiler_params=params,
        cost_estimate=cost(work * 2000, work * 18),
        name="stage",
    )(*from_far(inputs, cotangent), prev, filt)
    arrived, held, cot_held, kv = lax.optimization_barrier((arrived, held, cot_held, kv))


    def own_rows(values):
        rows = jnp.tile(values.reshape(half, LANES), (2, 1))
        return lax.dynamic_slice_in_dim(rows, first, state_rows, 0)

    entering = pl.pallas_call(
        functools.partial(chain_kernel, row_count, half),
        in_specs=[
            pl.BlockSpec(memory_space=pltpu.SMEM),
            at_vmem,
            at_vmem,
            at_vmem,
        ],
        out_specs=at_vmem,
        out_shape=shaped(F32, blocks, state_rows, LANES),
        compiler_params=small,
        cost_estimate=cost(blocks * state_rows * LANES * 2, blocks * state_rows * LANES * 8),
        name="chain",
    )(first[None], arrived, own_rows(decay_rate), own_rows(residue))
    entering = exchange(entering, "ctx").reshape(2 * modes, groups, LANES)

    ahead, behind, seg_states = pl.pallas_call(
        local_kernel,
        in_specs=[at_vmem] * 4,
        out_specs=[at_vmem] * 2 + [at_hbm],
        out_shape=[near(F32, *row_dims), near(F32, *row_dims), far(F32, *seg_dims)],
        scratch_shapes=[pltpu.VMEM(seg_dims, F32), sems((1, groups))],
        input_output_aliases={0: 0, 1: 1},
        compiler_params=params,
        cost_estimate=cost(work * 128, work * 18),
        name="local",
    )(*from_near(gated, gradm), weight, rate)
    entering, seg_states = lax.optimization_barrier((entering, seg_states))

    share = -(-3 * taps * groups // blocks)
    share += share % 2
    short_rows = share * blocks // groups
    *grad_mix, head, short_part = pl.pallas_call(
        grad_kernel,
        in_specs=[at_hbm] * 4 + [at_vmem] * 4,
        out_specs=[at_vmem] * 5,
        out_shape=[
            near(F32, *row_dims),
            near(F32, *row_dims),
            near(F32, *row_dims),
            shaped(BF16, 3, HALO, channels),
            far(F32, short_rows, groups, LANES),
        ],
        scratch_shapes=[
            pltpu.VMEM(held_dims, F32),
            pltpu.VMEM(row_dims, F32),
            pltpu.VMEM(kv_dims, F32),
            pltpu.VMEM(seg_dims, F32),
            sems((4, groups)),
        ],
        input_output_aliases={4: 0, 5: 1},
        compiler_params=params,
        cost_estimate=cost(work * 110, work * 30),
        name="grad",
    )(
        *from_far(held, cot_held, kv, seg_states), *from_near(ahead, behind), entering, rate
    )

    gathered = exchange(short_part.reshape(blocks, share, LANES), "ctx")
    late = passed_along(head, -1)
    own_sum = pl.pallas_call(
        fold_kernel,
        in_specs=[at_vmem],
        out_specs=at_vmem,
        out_shape=shaped(F32, blocks, share, LANES),
        compiler_params=small,
        name="fold",
    )(gathered)
    own_sum, late = lax.optimization_barrier((own_sum, late))
    all_sums = exchange(own_sum, "ctx")
    grad_inputs = pl.pallas_call(
        back_kernel,
        in_specs=[at_vmem] * 5,
        out_specs=at_hbm,
        out_shape=far(BF16, 3, row_count, channels),
        scratch_shapes=[
            pltpu.VMEM((3, HALO, channels), F32),
            pltpu.VMEM((row_count, channels), BF16),
            pltpu.VMEM((3, row_count, channels), BF16),
            sems((3,)),
        ],
        compiler_params=params,
        cost_estimate=cost(work * 48, work * 12),
        name="back",
    )(*from_near(*grad_mix), late, filt)
    all_sums, grad_inputs = lax.optimization_barrier((all_sums, grad_inputs))
    all_sums = all_sums.reshape(short_rows, groups, LANES)
    tp_count = lax.axis_size("tp")
    squares = pl.pallas_call(
        square_kernel,
        in_specs=[at_vmem],
        out_specs=at_vmem,
        out_shape=shaped(F32, tp_count, LANES),
        compiler_params=small,
        name="square",
    )(all_sums)
    squares = exchange(squares, "tp")
    clip_limit = math.sqrt(3 * channels * tp_count * taps)
    grad_short = pl.pallas_call(
        functools.partial(scale_kernel, clip_limit),
        in_specs=[at_vmem, at_vmem],
        out_specs=at_vmem,
        out_shape=shaped(F32, 3, taps, channels),
        compiler_params=small,
        name="scale",
    )(all_sums, squares)
    return (grad_inputs, grad_short)


def solution(mesh):
    return jax.shard_map(
        per_device,
        mesh=mesh,
        in_specs=(
            P(None, "ctx", "tp"),
            P("ctx", "tp"),
            P(None, None, "tp"),
            P(None, "tp"),
            P(None, "tp"),
        ),
        out_specs=(P(None, "ctx", "tp"), P(None, None, "tp")),
        check_vma=False,
    )
```

time: 140 us -> 131 us (0.936)
  blocking collectives: 35 us -> 14.6 us
  waiting for transfers between devices: 25.8 us -> 39.3 us
  starting transfers between devices: 40.4 us -> 43 us
  local copies, waits for them, and re-layouts: 3.18 us -> 0.89 us
  Pallas kernels: 33.9 us -> 31.7 us
    all_to_all x2 -> x1, blocking collectives: 35 us -> 14.6 us  [exchange(): return lax.all_to_all(blocks, axis, split_axis=0, concat_axis=0, tiled=True)]
    all_to_all x3 -> x4, waiting for transfers between devices: 20.6 us -> 39.3 us  [exchange(): return lax.all_to_all(blocks, axis, split_axis=0, concat_axis=0, tiled=True)]
    ppermute x2, waiting for transfers between devices: 5.21 us -> 0.01 us  [passed_along(): return lax.ppermute(shard, 'ctx', pairs)]
    pallas_call x7 -> x9, Pallas kernels: 33.7 us -> 30.9 us  [the longest x1 6.93 us: per_device(): pl.pallas_call(grad_kernel, in_specs=[at_hbm] * 4 + [at_vmem] * 4, out_sp...]
    all_to_all x3 -> x4, starting transfers between devices: 34.8 us -> 37.3 us  [exchange(): return lax.all_to_all(blocks, axis, split_axis=0, concat_axis=0, tiled=True)]
  transfers between devices with their start and end apart: 5 -> 6, of which waited for: 5 -> 4; matrix products, arithmetic and copies ran while one was open for 1% -> 0% of each run, Pallas kernels for 10% -> 14%
where the time goes in v2:
time: 131 us; the launch traced here: 130 us
  starting transfers between devices  43 us (33%)
  waiting for transfers between devices  39.3 us (30%)
  Pallas kernels  31.7 us (24%)
  blocking collectives  14.6 us (11%)
    all_to_all x4, waiting for transfers between devices, exchange(): return lax.all_to_all(blocks, axis, split_axis=0, concat_axis=0, tiled=True)  39.3 us
    all_to_all x4, starting transfers between devices, exchange(): return lax.all_to_all(blocks, axis, split_axis=0, concat_axis=0, tiled=True)  37.3 us
    all_to_all x1, blocking collectives, exchange(): return lax.all_to_all(blocks, axis, split_axis=0, concat_axis=0, tiled=True)  14.6 us
    pallas_call x1, Pallas kernels, per_device(): pl.pallas_call(grad_kernel, in_specs=[at_hbm] * 4 + [at_vmem] * 4, out_sp...  6.93 us
    pallas_call x1, Pallas kernels, per_device(): pl.pallas_call(local_kernel, in_specs=[at_vmem] * 4, out_specs=[at_vmem]...  6.36 us
    ppermute x2, starting transfers between devices, passed_along(): return lax.ppermute(shard, 'ctx', pairs)  5.65 us
    pallas_call x1, Pallas kernels, per_device(): pl.pallas_call(stage_kernel, in_specs=[at_hbm] * 2 + [at_vmem] * 2, out_s...  5.39 us
    pallas_call x1, Pallas kernels, per_device(): pl.pallas_call(mix_kernel, in_specs=[at_vmem] * 5, out_specs=[at_vmem] *...  4.88 us
  transfers between devices with their start and end apart: 6, of which 4 were waited for; matrix products, arithmetic and copies ran while one was open for 0% of the time, Pallas kernels for 14%

profile of v2, /device:TPU:1, one launch (start us, length us, event | category | flops | bytes accessed | tf_op | source)
XLA Modules:
  0.0 130.2 jit_solution(482452881799460272)
XLA Ops:
  0.6 0.8 slice.3
  1.4 4.4 %collective-permute-start = (bf16[3,8,1024]{2,1,0:T(8,128)(2,1)S(1)}, bf16[3,8,1024]{2,1,0:T(8,128)(2,1)S(1)}, u32[]{:S(2)}, u32[]{:S(2)}) collective-permute-start(bf16[3,8,1024]{2,1,0:T(8,128)(2,1)S(1)} %slice.3), channel_id=1, source_target_pairs={{0,8},{8,16},{16,24},{24,32},{32,40},{40,48},{48,56},{56,64},{64,7... | collective-permute-start | bytes 147464 | tf_op jit(solution)/shard_map/ppermute | solution.py:464
  5.8 2.3 %load.1 = (f32[8,3,256,128]{3,2,1,0:T(8,128)S(1)}, f32[8,256,128]{2,1,0:T(8,128)S(1)}, f32[3,7,1024]{2,1,0:T(8,128)S(1)}, f32[16,1024]{1,0:T(8,128)S(1)}, f32[16,1024]{1,0:T(8,128)S(1)}) custom-call(bf16[3,256,1024]{2,1,0:T(8,128)(2,1)} %x_ref.3, bf16[256,1024]{1,0:T(8,128)(2,1)} %cot_ref.3, f32[3,7,1024]{2,1,0:T(8,128)} %filt_ref.1, f32[16,1024]{1,0:T(8,128)} %rate_ref.1, ...), custom_call_target="tpu_custom_call" | custom-call | flops 524288000 | bytes 2097152 | tf_op jit(solution)/shard_map/load/pallas_call | solution.py:511
  8.1 0.0 collective-permute-done.prev_ref
  8.2 0.0 copy-start
  8.2 0.0 copy-start.1
  8.2 4.9 %mix.1 = (f32[8,256,128]{2,1,0:T(8,128)S(1)}, f32[8,256,128]{2,1,0:T(8,128)S(1)}, f32[32,8,128]{2,1,0:T(8,128)}) custom-call(f32[8,3,256,128]{3,2,1,0:T(8,128)S(1)} %get-tuple-element.36.held, bf16[3,8,1024]{2,1,0:T(8,128)(2,1)S(1)} %collective-permute-done.prev_ref, f32[8,256,128]{2,1,0:T(8,128)S(1)} %get-tuple-element.38.cot_ref, ...), custom_call_target="tpu_custom_call" | custom-call | flops 28835840 | bytes 6291456 | tf_op jit(solution)/shard_map/mix/pallas_call | solution.py:529
  13.1 18.6 %all-to-all-start = ((f32[64,4,128]{2,1,0:T(4,128)}), f32[64,4,128]{2,1,0:T(4,128)S(1)}, u32[]{:S(2)}, u32[]{:S(2)}) async-start(f32[64,4,128]{2,1,0:T(4,128)} %bitcast), calls=%async_computation | async-start | bytes 262144 | tf_op jit(solution)/shard_map/all_to_all | solution.py:468
  31.6 0.0 copy-done
  31.7 0.0 copy-done.1
  31.8 5.4 %stage.1 = (f32[8,3,304,128]{3,2,1,0:T(8,128)}, f32[8,256,128]{2,1,0:T(8,128)}, f32[8,2,256,128]{3,2,1,0:T(8,128)}) custom-call(bf16[3,256,1024]{2,1,0:T(8,128)(2,1)} %x_ref.3, bf16[256,1024]{1,0:T(8,128)(2,1)} %cot_ref.3, bf16[3,8,1024]{2,1,0:T(8,128)(2,1)S(1)} %collective-permute-done.prev_ref, f32[3,7,1024]{2,1,0:T(8,128)S(1)} %get-tuple-element.39.filt_ref), custom_call_target="tpu_custom_call" | custom-call | flops 524288000 | bytes 4718592 | tf_op jit(solution)/shard_map/stage/pallas_call | solution.py:548
  37.2 8.5 %all-to-all-done.arrived_ref = f32[64,4,128]{2,1,0:T(4,128)S(1)} async-done(((f32[64,4,128]{2,1,0:T(4,128)}), f32[64,4,128]{2,1,0:T(4,128)S(1)}, u32[]{:S(2)}, u32[]{:S(2)}) %all-to-all-start) | async-done | bytes 131104 | tf_op jit(solution)/shard_map/all_to_all | solution.py:468
  45.7 0.8 chain.1
  46.5 6.1 %all-to-all-start.1 = ((f32[64,4,128]{2,1,0:T(4,128)}), f32[64,4,128]{2,1,0:T(4,128)S(1)}, u32[]{:S(2)}, u32[]{:S(2)}) async-start(f32[64,4,128]{2,1,0:T(4,128)} %chain.1), calls=%async_computation.1 | async-start | bytes 262144 | tf_op jit(solution)/shard_map/all_to_all | solution.py:468
  52.6 6.4 %local.1 = (f32[8,256,128]{2,1,0:T(8,128)S(1)}, f32[8,256,128]{2,1,0:T(8,128)S(1)}, f32[8,2,16,8,128]{4,3,2,1,0:T(8,128)}) custom-call(f32[8,256,128]{2,1,0:T(8,128)S(1)} %get-tuple-element.49.gated, f32[8,256,128]{2,1,0:T(8,128)S(1)} %get-tuple-element.50.gradm, ...), custom_call_target="tpu_custom_call", output_to_operand_aliasing={{0}: (0, {}), {1}: (1, {})} | custom-call | flops 33554432 | bytes 4718592 | tf_op jit(solution)/shard_map/local/pallas_call | solution.py:589
  58.9 7.6 %all-to-all-done.1 = f32[64,4,128]{2,1,0:T(4,128)S(1)} async-done(((f32[64,4,128]{2,1,0:T(4,128)}), f32[64,4,128]{2,1,0:T(4,128)S(1)}, u32[]{:S(2)}, u32[]{:S(2)}) %all-to-all-start.1) | async-done | bytes 131104 | tf_op jit(solution)/shard_map/all_to_all | solution.py:468
  66.5 6.9 %grad.1 = (f32[8,256,128]{2,1,0:T(8,128)S(1)}, f32[8,256,128]{2,1,0:T(8,128)S(1)}, f32[8,256,128]{2,1,0:T(8,128)S(1)}, bf16[3,8,1024]{2,1,0:T(8,128)(2,1)S(1)}, f32[32,8,128]{2,1,0:T(8,128)}) custom-call(f32[8,3,304,128]{3,2,1,0:T(8,128)} %get-tuple-element.45.held_ref, ...), custom_call_target="tpu_custom_call", output_to_operand_aliasing={{0}: (4, {}), {1}: (5, {})} | custom-call | flops 28835840 | bytes 7864320 | tf_op jit(solution)/shard_map/grad/pallas_call | solution.py:605
  73.5 7.0 %all-to-all-start.2 = ((f32[64,4,128]{2,1,0:T(4,128)}), f32[64,4,128]{2,1,0:T(4,128)S(1)}, u32[]{:S(2)}, u32[]{:S(2)}) async-start(f32[64,4,128]{2,1,0:T(4,128)} %bitcast.18), calls=%async_computation.2 | async-start | bytes 262144 | tf_op jit(solution)/shard_map/all_to_all | solution.py:468
  80.5 1.3 collective-permute-start.1
  81.8 12.7 %all-to-all-done.2.part_ref = f32[64,4,128]{2,1,0:T(4,128)S(1)} async-done(((f32[64,4,128]{2,1,0:T(4,128)}), f32[64,4,128]{2,1,0:T(4,128)S(1)}, u32[]{:S(2)}, u32[]{:S(2)}) %all-to-all-start.2) | async-done | bytes 131104 | tf_op jit(solution)/shard_map/all_to_all | solution.py:468
  94.4 0.7 fold.1
  95.2 0.0 collective-permute-done.1.next_ref
  95.2 5.6 %all-to-all-start.3 = ((f32[64,4,128]{2,1,0:T(4,128)}), f32[64,4,128]{2,1,0:T(4,128)S(1)}, u32[]{:S(2)}, u32[]{:S(2)}) async-start(f32[64,4,128]{2,1,0:T(4,128)} %fold.1), calls=%async_computation.3 | async-start | bytes 262144 | tf_op jit(solution)/shard_map/all_to_all | solution.py:468
  100.8 3.4 %back.1 = bf16[3,256,1024]{2,1,0:T(8,128)(2,1)} custom-call(f32[8,256,128]{2,1,0:T(8,128)S(1)} %get-tuple-element.60.query_mix, f32[8,256,128]{2,1,0:T(8,128)S(1)} %get-tuple-element.61.key_mix, f32[8,256,128]{2,1,0:T(8,128)S(1)} %get-tuple-element.62.value_mix, bf16[3,8,1024]{2,1,0:T(8,128)(2,1)S(1)} %collective-permute-done.1.next_ref, ...), custom_call_target="tpu_custom_call" | custom-call | flops 12582912 | bytes 3145728 | tf_op jit(solution)/shard_map/back/pallas_call | solution.py:643
  104.2 10.6 %all-to-all-done.3 = f32[64,4,128]{2,1,0:T(4,128)S(1)} async-done(((f32[64,4,128]{2,1,0:T(4,128)}), f32[64,4,128]{2,1,0:T(4,128)S(1)}, u32[]{:S(2)}, u32[]{:S(2)}) %all-to-all-start.3) | async-done | bytes 131104 | tf_op jit(solution)/shard_map/all_to_all | solution.py:468
  114.8 0.1 square.1
  114.9 14.6 %all_to_all.31 = f32[8,1,128]{2,1,0:T(1,128)S(1)} all-to-all(f32[8,1,128]{2,1,0:T(1,128)S(1)} %bitcast.15), channel_id=1, replica_groups=mesh['ctx'=64,'tp'=8] {'tp'}, dimensions={0} | all-to-all | bytes 8192 | tf_op jit(solution)/shard_map/all_to_all | solution.py:468
  129.5 0.7 scale.1
  (5 shorter events, 0.1 us)
Async XLA Ops:
  1.4 6.7 %collective-permute-start = (bf16[3,8,1024]{2,1,0:T(8,128)(2,1)S(1)}, bf16[3,8,1024]{2,1,0:T(8,128)(2,1)S(1)}, u32[]{:S(2)}, u32[]{:S(2)}) collective-permute-start(bf16[3,8,1024]{2,1,0:T(8,128)(2,1)S(1)} %slice.3), channel_id=1, source_target_pairs={{0,8},{8,16},{16,24},{24,32},{32,40},{40,48},{48,56},{56,64},{64,7... | collective-permute-start | bytes 147464 | tf_op jit(solution)/shard_map/ppermute | solution.py:464
  8.2 23.5 %copy-start = (f32[16,1024]{1,0:T(8,128)S(1)}, f32[16,1024]{1,0:T(8,128)}, u32[]{:S(2)}) copy-start(f32[16,1024]{1,0:T(8,128)} %residue_ref.1) | copy-start | bytes 196612
  8.2 23.5 %copy-start.1 = (f32[16,1024]{1,0:T(8,128)S(1)}, f32[16,1024]{1,0:T(8,128)}, u32[]{:S(2)}) copy-start(f32[16,1024]{1,0:T(8,128)} %rate_ref.1) | copy-start | bytes 196612
  13.1 32.6 %all-to-all-start = ((f32[64,4,128]{2,1,0:T(4,128)}), f32[64,4,128]{2,1,0:T(4,128)S(1)}, u32[]{:S(2)}, u32[]{:S(2)}) async-start(f32[64,4,128]{2,1,0:T(4,128)} %bitcast), calls=%async_computation | async-start | bytes 262144 | tf_op jit(solution)/shard_map/all_to_all | solution.py:468
  46.5 20.1 %all-to-all-start.1 = ((f32[64,4,128]{2,1,0:T(4,128)}), f32[64,4,128]{2,1,0:T(4,128)S(1)}, u32[]{:S(2)}, u32[]{:S(2)}) async-start(f32[64,4,128]{2,1,0:T(4,128)} %chain.1), calls=%async_computation.1 | async-start | bytes 262144 | tf_op jit(solution)/shard_map/all_to_all | solution.py:468
  73.5 21.0 %all-to-all-start.2 = ((f32[64,4,128]{2,1,0:T(4,128)}), f32[64,4,128]{2,1,0:T(4,128)S(1)}, u32[]{:S(2)}, u32[]{:S(2)}) async-start(f32[64,4,128]{2,1,0:T(4,128)} %bitcast.18), calls=%async_computation.2 | async-start | bytes 262144 | tf_op jit(solution)/shard_map/all_to_all | solution.py:468
  80.5 14.7 %collective-permute-start.1 = (bf16[3,8,1024]{2,1,0:T(8,128)(2,1)S(1)}, bf16[3,8,1024]{2,1,0:T(8,128)(2,1)S(1)}, u32[]{:S(2)}, u32[]{:S(2)}) collective-permute-start(bf16[3,8,1024]{2,1,0:T(8,128)(2,1)S(1)} %get-tuple-element.58), channel_id=1, source_target_pairs={{8,0},{16,8},{24,16},{32,24},{40,32},{48,40},{56,48},{64,56},{72,6... | collective-permute-start | bytes 147464 | tf_op jit(solution)/shard_map/ppermute | solution.py:464
  95.2 19.6 %all-to-all-start.3 = ((f32[64,4,128]{2,1,0:T(4,128)}), f32[64,4,128]{2,1,0:T(4,128)S(1)}, u32[]{:S(2)}, u32[]{:S(2)}) async-start(f32[64,4,128]{2,1,0:T(4,128)} %fold.1), calls=%async_computation.3 | async-start | bytes 262144 | tf_op jit(solution)/shard_map/all_to_all | solution.py:468

commit v3 on v2

--- a/solution.py
+++ b/solution.py
@@ -12,6 +12,7 @@
 SUBS = 8
 HALO = 8
 CHUNK = 16
+LINES = 4
 F32 = jnp.float32
 BF16 = jnp.bfloat16
 
@@ -316,7 +317,7 @@
 
 
 def grad_kernel(
-    held_ref, cot_ref, kv_ref, seg_ref, ahead, behind, enter_ref, rate_ref,
+    share, held_ref, cot_ref, kv_ref, seg_ref, ahead, behind, enter_ref, rate_ref,
     query_mix, key_mix, value_mix, head_ref, short_ref,
     held, cot, kv, seg_states, sems,
 ):
@@ -381,7 +382,10 @@
             )
             for part, taken in zip(parts, sums):
                 for k in range(taps):
-                    short_ref[part * taps + k, place, :] = jnp.sum(taken[k], axis=0, keepdims=True)
+                    row = (part * taps + k) * groups + group
+                    short_ref[row // share, pl.ds(row % share, 1), :] = jnp.sum(
+                        taken[k], axis=0, keepdims=True
+                    )
                 first = [mix[part][group, pl.ds(step * SUBS, 1), :] for step in range(lead)]
                 first += [jnp.zeros((1, LANES), F32)] * (HALO - lead)
                 head_ref[part, :, lanes] = jnp.concatenate(first, axis=0).astype(BF16)
@@ -436,26 +440,41 @@
     wait_all(copies)
 
 
-def fold_kernel(part_ref, out_ref):
-    total = jnp.sum(part_ref[...], axis=0, keepdims=True)
-    out_ref[...] = jnp.broadcast_to(total, out_ref.shape)
-
-
-def square_kernel(sums_ref, out_ref):
-    value = sums_ref[...]
-    total = jnp.sum(jnp.sum(value * value, axis=0))
-    out_ref[...] = jnp.full(out_ref.shape, total, F32)
-
-
-def scale_kernel(clip_limit, sums_ref, squares_ref, out_ref):
-    squares = jnp.sum(squares_ref[...], axis=0, keepdims=True)
+def line_kernel(part_ref, out_ref):
+    columns = out_ref.shape[1]
+    lines = part_ref.shape[0] // columns
+    for column in range(columns):
+        total = added([part_ref[line * columns + column] for line in range(lines)])
+        for plane in range(out_ref.shape[0]):
+            out_ref[plane, column] = total.astype(BF16)
+
+
+def plane_kernel(share, part_ref, out_ref):
+    planes, columns, rows, _ = part_ref.shape
+    totals = [
+        added([part_ref[plane, column].astype(F32) for plane in range(planes)])
+        for column in range(columns)
+    ]
+    squares = jnp.sum(added([total * total for total in totals]))
+    at_row = lax.broadcasted_iota(jnp.int32, (rows, LANES), 0)
+    for column in range(columns):
+        marked = jnp.where(at_row == share, squares, totals[column])
+        for line in range(out_ref.shape[0] // columns):
+            out_ref[line * columns + column] = marked
+
+
+def scale_kernel(clip_limit, share, sums_ref, out_ref):
+    squares = added([sums_ref[piece, share : share + 1, :] for piece in range(sums_ref.shape[0])])
     factor = jnp.minimum(1.0, clip_limit / (jnp.sqrt(squares) + 1e-06))
-    taps = out_ref.shape[1]
+    _, taps, channels = out_ref.shape
+    groups = channels // LANES
     for part in range(3):
         for k in range(taps):
-            rows = sums_ref[part * taps + k] * factor
-            for group in range(rows.shape[0]):
-                out_ref[part, pl.ds(k, 1), pl.ds(group * LANES, LANES)] = rows[group : group + 1]
+            for group in range(groups):
+                piece, row = divmod((part * taps + k) * groups + group, share)
+                out_ref[part, k : k + 1, pl.ds(group * LANES, LANES)] = (
+                    sums_ref[piece, row : row + 1, :] * factor
+                )
 
 
 def passed_along(shard, by):
@@ -464,8 +483,10 @@
     return lax.ppermute(shard, "ctx", pairs)
 
 
-def exchange(blocks, axis):
-    return lax.all_to_all(blocks, axis, split_axis=0, concat_axis=0, tiled=True)
+def exchange(blocks, axis, members=None):
+    return lax.all_to_all(
+        blocks, axis, split_axis=0, concat_axis=0, tiled=True, axis_index_groups=members
+    )
 
 
 def cost(flops, bytes_accessed):
@@ -599,11 +620,18 @@
     )(*from_near(gated, gradm), weight, rate)
     entering, seg_states = lax.optimization_barrier((entering, seg_states))
 
-    share = -(-3 * taps * groups // blocks)
-    share += share % 2
-    short_rows = share * blocks // groups
+    tp_count = lax.axis_size("tp")
+    planes = blocks // LINES
+    in_plane = LINES * tp_count
+    share = -(-3 * taps * groups // in_plane)
+    piece_rows = -(-(share + 1) // SUBS) * SUBS
+    plane_members = [
+        [(y * planes + z) * tp_count + m for y in range(LINES) for m in range(tp_count)]
+        for z in range(planes)
+    ]
+    line_members = [[y * planes + z for z in range(planes)] for y in range(LINES)]
     *grad_mix, head, short_part = pl.pallas_call(
-        grad_kernel,
+        functools.partial(grad_kernel, share),
         in_specs=[at_hbm] * 4 + [at_vmem] * 4,
         out_specs=[at_vmem] * 5,
         out_shape=[
@@ -611,7 +639,7 @@
             near(F32, *row_dims),
             near(F32, *row_dims),
             shaped(BF16, 3, HALO, channels),
-            far(F32, short_rows, groups, LANES),
+            far(F32, in_plane, piece_rows, LANES),
         ],
         scratch_shapes=[
             pltpu.VMEM(held_dims, F32),
@@ -628,18 +656,18 @@
         *from_far(held, cot_held, kv, seg_states), *from_near(ahead, behind), entering, rate
     )
 
-    gathered = exchange(short_part.reshape(blocks, share, LANES), "ctx")
+    gathered = exchange(short_part, ("ctx", "tp"), plane_members)
     late = passed_along(head, -1)
     own_sum = pl.pallas_call(
-        fold_kernel,
+        line_kernel,
         in_specs=[at_vmem],
         out_specs=at_vmem,
-        out_shape=shaped(F32, blocks, share, LANES),
+        out_shape=shaped(BF16, planes, tp_count, piece_rows, LANES),
         compiler_params=small,
-        name="fold",
+        name="line",
     )(gathered)
     own_sum, late = lax.optimization_barrier((own_sum, late))
-    all_sums = exchange(own_sum, "ctx")
+    all_sums = exchange(own_sum, "ctx", line_members)
     grad_inputs = pl.pallas_call(
         back_kernel,
         in_specs=[at_vmem] * 5,
@@ -656,26 +684,24 @@
         name="back",
     )(*from_near(*grad_mix), late, filt)
     all_sums, grad_inputs = lax.optimization_barrier((all_sums, grad_inputs))
-    all_sums = all_sums.reshape(short_rows, groups, LANES)
-    tp_count = lax.axis_size("tp")
-    squares = pl.pallas_call(
-        square_kernel,
+    all_sums = pl.pallas_call(
+        functools.partial(plane_kernel, share),
         in_specs=[at_vmem],
         out_specs=at_vmem,
-        out_shape=shaped(F32, tp_count, LANES),
+        out_shape=shaped(F32, in_plane, piece_rows, LANES),
         compiler_params=small,
-        name="square",
+        name="plane",
     )(all_sums)
-    squares = exchange(squares, "tp")
+    all_sums = exchange(all_sums, ("ctx", "tp"), plane_members)
     clip_limit = math.sqrt(3 * channels * tp_count * taps)
     grad_short = pl.pallas_call(
-        functools.partial(scale_kernel, clip_limit),
-        in_specs=[at_vmem, at_vmem],
+        functools.partial(scale_kernel, clip_limit, share),
+        in_specs=[at_vmem],
         out_specs=at_vmem,
         out_shape=shaped(F32, 3, taps, channels),
         compiler_params=small,
         name="scale",
-    )(all_sums, squares)
+    )(all_sums)
     return (grad_inputs, grad_short)
 
 

time: 131 us -> 129 us (0.985)
  waiting for transfers between devices: 39.3 us -> 32.9 us
  blocking collectives: 14.6 us -> 17.2 us
    all_to_all x4, waiting for transfers between devices: 39.3 us -> 32.9 us  [exchange(): lax.all_to_all(blocks, axis, split_axis=0, concat_axis=0, tiled=True, axi...]
    all_to_all x1, blocking collectives: 14.6 us -> 17.2 us  [exchange(): lax.all_to_all(blocks, axis, split_axis=0, concat_axis=0, tiled=True, axi...]
where the time goes in v3:
time: 129 us; the launch traced here: 128 us
  starting transfers between devices  44 us (34%)
  waiting for transfers between devices  32.9 us (26%)
  Pallas kernels  32.4 us (25%)
  blocking collectives  17.2 us (13%)
    all_to_all x4, starting transfers between devices, exchange(): lax.all_to_all(blocks, axis, split_axis=0, concat_axis=0, tiled=True, axi...  38.3 us
    all_to_all x4, waiting for transfers between devices, exchange(): lax.all_to_all(blocks, axis, split_axis=0, concat_axis=0, tiled=True, axi...  32.9 us
    all_to_all x1, blocking collectives, exchange(): lax.all_to_all(blocks, axis, split_axis=0, concat_axis=0, tiled=True, axi...  17.2 us
    pallas_call x1, Pallas kernels, per_device(): pl.pallas_call(functools.partial(grad_kernel, share), in_specs=[at_hbm] *...  7.64 us
    pallas_call x1, Pallas kernels, per_device(): pl.pallas_call(local_kernel, in_specs=[at_vmem] * 4, out_specs=[at_vmem]...  6.36 us
    ppermute x2, starting transfers between devices, passed_along(): return lax.ppermute(shard, 'ctx', pairs)  5.65 us
    pallas_call x1, Pallas kernels, per_device(): pl.pallas_call(stage_kernel, in_specs=[at_hbm] * 2 + [at_vmem] * 2, out_s...  5.39 us
    pallas_call x1, Pallas kernels, per_device(): pl.pallas_call(mix_kernel, in_specs=[at_vmem] * 5, out_specs=[at_vmem] *...  4.88 us
  transfers between devices with their start and end apart: 6, of which 4 were waited for; matrix products, arithmetic and copies ran while one was open for 0% of the time, Pallas kernels for 14%

profile of v3, /device:TPU:1, one launch (start us, length us, event | category | flops | bytes accessed | tf_op | source)
XLA Modules:
  0.0 128.2 jit_solution(1001812413744324086)
XLA Ops:
  0.6 0.8 slice.3
  1.4 4.4 %collective-permute-start = (bf16[3,8,1024]{2,1,0:T(8,128)(2,1)S(1)}, bf16[3,8,1024]{2,1,0:T(8,128)(2,1)S(1)}, u32[]{:S(2)}, u32[]{:S(2)}) collective-permute-start(bf16[3,8,1024]{2,1,0:T(8,128)(2,1)S(1)} %slice.3), channel_id=1, source_target_pairs={{0,8},{8,16},{16,24},{24,32},{32,40},{40,48},{48,56},{56,64},{64,7... | collective-permute-start | bytes 147464 | tf_op jit(solution)/shard_map/ppermute | solution.py:483
  5.8 2.3 %load.1 = (f32[8,3,256,128]{3,2,1,0:T(8,128)S(1)}, f32[8,256,128]{2,1,0:T(8,128)S(1)}, f32[3,7,1024]{2,1,0:T(8,128)S(1)}, f32[16,1024]{1,0:T(8,128)S(1)}, f32[16,1024]{1,0:T(8,128)S(1)}) custom-call(bf16[3,256,1024]{2,1,0:T(8,128)(2,1)} %x_ref.3, bf16[256,1024]{1,0:T(8,128)(2,1)} %cot_ref.3, f32[3,7,1024]{2,1,0:T(8,128)} %filt_ref.1, f32[16,1024]{1,0:T(8,128)} %rate_ref.1, ...), custom_call_target="tpu_custom_call" | custom-call | flops 524288000 | bytes 2097152 | tf_op jit(solution)/shard_map/load/pallas_call | solution.py:532
  8.1 0.0 collective-permute-done.prev_ref
  8.2 0.0 copy-start
  8.2 0.0 copy-start.1
  8.2 4.9 %mix.1 = (f32[8,256,128]{2,1,0:T(8,128)S(1)}, f32[8,256,128]{2,1,0:T(8,128)S(1)}, f32[32,8,128]{2,1,0:T(8,128)}) custom-call(f32[8,3,256,128]{3,2,1,0:T(8,128)S(1)} %get-tuple-element.36.held, bf16[3,8,1024]{2,1,0:T(8,128)(2,1)S(1)} %collective-permute-done.prev_ref, f32[8,256,128]{2,1,0:T(8,128)S(1)} %get-tuple-element.38.cot_ref, ...), custom_call_target="tpu_custom_call" | custom-call | flops 28835840 | bytes 6291456 | tf_op jit(solution)/shard_map/mix/pallas_call | solution.py:550
  13.1 18.6 %all-to-all-start = ((f32[64,4,128]{2,1,0:T(4,128)}), f32[64,4,128]{2,1,0:T(4,128)S(1)}, u32[]{:S(2)}, u32[]{:S(2)}) async-start(f32[64,4,128]{2,1,0:T(4,128)} %bitcast), calls=%async_computation | async-start | bytes 262144 | tf_op jit(solution)/shard_map/all_to_all | solution.py:487
  31.6 0.0 copy-done
  31.7 0.0 copy-done.1
  31.8 5.4 %stage.1 = (f32[8,3,304,128]{3,2,1,0:T(8,128)}, f32[8,256,128]{2,1,0:T(8,128)}, f32[8,2,256,128]{3,2,1,0:T(8,128)}) custom-call(bf16[3,256,1024]{2,1,0:T(8,128)(2,1)} %x_ref.3, bf16[256,1024]{1,0:T(8,128)(2,1)} %cot_ref.3, bf16[3,8,1024]{2,1,0:T(8,128)(2,1)S(1)} %collective-permute-done.prev_ref, f32[3,7,1024]{2,1,0:T(8,128)S(1)} %get-tuple-element.39.filt_ref), custom_call_target="tpu_custom_call" | custom-call | flops 524288000 | bytes 4718592 | tf_op jit(solution)/shard_map/stage/pallas_call | solution.py:569
  37.2 8.5 %all-to-all-done.arrived_ref = f32[64,4,128]{2,1,0:T(4,128)S(1)} async-done(((f32[64,4,128]{2,1,0:T(4,128)}), f32[64,4,128]{2,1,0:T(4,128)S(1)}, u32[]{:S(2)}, u32[]{:S(2)}) %all-to-all-start) | async-done | bytes 131104 | tf_op jit(solution)/shard_map/all_to_all | solution.py:487
  45.7 0.8 chain.1
  46.5 6.1 %all-to-all-start.1 = ((f32[64,4,128]{2,1,0:T(4,128)}), f32[64,4,128]{2,1,0:T(4,128)S(1)}, u32[]{:S(2)}, u32[]{:S(2)}) async-start(f32[64,4,128]{2,1,0:T(4,128)} %chain.1), calls=%async_computation.1 | async-start | bytes 262144 | tf_op jit(solution)/shard_map/all_to_all | solution.py:487
  52.6 6.4 %local.1 = (f32[8,256,128]{2,1,0:T(8,128)S(1)}, f32[8,256,128]{2,1,0:T(8,128)S(1)}, f32[8,2,16,8,128]{4,3,2,1,0:T(8,128)}) custom-call(f32[8,256,128]{2,1,0:T(8,128)S(1)} %get-tuple-element.49.gated, f32[8,256,128]{2,1,0:T(8,128)S(1)} %get-tuple-element.50.gradm, ...), custom_call_target="tpu_custom_call", output_to_operand_aliasing={{0}: (0, {}), {1}: (1, {})} | custom-call | flops 33554432 | bytes 4718592 | tf_op jit(solution)/shard_map/local/pallas_call | solution.py:610
  58.9 7.6 %all-to-all-done.1 = f32[64,4,128]{2,1,0:T(4,128)S(1)} async-done(((f32[64,4,128]{2,1,0:T(4,128)}), f32[64,4,128]{2,1,0:T(4,128)S(1)}, u32[]{:S(2)}, u32[]{:S(2)}) %all-to-all-start.1) | async-done | bytes 131104 | tf_op jit(solution)/shard_map/all_to_all | solution.py:487
  66.5 7.6 %grad.1 = (f32[8,256,128]{2,1,0:T(8,128)S(1)}, f32[8,256,128]{2,1,0:T(8,128)S(1)}, f32[8,256,128]{2,1,0:T(8,128)S(1)}, bf16[3,8,1024]{2,1,0:T(8,128)(2,1)S(1)}, f32[32,8,128]{2,1,0:T(8,128)}) custom-call(f32[8,3,304,128]{3,2,1,0:T(8,128)} %get-tuple-element.45.held_ref, ...), custom_call_target="tpu_custom_call", output_to_operand_aliasing={{0}: (4, {}), {1}: (5, {})} | custom-call | flops 28835840 | bytes 7864320 | tf_op jit(solution)/shard_map/grad/pallas_call | solution.py:633
  74.2 10.1 %all-to-all-start.2 = ((f32[32,8,128]{2,1,0:T(8,128)}), f32[32,8,128]{2,1,0:T(8,128)S(1)}, u32[]{:S(2)}, u32[]{:S(2)}) async-start(f32[32,8,128]{2,1,0:T(8,128)} %get-tuple-element.57), calls=%async_computation.2 | async-start | bytes 262144 | tf_op jit(solution)/shard_map/all_to_all | solution.py:487
  84.3 1.3 %collective-permute-start.1 = (bf16[3,8,1024]{2,1,0:T(8,128)(2,1)S(1)}, bf16[3,8,1024]{2,1,0:T(8,128)(2,1)S(1)}, u32[]{:S(2)}, u32[]{:S(2)}) collective-permute-start(bf16[3,8,1024]{2,1,0:T(8,128)(2,1)S(1)} %get-tuple-element.58), channel_id=1, source_target_pairs={{8,0},{16,8},{24,16},{32,24},{40,32},{48,40},{56,48},{64,56},{72,6... | collective-permute-start | bytes 147464 | tf_op jit(solution)/shard_map/ppermute | solution.py:483
  85.6 6.3 %all-to-all-done.2.part_ref = f32[32,8,128]{2,1,0:T(8,128)S(1)} async-done(((f32[32,8,128]{2,1,0:T(8,128)}), f32[32,8,128]{2,1,0:T(8,128)S(1)}, u32[]{:S(2)}, u32[]{:S(2)}) %all-to-all-start.2) | async-done | bytes 131104 | tf_op jit(solution)/shard_map/all_to_all | solution.py:487
  91.9 0.7 line.1
  92.7 0.0 collective-permute-done.1.next_ref
  92.7 3.6 %all-to-all-start.3 = ((bf16[16,8,8,128]{3,2,1,0:T(8,128)(2,1)}), bf16[16,8,8,128]{3,2,1,0:T(8,128)(2,1)S(1)}, u32[]{:S(2)}, u32[]{:S(2)}) async-start(bf16[16,8,8,128]{3,2,1,0:T(8,128)(2,1)} %line.1), calls=%async_computation.3 | async-start | bytes 524288 | tf_op jit(solution)/shard_map/all_to_all | solution.py:487
  96.2 3.4 %back.1 = bf16[3,256,1024]{2,1,0:T(8,128)(2,1)} custom-call(f32[8,256,128]{2,1,0:T(8,128)S(1)} %get-tuple-element.60.query_mix, f32[8,256,128]{2,1,0:T(8,128)S(1)} %get-tuple-element.61.key_mix, f32[8,256,128]{2,1,0:T(8,128)S(1)} %get-tuple-element.62.value_mix, bf16[3,8,1024]{2,1,0:T(8,128)(2,1)S(1)} %collective-permute-done.1.next_ref, ...), custom_call_target="tpu_custom_call" | custom-call | flops 12582912 | bytes 3145728 | tf_op jit(solution)/shard_map/back/pallas_call | solution.py:671
  99.6 10.5 %all-to-all-done.3.part_ref = bf16[16,8,8,128]{3,2,1,0:T(8,128)(2,1)S(1)} async-done(((bf16[16,8,8,128]{3,2,1,0:T(8,128)(2,1)}), bf16[16,8,8,128]{3,2,1,0:T(8,128)(2,1)S(1)}, u32[]{:S(2)}, u32[]{:S(2)}) %all-to-all-start.3) | async-done | bytes 262176 | tf_op jit(solution)/shard_map/all_to_all | solution.py:487
  110.1 0.2 plane.1
  110.3 17.2 %all_to_all.25.sums_ref = f32[32,8,128]{2,1,0:T(8,128)S(1)} all-to-all(f32[32,8,128]{2,1,0:T(8,128)S(1)} %plane.1), channel_id=1, replica_groups={{0,1,2,3,4,5,6,7,128,129,130,131,132,133,134,135,256,257,258,259,260,26..., dimensions={0} | all-to-all | bytes 262144 | tf_op jit(solution)/shard_map/all_to_all | solution.py:487
  127.5 0.7 scale.1
  (5 shorter events, 0.1 us)
Async XLA Ops:
  1.4 6.7 %collective-permute-start = (bf16[3,8,1024]{2,1,0:T(8,128)(2,1)S(1)}, bf16[3,8,1024]{2,1,0:T(8,128)(2,1)S(1)}, u32[]{:S(2)}, u32[]{:S(2)}) collective-permute-start(bf16[3,8,1024]{2,1,0:T(8,128)(2,1)S(1)} %slice.3), channel_id=1, source_target_pairs={{0,8},{8,16},{16,24},{24,32},{32,40},{40,48},{48,56},{56,64},{64,7... | collective-permute-start | bytes 147464 | tf_op jit(solution)/shard_map/ppermute | solution.py:483
  8.2 23.5 %copy-start = (f32[16,1024]{1,0:T(8,128)S(1)}, f32[16,1024]{1,0:T(8,128)}, u32[]{:S(2)}) copy-start(f32[16,1024]{1,0:T(8,128)} %residue_ref.1) | copy-start | bytes 196612
  8.2 23.5 %copy-start.1 = (f32[16,1024]{1,0:T(8,128)S(1)}, f32[16,1024]{1,0:T(8,128)}, u32[]{:S(2)}) copy-start(f32[16,1024]{1,0:T(8,128)} %rate_ref.1) | copy-start | bytes 196612
  13.1 32.6 %all-to-all-start = ((f32[64,4,128]{2,1,0:T(4,128)}), f32[64,4,128]{2,1,0:T(4,128)S(1)}, u32[]{:S(2)}, u32[]{:S(2)}) async-start(f32[64,4,128]{2,1,0:T(4,128)} %bitcast), calls=%async_computation | async-start | bytes 262144 | tf_op jit(solution)/shard_map/all_to_all | solution.py:487
  46.5 20.1 %all-to-all-start.1 = ((f32[64,4,128]{2,1,0:T(4,128)}), f32[64,4,128]{2,1,0:T(4,128)S(1)}, u32[]{:S(2)}, u32[]{:S(2)}) async-start(f32[64,4,128]{2,1,0:T(4,128)} %chain.1), calls=%async_computation.1 | async-start | bytes 262144 | tf_op jit(solution)/shard_map/all_to_all | solution.py:487
  74.2 17.7 %all-to-all-start.2 = ((f32[32,8,128]{2,1,0:T(8,128)}), f32[32,8,128]{2,1,0:T(8,128)S(1)}, u32[]{:S(2)}, u32[]{:S(2)}) async-start(f32[32,8,128]{2,1,0:T(8,128)} %get-tuple-element.57), calls=%async_computation.2 | async-start | bytes 262144 | tf_op jit(solution)/shard_map/all_to_all | solution.py:487
  84.3 8.4 %collective-permute-start.1 = (bf16[3,8,1024]{2,1,0:T(8,128)(2,1)S(1)}, bf16[3,8,1024]{2,1,0:T(8,128)(2,1)S(1)}, u32[]{:S(2)}, u32[]{:S(2)}) collective-permute-start(bf16[3,8,1024]{2,1,0:T(8,128)(2,1)S(1)} %get-tuple-element.58), channel_id=1, source_target_pairs={{8,0},{16,8},{24,16},{32,24},{40,32},{48,40},{56,48},{64,56},{72,6... | collective-permute-start | bytes 147464 | tf_op jit(solution)/shard_map/ppermute | solution.py:483
  92.7 17.4 %all-to-all-start.3 = ((bf16[16,8,8,128]{3,2,1,0:T(8,128)(2,1)}), bf16[16,8,8,128]{3,2,1,0:T(8,128)(2,1)S(1)}, u32[]{:S(2)}, u32[]{:S(2)}) async-start(bf16[16,8,8,128]{3,2,1,0:T(8,128)(2,1)} %line.1), calls=%async_computation.3 | async-start | bytes 524288 | tf_op jit(solution)/shard_map/all_to_all | solution.py:487

commit v4 on v3

--- a/solution.py
+++ b/solution.py
@@ -101,24 +101,20 @@
     return [tapped(weights, window[at : at + taps][::-1]) for at in range(CHUNK)]
 
 
-def load_rows(x_ref, cot_ref, held, cot_held, wide, sems):
-    row_count, channels = cot_ref.shape
+def load_rows(sources, targets, wide, sems):
+    row_count, channels = sources[0].shape
     copies = [
-        pltpu.make_async_copy(x_ref.at[part] if part < 3 else cot_ref, wide.at[part], sems.at[part])
-        for part in range(4)
+        pltpu.make_async_copy(source, wide.at[part], sems.at[part])
+        for part, source in enumerate(sources)
     ]
     start_all(copies)
     perm = step_major(row_count, False)
-    lead_rows = held.shape[2] - row_count
     for part, copy in enumerate(copies):
         copy.wait()
         rows = jnp.dot(perm, wide[part], preferred_element_type=F32)
         for group in range(channels // LANES):
             slab = rows[:, group * LANES : (group + 1) * LANES]
-            if part < 3:
-                held[group, part, pl.ds(lead_rows, row_count), :] = slab
-            else:
-                cot_held[group] = slab
+            targets[part](group)[...] = slab
 
 
 def load_kernel(
@@ -133,19 +129,34 @@
         for index, (source, target) in enumerate(zip(sources, targets))
     ]
     start_all(copies)
-    load_rows(x_ref, cot_ref, held_ref, cot_held_ref, wide, sems)
+    load_rows(
+        [x_ref.at[part] for part in range(3)] + [cot_ref],
+        [lambda group, part=part: held_ref.at[group, part] for part in range(3)]
+        + [lambda group: cot_held_ref.at[group]],
+        wide,
+        sems,
+    )
     wait_all(copies)
 
 
 def stage_kernel(
-    x_ref, cot_ref, prev_ref, filt_ref, held_out, cot_out, kv_out,
-    held, cot_held, kv, early, wide, sems, out_sems,
+    x_ref, filt_in, prev_ref, held_out, kv_out,
+    held, kv, filt_ref, early, wide, sems, filt_sem, out_sems,
 ):
-    groups, row_count, _ = cot_out.shape
+    filt_copy = pltpu.make_async_copy(filt_in, filt_ref, filt_sem.at[0])
+    filt_copy.start()
+    groups, _, row_count, _ = kv_out.shape
     lead = filt_ref.shape[1] - 1
-    load_rows(x_ref, cot_ref, held, cot_held, wide, sems)
+    below = pl.ds(lead * SUBS, row_count)
+    load_rows(
+        [x_ref.at[part] for part in range(3)],
+        [lambda group, part=part: held.at[group, part, below, :] for part in range(3)],
+        wide,
+        sems,
+    )
     early[...] = prev_ref[...].astype(F32)
-    leaving = slabs(out_sems, [(held, held_out), (cot_held, cot_out), (kv, kv_out)])
+    leaving = slabs(out_sems, [(held, held_out), (kv, kv_out)])
+    filt_copy.wait()
 
     def one_group(group):
         lanes = pl.ds(pl.multiple_of(group * LANES, LANES), LANES)
@@ -317,13 +328,13 @@
 
 
 def grad_kernel(
-    share, held_ref, cot_ref, kv_ref, seg_ref, ahead, behind, enter_ref, rate_ref,
+    share, held_ref, kv_ref, seg_ref, ahead, behind, cot, enter_ref, rate_ref,
     query_mix, key_mix, value_mix, head_ref, short_ref,
-    held, cot, kv, seg_states, sems,
+    held, kv, seg_states, short, sems,
 ):
     groups, row_count, _ = cot.shape
     arriving = slabs(
-        sems, [(seg_ref, seg_states), (cot_ref, cot), (held_ref, held), (kv_ref, kv)]
+        sems, [(seg_ref, seg_states), (held_ref, held), (kv_ref, kv)]
     )
     each_group(groups, lambda group: start_all(arriving(group)))
     modes = rate_ref.shape[0]
@@ -382,20 +393,25 @@
             )
             for part, taken in zip(parts, sums):
                 for k in range(taps):
-                    row = (part * taps + k) * groups + group
-                    short_ref[row // share, pl.ds(row % share, 1), :] = jnp.sum(
-                        taken[k], axis=0, keepdims=True
-                    )
+                    short[part * taps + k, place, :] = jnp.sum(taken[k], axis=0, keepdims=True)
                 first = [mix[part][group, pl.ds(step * SUBS, 1), :] for step in range(lead)]
                 first += [jnp.zeros((1, LANES), F32)] * (HALO - lead)
                 head_ref[part, :, lanes] = jnp.concatenate(first, axis=0).astype(BF16)
 
     each_group(groups, one_group)
+    for piece in range(short_ref.shape[0]):
+        for slot in range(share):
+            row, group = divmod(piece * share + slot, groups)
+            if row < 3 * taps:
+                short_ref[piece, slot : slot + 1, :] = short[row, group : group + 1, :]
 
 
 def back_kernel(
-    query_mix, key_mix, value_mix, next_ref, filt_ref, out_ref, late, made, wide, sems
+    query_mix, key_mix, value_mix, next_ref, filt_in, out_ref,
+    late, made, wide, filt_ref, sems, filt_sem,
 ):
+    filt_copy = pltpu.make_async_copy(filt_in, filt_ref, filt_sem.at[0])
+    filt_copy.start()
     mix = (query_mix, key_mix, value_mix)
     taps = filt_ref.shape[1]
     row_count, channels = made.shape
@@ -403,6 +419,7 @@
     steps = row_count // SUBS
     perm = step_major(row_count, True)
     late[...] = next_ref[...].astype(F32)
+    filt_copy.wait()
     copies = []
     for part in range(3):
 
@@ -440,27 +457,29 @@
     wait_all(copies)
 
 
-def line_kernel(part_ref, out_ref):
-    columns = out_ref.shape[1]
+def line_kernel(share, columns, part_ref, out_ref):
     lines = part_ref.shape[0] // columns
-    for column in range(columns):
-        total = added([part_ref[line * columns + column] for line in range(lines)])
-        for plane in range(out_ref.shape[0]):
-            out_ref[plane, column] = total.astype(BF16)
-
-
-def plane_kernel(share, part_ref, out_ref):
-    planes, columns, rows, _ = part_ref.shape
     totals = [
-        added([part_ref[plane, column].astype(F32) for plane in range(planes)])
+        added([part_ref[line * columns + column, :share, :] for line in range(lines)])
         for column in range(columns)
     ]
-    squares = jnp.sum(added([total * total for total in totals]))
-    at_row = lax.broadcasted_iota(jnp.int32, (rows, LANES), 0)
+    totals = jnp.concatenate(totals, axis=0).astype(BF16)
+    for plane in range(out_ref.shape[0]):
+        out_ref[plane] = totals
+
+
+def plane_kernel(share, part_ref, out_ref):
+    planes, rows, _ = part_ref.shape
+    piece_rows = out_ref.shape[1]
+    totals = added([part_ref[plane].astype(F32) for plane in range(planes)])
+    squares = jnp.sum(totals * totals)
+    marks = jnp.full((piece_rows - share, LANES), squares, F32)
+    columns = rows // share
     for column in range(columns):
-        marked = jnp.where(at_row == share, squares, totals[column])
+        own = totals[column * share : (column + 1) * share]
+        piece = jnp.concatenate([own, marks], axis=0)
         for line in range(out_ref.shape[0] // columns):
-            out_ref[line * columns + column] = marked
+            out_ref[line * columns + column] = piece
 
 
 def scale_kernel(clip_limit, share, sums_ref, out_ref):
@@ -554,7 +573,7 @@
         out_shape=[
             near(F32, *row_dims),
             near(F32, *row_dims),
-            shaped(F32, 2 * modes, groups, LANES),
+            far(F32, 2 * modes, groups, LANES),
         ],
         scratch_shapes=[pltpu.VMEM((3, HALO, channels), F32)],
         compiler_params=params,
@@ -566,26 +585,26 @@
     first = lax.axis_index("ctx") * state_rows
     half = modes * groups
     arrived = exchange(states.reshape(blocks, state_rows, LANES), "ctx")
-    held, cot_held, kv = pl.pallas_call(
+    held, kv = pl.pallas_call(
         stage_kernel,
-        in_specs=[at_hbm] * 2 + [at_vmem] * 2,
-        out_specs=[at_hbm] * 3,
-        out_shape=[far(F32, *held_dims), far(F32, *row_dims), far(F32, *kv_dims)],
+        in_specs=[at_hbm] * 2 + [at_vmem],
+        out_specs=[at_hbm] * 2,
+        out_shape=[far(F32, *held_dims), far(F32, *kv_dims)],
         scratch_shapes=[
             pltpu.VMEM(held_dims, F32),
-            pltpu.VMEM(row_dims, F32),
             pltpu.VMEM(kv_dims, F32),
+            pltpu.VMEM((3, taps, channels), F32),
             pltpu.VMEM((3, HALO, channels), F32),
-            pltpu.VMEM((4, row_count, channels), BF16),
-            sems((4,)),
-            sems((3, groups)),
+            pltpu.VMEM((3, row_count, channels), BF16),
+            sems((3,)),
+            sems((1,)),
+            sems((2, groups)),
         ],
         compiler_params=params,
         cost_estimate=cost(work * 2000, work * 18),
         name="stage",
-    )(*from_far(inputs, cotangent), prev, filt)
-    arrived, held, cot_held, kv = lax.optimization_barrier((arrived, held, cot_held, kv))
-
+    )(*from_far(inputs, short_filter), prev)
+    arrived, held, kv = lax.optimization_barrier((arrived, held, kv))
 
     def own_rows(values):
         rows = jnp.tile(values.reshape(half, LANES), (2, 1))
@@ -617,7 +636,7 @@
         compiler_params=params,
         cost_estimate=cost(work * 128, work * 18),
         name="local",
-    )(*from_near(gated, gradm), weight, rate)
+    )(*from_near(gated, gradm, weight, rate))
     entering, seg_states = lax.optimization_barrier((entering, seg_states))
 
     tp_count = lax.axis_size("tp")
@@ -632,7 +651,7 @@
     line_members = [[y * planes + z for z in range(planes)] for y in range(LINES)]
     *grad_mix, head, short_part = pl.pallas_call(
         functools.partial(grad_kernel, share),
-        in_specs=[at_hbm] * 4 + [at_vmem] * 4,
+        in_specs=[at_hbm] * 3 + [at_vmem] * 5,
         out_specs=[at_vmem] * 5,
         out_shape=[
             near(F32, *row_dims),
@@ -643,26 +662,26 @@
         ],
         scratch_shapes=[
             pltpu.VMEM(held_dims, F32),
-            pltpu.VMEM(row_dims, F32),
             pltpu.VMEM(kv_dims, F32),
             pltpu.VMEM(seg_dims, F32),
-            sems((4, groups)),
+            pltpu.VMEM((3 * taps, groups, LANES), F32),
+            sems((3, groups)),
         ],
-        input_output_aliases={4: 0, 5: 1},
+        input_output_aliases={3: 0, 4: 1, 5: 2},
         compiler_params=params,
         cost_estimate=cost(work * 110, work * 30),
         name="grad",
     )(
-        *from_far(held, cot_held, kv, seg_states), *from_near(ahead, behind), entering, rate
+        *from_far(held, kv, seg_states), *from_near(ahead, behind, cot_held), entering, rate
     )
 
     gathered = exchange(short_part, ("ctx", "tp"), plane_members)
     late = passed_along(head, -1)
     own_sum = pl.pallas_call(
-        line_kernel,
+        functools.partial(line_kernel, share, tp_count),
         in_specs=[at_vmem],
         out_specs=at_vmem,
-        out_shape=shaped(BF16, planes, tp_count, piece_rows, LANES),
+        out_shape=shaped(BF16, planes, tp_count * share, LANES),
         compiler_params=small,
         name="line",
     )(gathered)
@@ -670,19 +689,21 @@
     all_sums = exchange(own_sum, "ctx", line_members)
     grad_inputs = pl.pallas_call(
         back_kernel,
-        in_specs=[at_vmem] * 5,
+        in_specs=[at_vmem] * 4 + [at_hbm],
         out_specs=at_hbm,
         out_shape=far(BF16, 3, row_count, channels),
         scratch_shapes=[
             pltpu.VMEM((3, HALO, channels), F32),
             pltpu.VMEM((row_count, channels), BF16),
             pltpu.VMEM((3, row_count, channels), BF16),
+            pltpu.VMEM((3, taps, channels), F32),
             sems((3,)),
+            sems((1,)),
         ],
         compiler_params=params,
         cost_estimate=cost(work * 48, work * 12),
         name="back",
-    )(*from_near(*grad_mix), late, filt)
+    )(*from_near(*grad_mix), late, *from_far(short_filter))
     all_sums, grad_inputs = lax.optimization_barrier((all_sums, grad_inputs))
     all_sums = pl.pallas_call(
         functools.partial(plane_kernel, share),

time: 129 us -> 128 us (level)
  waiting for transfers between devices: 32.9 us -> 29.4 us
  local copies, waits for them, and re-layouts: 0.89 us -> 3.19 us
  starting transfers between devices: 44 us -> 45.5 us
    all_to_all x4, waiting for transfers between devices: 32.9 us -> 29.4 us  [exchange(): lax.all_to_all(blocks, axis, split_axis=0, concat_axis=0, tiled=True, axi...]
    another operation x4, local copies, waits for them, and re-layouts: 0.06 us -> 2.36 us  [own_rows(): rows = jnp.tile(values.reshape(half, LANES), (2, 1))]
    all_to_all x4, starting transfers between devices: 38.3 us -> 39.8 us  [exchange(): lax.all_to_all(blocks, axis, split_axis=0, concat_axis=0, tiled=True, axi...]
  transfers between devices with their start and end apart: 6 -> 6, of which waited for: 4 -> 4; matrix products, arithmetic and copies ran while one was open for 0% -> 2% of each run, Pallas kernels for 14% -> 14%
where the time goes in v4:
time: 128 us; the launch traced here: 127 us
  starting transfers between devices  45.5 us (36%)
  Pallas kernels  31.8 us (25%)
  waiting for transfers between devices  29.4 us (23%)
  blocking collectives  16.4 us (13%)
  local copies, waits for them, and re-layouts  3.19 us (2%)
    all_to_all x4, starting transfers between devices, exchange(): lax.all_to_all(blocks, axis, split_axis=0, concat_axis=0, tiled=True, axi...  39.8 us
    all_to_all x4, waiting for transfers between devices, exchange(): lax.all_to_all(blocks, axis, split_axis=0, concat_axis=0, tiled=True, axi...  29.4 us
    all_to_all x1, blocking collectives, exchange(): lax.all_to_all(blocks, axis, split_axis=0, concat_axis=0, tiled=True, axi...  16.4 us
    pallas_call x1, Pallas kernels, per_device(): pl.pallas_call(functools.partial(grad_kernel, share), in_specs=[at_hbm] *...  6.83 us
    pallas_call x1, Pallas kernels, per_device(): pl.pallas_call(local_kernel, in_specs=[at_vmem] * 4, out_specs=[at_vmem]...  6.38 us
    ppermute x2, starting transfers between devices, passed_along(): return lax.ppermute(shard, 'ctx', pairs)  5.65 us
    pallas_call x1, Pallas kernels, per_device(): pl.pallas_call(mix_kernel, in_specs=[at_vmem] * 5, out_specs=[at_vmem] *...  4.88 us
    pallas_call x1, Pallas kernels, per_device(): pl.pallas_call(stage_kernel, in_specs=[at_hbm] * 2 + [at_vmem], out_specs...  4.71 us
  transfers between devices with their start and end apart: 6, of which 4 were waited for; matrix products, arithmetic and copies ran while one was open for 2% of the time, Pallas kernels for 14%

profile of v4, /device:TPU:1, one launch (start us, length us, event | category | flops | bytes accessed | tf_op | source)
XLA Modules:
  0.0 127.0 jit_solution(1219377647157601546)
XLA Ops:
  0.6 0.8 slice.3
  1.4 4.4 %collective-permute-start = (bf16[3,8,1024]{2,1,0:T(8,128)(2,1)S(1)}, bf16[3,8,1024]{2,1,0:T(8,128)(2,1)S(1)}, u32[]{:S(2)}, u32[]{:S(2)}) collective-permute-start(bf16[3,8,1024]{2,1,0:T(8,128)(2,1)S(1)} %slice.3), channel_id=1, source_target_pairs={{0,8},{8,16},{16,24},{24,32},{32,40},{40,48},{48,56},{56,64},{64,7... | collective-permute-start | bytes 147464 | tf_op jit(solution)/shard_map/ppermute | solution.py:502
  5.8 2.3 %load.1 = (f32[8,3,256,128]{3,2,1,0:T(8,128)S(1)}, f32[8,256,128]{2,1,0:T(8,128)S(1)}, f32[3,7,1024]{2,1,0:T(8,128)S(1)}, f32[16,1024]{1,0:T(8,128)S(1)}, f32[16,1024]{1,0:T(8,128)S(1)}) custom-call(bf16[3,256,1024]{2,1,0:T(8,128)(2,1)} %x_ref.3, bf16[256,1024]{1,0:T(8,128)(2,1)} %cot_ref.1, f32[3,7,1024]{2,1,0:T(8,128)} %filt_in.3, f32[16,1024]{1,0:T(8,128)} %rate_ref.1, ...), custom_call_target="tpu_custom_call" | custom-call | flops 524288000 | bytes 2097152 | tf_op jit(solution)/shard_map/load/pallas_call | solution.py:551
  8.1 0.0 collective-permute-done.prev_ref
  8.2 0.0 copy-start
  8.2 4.9 %mix.1 = (f32[8,256,128]{2,1,0:T(8,128)S(1)}, f32[8,256,128]{2,1,0:T(8,128)S(1)}, f32[32,8,128]{2,1,0:T(8,128)}) custom-call(f32[8,3,256,128]{3,2,1,0:T(8,128)S(1)} %get-tuple-element.34.held, bf16[3,8,1024]{2,1,0:T(8,128)(2,1)S(1)} %collective-permute-done.prev_ref, f32[8,256,128]{2,1,0:T(8,128)S(1)} %get-tuple-element.36.cot_ref.cot, ...), custom_call_target="tpu_custom_call" | custom-call | flops 28835840 | bytes 6291456 | tf_op jit(solution)/shard_map/mix/pallas_call | solution.py:569
  13.0 18.6 %all-to-all-start = ((f32[64,4,128]{2,1,0:T(4,128)}), f32[64,4,128]{2,1,0:T(4,128)S(1)}, u32[]{:S(2)}, u32[]{:S(2)}) async-start(f32[64,4,128]{2,1,0:T(4,128)} %bitcast.8), calls=%async_computation | async-start | bytes 262144 | tf_op jit(solution)/shard_map/all_to_all | solution.py:506
  31.6 0.0 copy-done
  31.7 0.6 tile.23
  32.3 0.9 tile.20
  33.2 0.9 tile.24
  34.1 4.7 %stage.1 = (f32[8,3,304,128]{3,2,1,0:T(8,128)}, f32[8,2,256,128]{3,2,1,0:T(8,128)}) custom-call(bf16[3,256,1024]{2,1,0:T(8,128)(2,1)} %x_ref.3, f32[3,7,1024]{2,1,0:T(8,128)} %filt_in.3, bf16[3,8,1024]{2,1,0:T(8,128)(2,1)S(1)} %collective-permute-done.prev_ref), custom_call_target="tpu_custom_call" | custom-call | flops 524288000 | bytes 4718592 | tf_op jit(solution)/shard_map/stage/pallas_call | solution.py:588
  38.8 6.9 %all-to-all-done.arrived_ref = f32[64,4,128]{2,1,0:T(4,128)S(1)} async-done(((f32[64,4,128]{2,1,0:T(4,128)}), f32[64,4,128]{2,1,0:T(4,128)S(1)}, u32[]{:S(2)}, u32[]{:S(2)}) %all-to-all-start) | async-done | bytes 131104 | tf_op jit(solution)/shard_map/all_to_all | solution.py:506
  45.7 0.8 chain.1
  46.5 7.7 %all-to-all-start.1 = ((f32[64,4,128]{2,1,0:T(4,128)}), f32[64,4,128]{2,1,0:T(4,128)S(1)}, u32[]{:S(2)}, u32[]{:S(2)}) async-start(f32[64,4,128]{2,1,0:T(4,128)} %chain.1), calls=%async_computation.1 | async-start | bytes 262144 | tf_op jit(solution)/shard_map/all_to_all | solution.py:506
  54.2 6.4 %local.1 = (f32[8,256,128]{2,1,0:T(8,128)S(1)}, f32[8,256,128]{2,1,0:T(8,128)S(1)}, f32[8,2,16,8,128]{4,3,2,1,0:T(8,128)}) custom-call(f32[8,256,128]{2,1,0:T(8,128)S(1)} %get-tuple-element.45.gated, f32[8,256,128]{2,1,0:T(8,128)S(1)} %get-tuple-element.46.gradm, ...), custom_call_target="tpu_custom_call", output_to_operand_aliasing={{0}: (0, {}), {1}: (1, {})} | custom-call | flops 33554432 | bytes 4718592 | tf_op jit(solution)/shard_map/local/pallas_call | solution.py:629
  60.6 7.6 %all-to-all-done.1 = f32[64,4,128]{2,1,0:T(4,128)S(1)} async-done(((f32[64,4,128]{2,1,0:T(4,128)}), f32[64,4,128]{2,1,0:T(4,128)S(1)}, u32[]{:S(2)}, u32[]{:S(2)}) %all-to-all-start.1) | async-done | bytes 131104 | tf_op jit(solution)/shard_map/all_to_all | solution.py:506
  68.2 6.8 %grad.1 = (f32[8,256,128]{2,1,0:T(8,128)S(1)}, f32[8,256,128]{2,1,0:T(8,128)S(1)}, f32[8,256,128]{2,1,0:T(8,128)S(1)}, bf16[3,8,1024]{2,1,0:T(8,128)(2,1)S(1)}, f32[32,8,128]{2,1,0:T(8,128)}) custom-call(f32[8,3,304,128]{3,2,1,0:T(8,128)} %get-tuple-element.42.held_ref, ...), custom_call_target="tpu_custom_call", output_to_operand_aliasing={{0}: (3, {}), {1}: (4, {}), {2}: (5, {})} | custom-call | flops 28835840 | bytes 7864320 | tf_op jit(solution)/shard_map/grad/pallas_call | solution.py:652
  75.0 9.8 %all-to-all-start.2 = ((f32[32,8,128]{2,1,0:T(8,128)}), f32[32,8,128]{2,1,0:T(8,128)S(1)}, u32[]{:S(2)}, u32[]{:S(2)}) async-start(f32[32,8,128]{2,1,0:T(8,128)} %get-tuple-element.53), calls=%async_computation.2 | async-start | bytes 262144 | tf_op jit(solution)/shard_map/all_to_all | solution.py:506
  84.8 1.3 %collective-permute-start.1 = (bf16[3,8,1024]{2,1,0:T(8,128)(2,1)S(1)}, bf16[3,8,1024]{2,1,0:T(8,128)(2,1)S(1)}, u32[]{:S(2)}, u32[]{:S(2)}) collective-permute-start(bf16[3,8,1024]{2,1,0:T(8,128)(2,1)S(1)} %get-tuple-element.54), channel_id=1, source_target_pairs={{8,0},{16,8},{24,16},{32,24},{40,32},{48,40},{56,48},{64,56},{72,6... | collective-permute-start | bytes 147464 | tf_op jit(solution)/shard_map/ppermute | solution.py:502
  86.1 6.3 %all-to-all-done.2.part_ref = f32[32,8,128]{2,1,0:T(8,128)S(1)} async-done(((f32[32,8,128]{2,1,0:T(8,128)}), f32[32,8,128]{2,1,0:T(8,128)S(1)}, u32[]{:S(2)}, u32[]{:S(2)}) %all-to-all-start.2) | async-done | bytes 131104 | tf_op jit(solution)/shard_map/all_to_all | solution.py:506
  92.5 0.7 line.1
  93.2 0.0 collective-permute-done.1.next_ref
  93.2 3.7 %all-to-all-start.3 = ((bf16[16,48,128]{2,1,0:T(8,128)(2,1)}), bf16[16,48,128]{2,1,0:T(8,128)(2,1)S(1)}, u32[]{:S(2)}, u32[]{:S(2)}) async-start(bf16[16,48,128]{2,1,0:T(8,128)(2,1)} %line.1), calls=%async_computation.3 | async-start | bytes 393216 | tf_op jit(solution)/shard_map/all_to_all | solution.py:506
  96.9 4.2 %back.1 = bf16[3,256,1024]{2,1,0:T(8,128)(2,1)} custom-call(f32[8,256,128]{2,1,0:T(8,128)S(1)} %get-tuple-element.56.query_mix, f32[8,256,128]{2,1,0:T(8,128)S(1)} %get-tuple-element.57.key_mix, f32[8,256,128]{2,1,0:T(8,128)S(1)} %get-tuple-element.58.value_mix, bf16[3,8,1024]{2,1,0:T(8,128)(2,1)S(1)} %collective-permute-done.1.next_ref, f32[3,7,1024]{2,1,0:T(8,128)} %filt_in.3), custom_call_target="tpu_custom_call" | custom-call | flops 12582912 | bytes 3145728 | tf_op jit(solution)/shard_map/back/pallas_call | solution.py:690
  101.1 8.6 %all-to-all-done.3.part_ref = bf16[16,48,128]{2,1,0:T(8,128)(2,1)S(1)} async-done(((bf16[16,48,128]{2,1,0:T(8,128)(2,1)}), bf16[16,48,128]{2,1,0:T(8,128)(2,1)S(1)}, u32[]{:S(2)}, u32[]{:S(2)}) %all-to-all-start.3) | async-done | bytes 196640 | tf_op jit(solution)/shard_map/all_to_all | solution.py:506
  109.7 0.2 plane.1
  109.9 16.4 %all_to_all.25.sums_ref = f32[32,8,128]{2,1,0:T(8,128)S(1)} all-to-all(f32[32,8,128]{2,1,0:T(8,128)S(1)} %plane.1), channel_id=1, replica_groups={{0,1,2,3,4,5,6,7,128,129,130,131,132,133,134,135,256,257,258,259,260,26..., dimensions={0} | all-to-all | bytes 262144 | tf_op jit(solution)/shard_map/all_to_all | solution.py:506
  126.3 0.7 scale.1
  (2 shorter events, 0.0 us)
Async XLA Ops:
  1.4 6.7 %collective-permute-start = (bf16[3,8,1024]{2,1,0:T(8,128)(2,1)S(1)}, bf16[3,8,1024]{2,1,0:T(8,128)(2,1)S(1)}, u32[]{:S(2)}, u32[]{:S(2)}) collective-permute-start(bf16[3,8,1024]{2,1,0:T(8,128)(2,1)S(1)} %slice.3), channel_id=1, source_target_pairs={{0,8},{8,16},{16,24},{24,32},{32,40},{40,48},{48,56},{56,64},{64,7... | collective-permute-start | bytes 147464 | tf_op jit(solution)/shard_map/ppermute | solution.py:502
  8.2 23.5 %copy-start = (f32[16,1024]{1,0:T(8,128)S(1)}, f32[16,1024]{1,0:T(8,128)}, u32[]{:S(2)}) copy-start(f32[16,1024]{1,0:T(8,128)} %residue_ref.1) | copy-start | bytes 196612
  13.0 32.6 %all-to-all-start = ((f32[64,4,128]{2,1,0:T(4,128)}), f32[64,4,128]{2,1,0:T(4,128)S(1)}, u32[]{:S(2)}, u32[]{:S(2)}) async-start(f32[64,4,128]{2,1,0:T(4,128)} %bitcast.8), calls=%async_computation | async-start | bytes 262144 | tf_op jit(solution)/shard_map/all_to_all | solution.py:506
  46.5 21.7 %all-to-all-start.1 = ((f32[64,4,128]{2,1,0:T(4,128)}), f32[64,4,128]{2,1,0:T(4,128)S(1)}, u32[]{:S(2)}, u32[]{:S(2)}) async-start(f32[64,4,128]{2,1,0:T(4,128)} %chain.1), calls=%async_computation.1 | async-start | bytes 262144 | tf_op jit(solution)/shard_map/all_to_all | solution.py:506
  75.0 17.5 %all-to-all-start.2 = ((f32[32,8,128]{2,1,0:T(8,128)}), f32[32,8,128]{2,1,0:T(8,128)S(1)}, u32[]{:S(2)}, u32[]{:S(2)}) async-start(f32[32,8,128]{2,1,0:T(8,128)} %get-tuple-element.53), calls=%async_computation.2 | async-start | bytes 262144 | tf_op jit(solution)/shard_map/all_to_all | solution.py:506
  84.8 8.3 %collective-permute-start.1 = (bf16[3,8,1024]{2,1,0:T(8,128)(2,1)S(1)}, bf16[3,8,1024]{2,1,0:T(8,128)(2,1)S(1)}, u32[]{:S(2)}, u32[]{:S(2)}) collective-permute-start(bf16[3,8,1024]{2,1,0:T(8,128)(2,1)S(1)} %get-tuple-element.54), channel_id=1, source_target_pairs={{8,0},{16,8},{24,16},{32,24},{40,32},{48,40},{56,48},{64,56},{72,6... | collective-permute-start | bytes 147464 | tf_op jit(solution)/shard_map/ppermute | solution.py:502
  93.2 16.5 %all-to-all-start.3 = ((bf16[16,48,128]{2,1,0:T(8,128)(2,1)}), bf16[16,48,128]{2,1,0:T(8,128)(2,1)S(1)}, u32[]{:S(2)}, u32[]{:S(2)}) async-start(bf16[16,48,128]{2,1,0:T(8,128)(2,1)} %line.1), calls=%async_computation.3 | async-start | bytes 393216 | tf_op jit(solution)/shard_map/all_to_all | solution.py:506

commit v5 on v4

--- a/solution.py
+++ b/solution.py
@@ -52,11 +52,13 @@
 
 
 def each_group(groups, body):
+    first, last = groups if isinstance(groups, tuple) else (0, groups)
+
     def step(group, carry):
         body(group)
         return carry
 
-    lax.fori_loop(0, groups, step, 0)
+    lax.fori_loop(first, last, step, 0)
 
 
 def slabs(sems, pairs):
@@ -273,12 +275,9 @@
         run(lambda index: blocks - 1 - index)
 
 
-def local_kernel(
-    gated, gradm, residue_ref, rate_ref,
-    ahead, behind, seg_out,
-    seg_states, sems,
-):
-    groups, row_count, _ = gated.shape
+def local_kernel(groups, given, gated, gradm, residue_ref, rate_ref, *refs):
+    ahead, behind, seg_out, seg_states, sems = refs[given:]
+    _, row_count, _ = gated.shape
     modes = rate_ref.shape[0]
     steps = row_count // SUBS
     leaving = slabs(sems, [(seg_states, seg_out)])
@@ -565,7 +564,21 @@
         name="load",
     )(*from_far(inputs, cotangent, short_filter, decay_rate, residue))
     prev = passed_along(inputs[:, row_count - HALO :, :], 1)
-    prev, held, cot_held = lax.optimization_barrier((prev, held, cot_held))
+    state_rows = 2 * modes * groups // blocks
+    first = lax.axis_index("ctx") * state_rows
+    half = modes * groups
+
+    def own_rows(values):
+        start = lax.rem(first, half)
+        if state_rows < groups:
+            corner, taken = (start // groups, start % groups * LANES), (1, state_rows * LANES)
+        else:
+            corner, taken = (start // groups, 0), (state_rows // groups, channels)
+        return lax.dynamic_slice(values, corner, taken).reshape(state_rows, LANES)
+
+    prev, held, cot_held, own_rate, own_residue = lax.optimization_barrier(
+        (prev, held, cot_held, own_rows(decay_rate), own_rows(residue))
+    )
     gated, gradm, states = pl.pallas_call(
         mix_kernel,
         in_specs=[at_vmem] * 5,
@@ -581,9 +594,6 @@
         name="mix",
     )(*from_near(held), prev, *from_near(cot_held, filt, rate))
 
-    state_rows = 2 * modes * groups // blocks
-    first = lax.axis_index("ctx") * state_rows
-    half = modes * groups
     arrived = exchange(states.reshape(blocks, state_rows, LANES), "ctx")
     held, kv = pl.pallas_call(
         stage_kernel,
@@ -604,11 +614,27 @@
         cost_estimate=cost(work * 2000, work * 18),
         name="stage",
     )(*from_far(inputs, short_filter), prev)
-    arrived, held, kv = lax.optimization_barrier((arrived, held, kv))
-
-    def own_rows(values):
-        rows = jnp.tile(values.reshape(half, LANES), (2, 1))
-        return lax.dynamic_slice_in_dim(rows, first, state_rows, 0)
+    def local_sums(span, gated, gradm, seg_states=None):
+        seg = [] if seg_states is None else from_far(seg_states)
+        return pl.pallas_call(
+            functools.partial(local_kernel, span, len(seg)),
+            in_specs=[at_vmem] * 4 + [at_hbm] * len(seg),
+            out_specs=[at_vmem] * 2 + [at_hbm],
+            out_shape=[near(F32, *row_dims), near(F32, *row_dims), far(F32, *seg_dims)],
+            scratch_shapes=[pltpu.VMEM(seg_dims, F32), sems((1, groups))],
+            input_output_aliases={0: 0, 1: 1, **({4: 2} if seg else {})},
+            compiler_params=params,
+            cost_estimate=cost(work * 16 * (span[1] - span[0]), work * 18),
+            name="local",
+        )(*from_near(gated, gradm, weight, rate), *seg)
+
+    early_groups = groups // 8
+    if early_groups:
+        ahead, behind, seg_states = local_sums((0, early_groups), gated, gradm)
+        arrived, held, kv, seg_states = lax.optimization_barrier((arrived, held, kv, seg_states))
+    else:
+        ahead, behind, seg_states = gated, gradm, None
+        arrived, held, kv = lax.optimization_barrier((arrived, held, kv))
 
     entering = pl.pallas_call(
         functools.partial(chain_kernel, row_count, half),
@@ -623,20 +649,10 @@
         compiler_params=small,
         cost_estimate=cost(blocks * state_rows * LANES * 2, blocks * state_rows * LANES * 8),
         name="chain",
-    )(first[None], arrived, own_rows(decay_rate), own_rows(residue))
+    )(first[None], arrived, own_rate, own_residue)
     entering = exchange(entering, "ctx").reshape(2 * modes, groups, LANES)
 
-    ahead, behind, seg_states = pl.pallas_call(
-        local_kernel,
-        in_specs=[at_vmem] * 4,
-        out_specs=[at_vmem] * 2 + [at_hbm],
-        out_shape=[near(F32, *row_dims), near(F32, *row_dims), far(F32, *seg_dims)],
-        scratch_shapes=[pltpu.VMEM(seg_dims, F32), sems((1, groups))],
-        input_output_aliases={0: 0, 1: 1},
-        compiler_params=params,
-        cost_estimate=cost(work * 128, work * 18),
-        name="local",
-    )(*from_near(gated, gradm, weight, rate))
+    ahead, behind, seg_states = local_sums((early_groups, groups), ahead, behind, seg_states)
     entering, seg_states = lax.optimization_barrier((entering, seg_states))
 
     tp_count = lax.axis_size("tp")

time: 128 us -> 127 us (level)
  starting transfers between devices: 45.5 us -> 43.3 us
  waiting for transfers between devices: 29.4 us -> 31.3 us
    another operation x4 -> x0, local copies, waits for them, and re-layouts: 2.36 us -> none  [own_rows(): rows = jnp.tile(values.reshape(half, LANES), (2, 1))]
    all_to_all x4, starting transfers between devices: 39.8 us -> 37.6 us  [exchange(): lax.all_to_all(blocks, axis, split_axis=0, concat_axis=0, tiled=True, axi...]
    all_to_all x4, waiting for transfers between devices: 29.4 us -> 31.3 us  [exchange(): lax.all_to_all(blocks, axis, split_axis=0, concat_axis=0, tiled=True, axi...]
    dynamic_slice x1 -> x2, local copies, waits for them, and re-layouts: 0.01 us -> 1.59 us  [own_rows(): return lax.dynamic_slice(values, corner, taken).reshape(state_rows, LANES)]
    pallas_call x1 -> x2, Pallas kernels: 6.38 us -> 7.11 us  [local_sums(): pl.pallas_call(functools.partial(local_kernel, span, len(seg)), in_specs=...]
  transfers between devices with their start and end apart: 6 -> 6, of which waited for: 4 -> 4; matrix products, arithmetic and copies ran while one was open for 2% -> 1% of each run, Pallas kernels for 14% -> 15%
where the time goes in v5:
time: 127 us
  starting transfers between devices  43.3 us (34%)
  Pallas kernels  32.5 us (26%)
  waiting for transfers between devices  31.3 us (25%)
  blocking collectives  16.3 us (13%)
  local copies, waits for them, and re-layouts  2.39 us (2%)
    all_to_all x4, starting transfers between devices, exchange(): lax.all_to_all(blocks, axis, split_axis=0, concat_axis=0, tiled=True, axi...  37.6 us
    all_to_all x4, waiting for transfers between devices, exchange(): lax.all_to_all(blocks, axis, split_axis=0, concat_axis=0, tiled=True, axi...  31.3 us
    all_to_all x1, blocking collectives, exchange(): lax.all_to_all(blocks, axis, split_axis=0, concat_axis=0, tiled=True, axi...  16.3 us
    pallas_call x2, Pallas kernels, local_sums(): pl.pallas_call(functools.partial(local_kernel, span, len(seg)), in_specs=...  7.11 us
    pallas_call x1, Pallas kernels, per_device(): pl.pallas_call(functools.partial(grad_kernel, share), in_specs=[at_hbm] *...  6.81 us
    ppermute x2, starting transfers between devices, passed_along(): return lax.ppermute(shard, 'ctx', pairs)  5.65 us
    pallas_call x1, Pallas kernels, per_device(): pl.pallas_call(mix_kernel, in_specs=[at_vmem] * 5, out_specs=[at_vmem] *...  4.88 us
    pallas_call x1, Pallas kernels, per_device(): pl.pallas_call(stage_kernel, in_specs=[at_hbm] * 2 + [at_vmem], out_specs...  4.74 us
  transfers between devices with their start and end apart: 6, of which 4 were waited for; matrix products, arithmetic and copies ran while one was open for 1% of the time, Pallas kernels for 15%

profile of v5, /device:TPU:1, one launch (start us, length us, event | category | flops | bytes accessed | tf_op | source)
XLA Modules:
  0.0 126.5 jit_solution(16975771971334494639)
XLA Ops:
  0.6 0.8 slice.3
  1.4 4.4 %collective-permute-start = (bf16[3,8,1024]{2,1,0:T(8,128)(2,1)S(1)}, bf16[3,8,1024]{2,1,0:T(8,128)(2,1)S(1)}, u32[]{:S(2)}, u32[]{:S(2)}) collective-permute-start(bf16[3,8,1024]{2,1,0:T(8,128)(2,1)S(1)} %slice.3), channel_id=1, source_target_pairs={{0,8},{8,16},{16,24},{24,32},{32,40},{40,48},{48,56},{56,64},{64,7... | collective-permute-start | bytes 147464 | tf_op jit(solution)/shard_map/ppermute | solution.py:501
  5.8 0.8 dynamic_slice.7
  6.6 0.8 dynamic_slice.6
  7.4 2.3 %load.1 = (f32[8,3,256,128]{3,2,1,0:T(8,128)S(1)}, f32[8,256,128]{2,1,0:T(8,128)S(1)}, f32[3,7,1024]{2,1,0:T(8,128)S(1)}, f32[16,1024]{1,0:T(8,128)S(1)}, f32[16,1024]{1,0:T(8,128)S(1)}) custom-call(bf16[3,256,1024]{2,1,0:T(8,128)(2,1)} %x_ref.3, bf16[256,1024]{1,0:T(8,128)(2,1)} %cot_ref.1, f32[3,7,1024]{2,1,0:T(8,128)} %filt_in.3, f32[16,1024]{1,0:T(8,128)} %rate_ref.1, ...), custom_call_target="tpu_custom_call" | custom-call | flops 524288000 | bytes 2097152 | tf_op jit(solution)/shard_map/load/pallas_call | solution.py:550
  9.8 0.0 collective-permute-done.prev_ref
  9.8 4.9 %mix.1 = (f32[8,256,128]{2,1,0:T(8,128)S(1)}, f32[8,256,128]{2,1,0:T(8,128)S(1)}, f32[32,8,128]{2,1,0:T(8,128)}) custom-call(f32[8,3,256,128]{3,2,1,0:T(8,128)S(1)} %get-tuple-element.40.held, bf16[3,8,1024]{2,1,0:T(8,128)(2,1)S(1)} %collective-permute-done.prev_ref, f32[8,256,128]{2,1,0:T(8,128)S(1)} %get-tuple-element.42.cot_ref.cot, ...), custom_call_target="tpu_custom_call" | custom-call | flops 28835840 | bytes 6291456 | tf_op jit(solution)/shard_map/mix/pallas_call | solution.py:582
  14.7 17.6 %all-to-all-start = ((f32[64,4,128]{2,1,0:T(4,128)}), f32[64,4,128]{2,1,0:T(4,128)S(1)}, u32[]{:S(2)}, u32[]{:S(2)}) async-start(f32[64,4,128]{2,1,0:T(4,128)} %bitcast.8), calls=%async_computation | async-start | bytes 262144 | tf_op jit(solution)/shard_map/all_to_all | solution.py:505
  32.2 1.4 %local.2 = (f32[8,256,128]{2,1,0:T(8,128)S(1)}, f32[8,256,128]{2,1,0:T(8,128)S(1)}, f32[8,2,16,8,128]{4,3,2,1,0:T(8,128)}) custom-call(f32[8,256,128]{2,1,0:T(8,128)S(1)} %get-tuple-element.48.gated, f32[8,256,128]{2,1,0:T(8,128)S(1)} %get-tuple-element.49.gradm, ...), custom_call_target="tpu_custom_call", output_to_operand_aliasing={{0}: (0, {}), {1}: (1, {})} | custom-call | flops 4194304 | bytes 4718592 | tf_op jit(solution)/shard_map/local/pallas_call | solution.py:619
  33.7 4.7 %stage.1 = (f32[8,3,304,128]{3,2,1,0:T(8,128)}, f32[8,2,256,128]{3,2,1,0:T(8,128)}) custom-call(bf16[3,256,1024]{2,1,0:T(8,128)(2,1)} %x_ref.3, f32[3,7,1024]{2,1,0:T(8,128)} %filt_in.3, bf16[3,8,1024]{2,1,0:T(8,128)(2,1)S(1)} %collective-permute-done.prev_ref), custom_call_target="tpu_custom_call" | custom-call | flops 524288000 | bytes 4718592 | tf_op jit(solution)/shard_map/stage/pallas_call | solution.py:598
  38.4 7.8 %all-to-all-done.arrived_ref = f32[64,4,128]{2,1,0:T(4,128)S(1)} async-done(((f32[64,4,128]{2,1,0:T(4,128)}), f32[64,4,128]{2,1,0:T(4,128)S(1)}, u32[]{:S(2)}, u32[]{:S(2)}) %all-to-all-start) | async-done | bytes 131104 | tf_op jit(solution)/shard_map/all_to_all | solution.py:505
  46.2 0.8 chain.1
  47.0 7.1 %all-to-all-start.1 = ((f32[64,4,128]{2,1,0:T(4,128)}), f32[64,4,128]{2,1,0:T(4,128)S(1)}, u32[]{:S(2)}, u32[]{:S(2)}) async-start(f32[64,4,128]{2,1,0:T(4,128)} %chain.1), calls=%async_computation.1 | async-start | bytes 262144 | tf_op jit(solution)/shard_map/all_to_all | solution.py:505
  54.1 5.7 %local.3 = (f32[8,256,128]{2,1,0:T(8,128)S(1)}, f32[8,256,128]{2,1,0:T(8,128)S(1)}, f32[8,2,16,8,128]{4,3,2,1,0:T(8,128)}) custom-call(f32[8,256,128]{2,1,0:T(8,128)S(1)} %get-tuple-element.57.gated, f32[8,256,128]{2,1,0:T(8,128)S(1)} %get-tuple-element.58.gradm, ...), custom_call_target="tpu_custom_call", output_to_operand_aliasing={{0}: (0, {}), {1}: (1, {}), {2}: (4, {})} | custom-call | flops 29360128 | bytes 4718592 | tf_op jit(solution)/shard_map/local/pallas_call | solution.py:619
  59.7 8.3 %all-to-all-done.1 = f32[64,4,128]{2,1,0:T(4,128)S(1)} async-done(((f32[64,4,128]{2,1,0:T(4,128)}), f32[64,4,128]{2,1,0:T(4,128)S(1)}, u32[]{:S(2)}, u32[]{:S(2)}) %all-to-all-start.1) | async-done | bytes 131104 | tf_op jit(solution)/shard_map/all_to_all | solution.py:505
  68.0 6.8 %grad.1 = (f32[8,256,128]{2,1,0:T(8,128)S(1)}, f32[8,256,128]{2,1,0:T(8,128)S(1)}, f32[8,256,128]{2,1,0:T(8,128)S(1)}, bf16[3,8,1024]{2,1,0:T(8,128)(2,1)S(1)}, f32[32,8,128]{2,1,0:T(8,128)}) custom-call(f32[8,3,304,128]{3,2,1,0:T(8,128)} %get-tuple-element.52.held_ref, ...), custom_call_target="tpu_custom_call", output_to_operand_aliasing={{0}: (3, {}), {1}: (4, {}), {2}: (5, {})} | custom-call | flops 28835840 | bytes 7864320 | tf_op jit(solution)/shard_map/grad/pallas_call | solution.py:668
  74.8 9.5 %all-to-all-start.2 = ((f32[32,8,128]{2,1,0:T(8,128)}), f32[32,8,128]{2,1,0:T(8,128)S(1)}, u32[]{:S(2)}, u32[]{:S(2)}) async-start(f32[32,8,128]{2,1,0:T(8,128)} %get-tuple-element.65), calls=%async_computation.2 | async-start | bytes 262144 | tf_op jit(solution)/shard_map/all_to_all | solution.py:505
  84.3 1.3 %collective-permute-start.1 = (bf16[3,8,1024]{2,1,0:T(8,128)(2,1)S(1)}, bf16[3,8,1024]{2,1,0:T(8,128)(2,1)S(1)}, u32[]{:S(2)}, u32[]{:S(2)}) collective-permute-start(bf16[3,8,1024]{2,1,0:T(8,128)(2,1)S(1)} %get-tuple-element.66), channel_id=1, source_target_pairs={{8,0},{16,8},{24,16},{32,24},{40,32},{48,40},{56,48},{64,56},{72,6... | collective-permute-start | bytes 147464 | tf_op jit(solution)/shard_map/ppermute | solution.py:501
  85.6 6.3 %all-to-all-done.2.part_ref = f32[32,8,128]{2,1,0:T(8,128)S(1)} async-done(((f32[32,8,128]{2,1,0:T(8,128)}), f32[32,8,128]{2,1,0:T(8,128)S(1)}, u32[]{:S(2)}, u32[]{:S(2)}) %all-to-all-start.2) | async-done | bytes 131104 | tf_op jit(solution)/shard_map/all_to_all | solution.py:505
  91.9 0.7 line.1
  92.6 0.0 collective-permute-done.1.next_ref
  92.6 3.5 %all-to-all-start.3 = ((bf16[16,48,128]{2,1,0:T(8,128)(2,1)}), bf16[16,48,128]{2,1,0:T(8,128)(2,1)S(1)}, u32[]{:S(2)}, u32[]{:S(2)}) async-start(bf16[16,48,128]{2,1,0:T(8,128)(2,1)} %line.1), calls=%async_computation.3 | async-start | bytes 393216 | tf_op jit(solution)/shard_map/all_to_all | solution.py:505
  96.2 4.2 %back.1 = bf16[3,256,1024]{2,1,0:T(8,128)(2,1)} custom-call(f32[8,256,128]{2,1,0:T(8,128)S(1)} %get-tuple-element.68.query_mix, f32[8,256,128]{2,1,0:T(8,128)S(1)} %get-tuple-element.69.key_mix, f32[8,256,128]{2,1,0:T(8,128)S(1)} %get-tuple-element.70.value_mix, bf16[3,8,1024]{2,1,0:T(8,128)(2,1)S(1)} %collective-permute-done.1.next_ref, f32[3,7,1024]{2,1,0:T(8,128)} %filt_in.3), custom_call_target="tpu_custom_call" | custom-call | flops 12582912 | bytes 3145728 | tf_op jit(solution)/shard_map/back/pallas_call | solution.py:706
  100.4 8.9 %all-to-all-done.3.part_ref = bf16[16,48,128]{2,1,0:T(8,128)(2,1)S(1)} async-done(((bf16[16,48,128]{2,1,0:T(8,128)(2,1)}), bf16[16,48,128]{2,1,0:T(8,128)(2,1)S(1)}, u32[]{:S(2)}, u32[]{:S(2)}) %all-to-all-start.3) | async-done | bytes 196640 | tf_op jit(solution)/shard_map/all_to_all | solution.py:505
  109.4 0.2 plane.1
  109.5 16.3 %all_to_all.25.sums_ref = f32[32,8,128]{2,1,0:T(8,128)S(1)} all-to-all(f32[32,8,128]{2,1,0:T(8,128)S(1)} %plane.1), channel_id=1, replica_groups={{0,1,2,3,4,5,6,7,128,129,130,131,132,133,134,135,256,257,258,259,260,26..., dimensions={0} | all-to-all | bytes 262144 | tf_op jit(solution)/shard_map/all_to_all | solution.py:505
  125.8 0.7 scale.1
Async XLA Ops:
  1.4 8.3 %collective-permute-start = (bf16[3,8,1024]{2,1,0:T(8,128)(2,1)S(1)}, bf16[3,8,1024]{2,1,0:T(8,128)(2,1)S(1)}, u32[]{:S(2)}, u32[]{:S(2)}) collective-permute-start(bf16[3,8,1024]{2,1,0:T(8,128)(2,1)S(1)} %slice.3), channel_id=1, source_target_pairs={{0,8},{8,16},{16,24},{24,32},{32,40},{40,48},{48,56},{56,64},{64,7... | collective-permute-start | bytes 147464 | tf_op jit(solution)/shard_map/ppermute | solution.py:501
  14.7 31.5 %all-to-all-start = ((f32[64,4,128]{2,1,0:T(4,128)}), f32[64,4,128]{2,1,0:T(4,128)S(1)}, u32[]{:S(2)}, u32[]{:S(2)}) async-start(f32[64,4,128]{2,1,0:T(4,128)} %bitcast.8), calls=%async_computation | async-start | bytes 262144 | tf_op jit(solution)/shard_map/all_to_all | solution.py:505
  47.0 21.0 %all-to-all-start.1 = ((f32[64,4,128]{2,1,0:T(4,128)}), f32[64,4,128]{2,1,0:T(4,128)S(1)}, u32[]{:S(2)}, u32[]{:S(2)}) async-start(f32[64,4,128]{2,1,0:T(4,128)} %chain.1), calls=%async_computation.1 | async-start | bytes 262144 | tf_op jit(solution)/shard_map/all_to_all | solution.py:505
  74.8 17.1 %all-to-all-start.2 = ((f32[32,8,128]{2,1,0:T(8,128)}), f32[32,8,128]{2,1,0:T(8,128)S(1)}, u32[]{:S(2)}, u32[]{:S(2)}) async-start(f32[32,8,128]{2,1,0:T(8,128)} %get-tuple-element.65), calls=%async_computation.2 | async-start | bytes 262144 | tf_op jit(solution)/shard_map/all_to_all | solution.py:505
  84.3 8.3 %collective-permute-start.1 = (bf16[3,8,1024]{2,1,0:T(8,128)(2,1)S(1)}, bf16[3,8,1024]{2,1,0:T(8,128)(2,1)S(1)}, u32[]{:S(2)}, u32[]{:S(2)}) collective-permute-start(bf16[3,8,1024]{2,1,0:T(8,128)(2,1)S(1)} %get-tuple-element.66), channel_id=1, source_target_pairs={{8,0},{16,8},{24,16},{32,24},{40,32},{48,40},{56,48},{64,56},{72,6... | collective-permute-start | bytes 147464 | tf_op jit(solution)/shard_map/ppermute | solution.py:501
  92.6 16.7 %all-to-all-start.3 = ((bf16[16,48,128]{2,1,0:T(8,128)(2,1)}), bf16[16,48,128]{2,1,0:T(8,128)(2,1)S(1)}, u32[]{:S(2)}, u32[]{:S(2)}) async-start(bf16[16,48,128]{2,1,0:T(8,128)(2,1)} %line.1), calls=%async_computation.3 | async-start | bytes 393216 | tf_op jit(solution)/shard_map/all_to_all | solution.py:505

commit v6 on v5

--- a/solution.py
+++ b/solution.py
@@ -117,6 +117,22 @@
         for group in range(channels // LANES):
             slab = rows[:, group * LANES : (group + 1) * LANES]
             targets[part](group)[...] = slab
+
+
+def own_rows(values, first, count):
+    modes, channels = values.shape
+    groups = channels // LANES
+    wide = min(count, groups)
+    at_mode = lax.broadcasted_iota(jnp.int32, (modes, wide * LANES), 0)
+    start = lax.rem(first, modes * groups)
+    mode, group = lax.div(start, groups), lax.rem(start, groups)
+    lanes = pl.ds(pl.multiple_of(group * LANES, LANES), wide * LANES)
+    rows = []
+    for index in range(count // wide):
+        picked = jnp.where(at_mode == mode + index, values[:, lanes], 0.0)
+        row = jnp.sum(picked, axis=0, keepdims=True)
+        rows += [row[:, at * LANES : (at + 1) * LANES] for at in range(wide)]
+    return jnp.concatenate(rows, axis=0)
 
 
 def load_kernel(
@@ -254,9 +270,10 @@
 
 
 def chain_kernel(row_count, half, first_ref, arrived_ref, rate_ref, residue_ref, out_ref):
-    blocks = arrived_ref.shape[0]
-    step_decay = jnp.exp(-rate_ref[...] * row_count)
-    weight = residue_ref[...] * jnp.exp(-rate_ref[...])
+    blocks, state_rows, _ = arrived_ref.shape
+    rate = own_rows(rate_ref, first_ref[0], state_rows)
+    step_decay = jnp.exp(-rate * row_count)
+    weight = own_rows(residue_ref, first_ref[0], state_rows) * jnp.exp(-rate)
 
     def run(order):
         def body(index, carry):
@@ -264,7 +281,7 @@
             out_ref[pl.ds(block, 1)] = (carry * weight)[None]
             return carry * step_decay + arrived_ref[pl.ds(block, 1)][0]
 
-        lax.fori_loop(0, blocks, body, jnp.zeros(rate_ref.shape, F32), unroll=32)
+        lax.fori_loop(0, blocks, body, jnp.zeros(rate.shape, F32), unroll=32)
 
     @pl.when(first_ref[0] < half)
     def _():
@@ -406,11 +423,8 @@
 
 
 def back_kernel(
-    query_mix, key_mix, value_mix, next_ref, filt_in, out_ref,
-    late, made, wide, filt_ref, sems, filt_sem,
+    query_mix, key_mix, value_mix, next_ref, filt_ref, out_ref, late, made, wide, sems
 ):
-    filt_copy = pltpu.make_async_copy(filt_in, filt_ref, filt_sem.at[0])
-    filt_copy.start()
     mix = (query_mix, key_mix, value_mix)
     taps = filt_ref.shape[1]
     row_count, channels = made.shape
@@ -418,7 +432,6 @@
     steps = row_count // SUBS
     perm = step_major(row_count, True)
     late[...] = next_ref[...].astype(F32)
-    filt_copy.wait()
     copies = []
     for part in range(3):
 
@@ -546,6 +559,10 @@
     row_dims = (groups, row_count, LANES)
     kv_dims = (groups, 2, row_count, LANES)
     seg_dims = (groups, 2, modes, SUBS, LANES)
+
+    state_rows = 2 * modes * groups // blocks
+    first = lax.axis_index("ctx") * state_rows
+    half = modes * groups
 
     held, cot_held, filt, rate, weight = pl.pallas_call(
         load_kernel,
@@ -564,21 +581,7 @@
         name="load",
     )(*from_far(inputs, cotangent, short_filter, decay_rate, residue))
     prev = passed_along(inputs[:, row_count - HALO :, :], 1)
-    state_rows = 2 * modes * groups // blocks
-    first = lax.axis_index("ctx") * state_rows
-    half = modes * groups
-
-    def own_rows(values):
-        start = lax.rem(first, half)
-        if state_rows < groups:
-            corner, taken = (start // groups, start % groups * LANES), (1, state_rows * LANES)
-        else:
-            corner, taken = (start // groups, 0), (state_rows // groups, channels)
-        return lax.dynamic_slice(values, corner, taken).reshape(state_rows, LANES)
-
-    prev, held, cot_held, own_rate, own_residue = lax.optimization_barrier(
-        (prev, held, cot_held, own_rows(decay_rate), own_rows(residue))
-    )
+    prev, held, cot_held = lax.optimization_barrier((prev, held, cot_held))
     gated, gradm, states = pl.pallas_call(
         mix_kernel,
         in_specs=[at_vmem] * 5,
@@ -649,7 +652,7 @@
         compiler_params=small,
         cost_estimate=cost(blocks * state_rows * LANES * 2, blocks * state_rows * LANES * 8),
         name="chain",
-    )(first[None], arrived, own_rate, own_residue)
+    )(first[None], arrived, *from_near(rate, weight))
     entering = exchange(entering, "ctx").reshape(2 * modes, groups, LANES)
 
     ahead, behind, seg_states = local_sums((early_groups, groups), ahead, behind, seg_states)
@@ -701,25 +704,22 @@
         compiler_params=small,
         name="line",
     )(gathered)
-    own_sum, late = lax.optimization_barrier((own_sum, late))
     all_sums = exchange(own_sum, "ctx", line_members)
     grad_inputs = pl.pallas_call(
         back_kernel,
-        in_specs=[at_vmem] * 4 + [at_hbm],
+        in_specs=[at_vmem] * 5,
         out_specs=at_hbm,
         out_shape=far(BF16, 3, row_count, channels),
         scratch_shapes=[
             pltpu.VMEM((3, HALO, channels), F32),
             pltpu.VMEM((row_count, channels), BF16),
             pltpu.VMEM((3, row_count, channels), BF16),
-            pltpu.VMEM((3, taps, channels), F32),
             sems((3,)),
-            sems((1,)),
         ],
         compiler_params=params,
         cost_estimate=cost(work * 48, work * 12),
         name="back",
-    )(*from_near(*grad_mix), late, *from_far(short_filter))
+    )(*from_near(*grad_mix), late, *from_near(filt))
     all_sums, grad_inputs = lax.optimization_barrier((all_sums, grad_inputs))
     all_sums = pl.pallas_call(
         functools.partial(plane_kernel, share),

time: 127 us -> 125 us (0.984)
  blocking collectives: 16.3 us -> 31.4 us
  starting transfers between devices: 43.3 us -> 34.5 us
  waiting for transfers between devices: 31.3 us -> 25 us
  local copies, waits for them, and re-layouts: 2.39 us -> 0.81 us
    all_to_all x4 -> x3, waiting for transfers between devices: 31.3 us -> 16.1 us  [exchange(): lax.all_to_all(blocks, axis, split_axis=0, concat_axis=0, tiled=True, axi...]
    all_to_all x1 -> x2, blocking collectives: 16.3 us -> 31.4 us  [exchange(): lax.all_to_all(blocks, axis, split_axis=0, concat_axis=0, tiled=True, axi...]
    ppermute x2, waiting for transfers between devices: 0.01 us -> 8.88 us  [passed_along(): return lax.ppermute(shard, 'ctx', pairs)]
    all_to_all x4 -> x3, starting transfers between devices: 37.6 us -> 28.9 us  [exchange(): lax.all_to_all(blocks, axis, split_axis=0, concat_axis=0, tiled=True, axi...]
    dynamic_slice x2 -> x0, local copies, waits for them, and re-layouts: 1.59 us -> none  [own_rows(): return lax.dynamic_slice(values, corner, taken).reshape(state_rows, LANES)]
  transfers between devices with their start and end apart: 6 -> 5, of which waited for: 4 -> 3; matrix products, arithmetic and copies ran while one was open for 1% -> 0% of each run, Pallas kernels for 15% -> 14%
where the time goes in v6:
time: 125 us; the launch traced here: 124 us
  starting transfers between devices  34.5 us (28%)
  Pallas kernels  31.7 us (25%)
  blocking collectives  31.4 us (25%)
  waiting for transfers between devices  25 us (20%)
    all_to_all x2, blocking collectives, exchange(): lax.all_to_all(blocks, axis, split_axis=0, concat_axis=0, tiled=True, axi...  31.4 us
    all_to_all x3, starting transfers between devices, exchange(): lax.all_to_all(blocks, axis, split_axis=0, concat_axis=0, tiled=True, axi...  28.9 us
    all_to_all x3, waiting for transfers between devices, exchange(): lax.all_to_all(blocks, axis, split_axis=0, concat_axis=0, tiled=True, axi...  16.1 us
    ppermute x2, waiting for transfers between devices, passed_along(): return lax.ppermute(shard, 'ctx', pairs)  8.88 us
    pallas_call x2, Pallas kernels, local_sums(): pl.pallas_call(functools.partial(local_kernel, span, len(seg)), in_specs=...  7.11 us
    pallas_call x1, Pallas kernels, per_device(): pl.pallas_call(functools.partial(grad_kernel, share), in_specs=[at_hbm] *...  6.82 us
    ppermute x2, starting transfers between devices, passed_along(): return lax.ppermute(shard, 'ctx', pairs)  5.65 us
    pallas_call x1, Pallas kernels, per_device(): pl.pallas_call(mix_kernel, in_specs=[at_vmem] * 5, out_specs=[at_vmem] *...  4.89 us
  transfers between devices with their start and end apart: 5, of which 3 were waited for; matrix products, arithmetic and copies ran while one was open for 0% of the time, Pallas kernels for 14%

profile of v6, /device:TPU:1, one launch (start us, length us, event | category | flops | bytes accessed | tf_op | source)
XLA Modules:
  0.0 124.1 jit_solution(7796321906665901625)
XLA Ops:
  0.6 0.8 slice.3
  1.4 4.4 %collective-permute-start = (bf16[3,8,1024]{2,1,0:T(8,128)(2,1)S(1)}, bf16[3,8,1024]{2,1,0:T(8,128)(2,1)S(1)}, u32[]{:S(2)}, u32[]{:S(2)}) collective-permute-start(bf16[3,8,1024]{2,1,0:T(8,128)(2,1)S(1)} %slice.3), channel_id=1, source_target_pairs={{0,8},{8,16},{16,24},{24,32},{32,40},{40,48},{48,56},{56,64},{64,7... | collective-permute-start | bytes 147464 | tf_op jit(solution)/shard_map/ppermute | solution.py:514
  5.8 2.3 %load.1 = (f32[8,3,256,128]{3,2,1,0:T(8,128)S(1)}, f32[8,256,128]{2,1,0:T(8,128)S(1)}, f32[3,7,1024]{2,1,0:T(8,128)S(1)}, f32[16,1024]{1,0:T(8,128)S(1)}, f32[16,1024]{1,0:T(8,128)S(1)}) custom-call(bf16[3,256,1024]{2,1,0:T(8,128)(2,1)} %x_ref.3, bf16[256,1024]{1,0:T(8,128)(2,1)} %cot_ref.1, f32[3,7,1024]{2,1,0:T(8,128)} %filt_in.1, f32[16,1024]{1,0:T(8,128)} %rate_ref.1, ...), custom_call_target="tpu_custom_call" | custom-call | flops 524288000 | bytes 2097152 | tf_op jit(solution)/shard_map/load/pallas_call | solution.py:567
  8.1 0.0 collective-permute-done.prev_ref
  8.2 4.9 %mix.1 = (f32[8,256,128]{2,1,0:T(8,128)S(1)}, f32[8,256,128]{2,1,0:T(8,128)S(1)}, f32[32,8,128]{2,1,0:T(8,128)}) custom-call(f32[8,3,256,128]{3,2,1,0:T(8,128)S(1)} %get-tuple-element.36.held, bf16[3,8,1024]{2,1,0:T(8,128)(2,1)S(1)} %collective-permute-done.prev_ref, f32[8,256,128]{2,1,0:T(8,128)S(1)} %get-tuple-element.38.cot_ref.cot, ...), custom_call_target="tpu_custom_call" | custom-call | flops 28835840 | bytes 6291456 | tf_op jit(solution)/shard_map/mix/pallas_call | solution.py:585
  13.0 18.6 %all-to-all-start = ((f32[64,4,128]{2,1,0:T(4,128)}), f32[64,4,128]{2,1,0:T(4,128)S(1)}, u32[]{:S(2)}, u32[]{:S(2)}) async-start(f32[64,4,128]{2,1,0:T(4,128)} %bitcast.4), calls=%async_computation | async-start | bytes 262144 | tf_op jit(solution)/shard_map/all_to_all | solution.py:518
  31.6 1.4 %local.2 = (f32[8,256,128]{2,1,0:T(8,128)S(1)}, f32[8,256,128]{2,1,0:T(8,128)S(1)}, f32[8,2,16,8,128]{4,3,2,1,0:T(8,128)}) custom-call(f32[8,256,128]{2,1,0:T(8,128)S(1)} %get-tuple-element.44.gated, f32[8,256,128]{2,1,0:T(8,128)S(1)} %get-tuple-element.45.gradm, ...), custom_call_target="tpu_custom_call", output_to_operand_aliasing={{0}: (0, {}), {1}: (1, {})} | custom-call | flops 4194304 | bytes 4718592 | tf_op jit(solution)/shard_map/local/pallas_call | solution.py:622
  33.1 4.7 %stage.1 = (f32[8,3,304,128]{3,2,1,0:T(8,128)}, f32[8,2,256,128]{3,2,1,0:T(8,128)}) custom-call(bf16[3,256,1024]{2,1,0:T(8,128)(2,1)} %x_ref.3, f32[3,7,1024]{2,1,0:T(8,128)} %filt_in.1, bf16[3,8,1024]{2,1,0:T(8,128)(2,1)S(1)} %collective-permute-done.prev_ref), custom_call_target="tpu_custom_call" | custom-call | flops 524288000 | bytes 4718592 | tf_op jit(solution)/shard_map/stage/pallas_call | solution.py:601
  37.8 7.8 %all-to-all-done.arrived_ref = f32[64,4,128]{2,1,0:T(4,128)S(1)} async-done(((f32[64,4,128]{2,1,0:T(4,128)}), f32[64,4,128]{2,1,0:T(4,128)S(1)}, u32[]{:S(2)}, u32[]{:S(2)}) %all-to-all-start) | async-done | bytes 131104 | tf_op jit(solution)/shard_map/all_to_all | solution.py:518
  45.7 0.8 chain.1
  46.5 6.7 %all-to-all-start.1 = ((f32[64,4,128]{2,1,0:T(4,128)}), f32[64,4,128]{2,1,0:T(4,128)S(1)}, u32[]{:S(2)}, u32[]{:S(2)}) async-start(f32[64,4,128]{2,1,0:T(4,128)} %chain.1), calls=%async_computation.1 | async-start | bytes 262144 | tf_op jit(solution)/shard_map/all_to_all | solution.py:518
  53.2 5.7 %local.3 = (f32[8,256,128]{2,1,0:T(8,128)S(1)}, f32[8,256,128]{2,1,0:T(8,128)S(1)}, f32[8,2,16,8,128]{4,3,2,1,0:T(8,128)}) custom-call(f32[8,256,128]{2,1,0:T(8,128)S(1)} %get-tuple-element.51.gated, f32[8,256,128]{2,1,0:T(8,128)S(1)} %get-tuple-element.52.gradm, ...), custom_call_target="tpu_custom_call", output_to_operand_aliasing={{0}: (0, {}), {1}: (1, {}), {2}: (4, {})} | custom-call | flops 29360128 | bytes 4718592 | tf_op jit(solution)/shard_map/local/pallas_call | solution.py:622
  58.9 8.3 %all-to-all-done.1 = f32[64,4,128]{2,1,0:T(4,128)S(1)} async-done(((f32[64,4,128]{2,1,0:T(4,128)}), f32[64,4,128]{2,1,0:T(4,128)S(1)}, u32[]{:S(2)}, u32[]{:S(2)}) %all-to-all-start.1) | async-done | bytes 131104 | tf_op jit(solution)/shard_map/all_to_all | solution.py:518
  67.2 6.8 %grad.1 = (f32[8,256,128]{2,1,0:T(8,128)S(1)}, f32[8,256,128]{2,1,0:T(8,128)S(1)}, f32[8,256,128]{2,1,0:T(8,128)S(1)}, bf16[3,8,1024]{2,1,0:T(8,128)(2,1)S(1)}, f32[32,8,128]{2,1,0:T(8,128)}) custom-call(f32[8,3,304,128]{3,2,1,0:T(8,128)} %get-tuple-element.48.held_ref, ...), custom_call_target="tpu_custom_call", output_to_operand_aliasing={{0}: (3, {}), {1}: (4, {}), {2}: (5, {})} | custom-call | flops 28835840 | bytes 7864320 | tf_op jit(solution)/shard_map/grad/pallas_call | solution.py:671
  74.0 17.5 %all_to_all.25.part_ref = f32[32,8,128]{2,1,0:T(8,128)S(1)} all-to-all(f32[32,8,128]{2,1,0:T(8,128)} %get-tuple-element.59), channel_id=1, replica_groups={{0,1,2,3,4,5,6,7,128,129,130,131,132,133,134,135,256,257,258,259,260,26..., dimensions={0} | all-to-all | bytes 262144 | tf_op jit(solution)/shard_map/all_to_all | solution.py:518
  91.5 0.7 line.1
  92.2 3.5 %all-to-all-start.3 = ((bf16[16,48,128]{2,1,0:T(8,128)(2,1)}), bf16[16,48,128]{2,1,0:T(8,128)(2,1)S(1)}, u32[]{:S(2)}, u32[]{:S(2)}) async-start(bf16[16,48,128]{2,1,0:T(8,128)(2,1)} %line.1), calls=%async_computation.3 | async-start | bytes 393216 | tf_op jit(solution)/shard_map/all_to_all | solution.py:518
  95.7 1.3 %collective-permute-start.1 = (bf16[3,8,1024]{2,1,0:T(8,128)(2,1)S(1)}, bf16[3,8,1024]{2,1,0:T(8,128)(2,1)S(1)}, u32[]{:S(2)}, u32[]{:S(2)}) collective-permute-start(bf16[3,8,1024]{2,1,0:T(8,128)(2,1)S(1)} %get-tuple-element.63), channel_id=1, source_target_pairs={{8,0},{16,8},{24,16},{32,24},{40,32},{48,40},{56,48},{64,56},{72,6... | collective-permute-start | bytes 147464 | tf_op jit(solution)/shard_map/ppermute | solution.py:514
  97.0 8.9 %collective-permute-done.1.next_ref = bf16[3,8,1024]{2,1,0:T(8,128)(2,1)S(1)} collective-permute-done((bf16[3,8,1024]{2,1,0:T(8,128)(2,1)S(1)}, bf16[3,8,1024]{2,1,0:T(8,128)(2,1)S(1)}, u32[]{:S(2)}, u32[]{:S(2)}) %collective-permute-start.1) | collective-permute-done | bytes 49184 | tf_op jit(solution)/shard_map/ppermute | solution.py:514
  105.9 3.4 %back.1 = bf16[3,256,1024]{2,1,0:T(8,128)(2,1)} custom-call(f32[8,256,128]{2,1,0:T(8,128)S(1)} %get-tuple-element.60.query_mix, f32[8,256,128]{2,1,0:T(8,128)S(1)} %get-tuple-element.61.key_mix, f32[8,256,128]{2,1,0:T(8,128)S(1)} %get-tuple-element.62.value_mix, bf16[3,8,1024]{2,1,0:T(8,128)(2,1)S(1)} %collective-permute-done.1.next_ref, ...), custom_call_target="tpu_custom_call" | custom-call | flops 12582912 | bytes 3145728 | tf_op jit(solution)/shard_map/back/pallas_call | solution.py:708
  109.3 0.0 all-to-all-done.3.part_ref
  109.3 0.2 plane.1
  109.5 13.9 %all_to_all.26.sums_ref = f32[32,8,128]{2,1,0:T(8,128)S(1)} all-to-all(f32[32,8,128]{2,1,0:T(8,128)S(1)} %plane.1), channel_id=1, replica_groups={{0,1,2,3,4,5,6,7,128,129,130,131,132,133,134,135,256,257,258,259,260,26..., dimensions={0} | all-to-all | bytes 262144 | tf_op jit(solution)/shard_map/all_to_all | solution.py:518
  123.4 0.7 scale.1
Async XLA Ops:
  1.4 6.7 %collective-permute-start = (bf16[3,8,1024]{2,1,0:T(8,128)(2,1)S(1)}, bf16[3,8,1024]{2,1,0:T(8,128)(2,1)S(1)}, u32[]{:S(2)}, u32[]{:S(2)}) collective-permute-start(bf16[3,8,1024]{2,1,0:T(8,128)(2,1)S(1)} %slice.3), channel_id=1, source_target_pairs={{0,8},{8,16},{16,24},{24,32},{32,40},{40,48},{48,56},{56,64},{64,7... | collective-permute-start | bytes 147464 | tf_op jit(solution)/shard_map/ppermute | solution.py:514
  13.0 32.6 %all-to-all-start = ((f32[64,4,128]{2,1,0:T(4,128)}), f32[64,4,128]{2,1,0:T(4,128)S(1)}, u32[]{:S(2)}, u32[]{:S(2)}) async-start(f32[64,4,128]{2,1,0:T(4,128)} %bitcast.4), calls=%async_computation | async-start | bytes 262144 | tf_op jit(solution)/shard_map/all_to_all | solution.py:518
  46.5 20.7 %all-to-all-start.1 = ((f32[64,4,128]{2,1,0:T(4,128)}), f32[64,4,128]{2,1,0:T(4,128)S(1)}, u32[]{:S(2)}, u32[]{:S(2)}) async-start(f32[64,4,128]{2,1,0:T(4,128)} %chain.1), calls=%async_computation.1 | async-start | bytes 262144 | tf_op jit(solution)/shard_map/all_to_all | solution.py:518
  92.2 17.1 %all-to-all-start.3 = ((bf16[16,48,128]{2,1,0:T(8,128)(2,1)}), bf16[16,48,128]{2,1,0:T(8,128)(2,1)S(1)}, u32[]{:S(2)}, u32[]{:S(2)}) async-start(bf16[16,48,128]{2,1,0:T(8,128)(2,1)} %line.1), calls=%async_computation.3 | async-start | bytes 393216 | tf_op jit(solution)/shard_map/all_to_all | solution.py:518
  95.7 10.2 %collective-permute-start.1 = (bf16[3,8,1024]{2,1,0:T(8,128)(2,1)S(1)}, bf16[3,8,1024]{2,1,0:T(8,128)(2,1)S(1)}, u32[]{:S(2)}, u32[]{:S(2)}) collective-permute-start(bf16[3,8,1024]{2,1,0:T(8,128)(2,1)S(1)} %get-tuple-element.63), channel_id=1, source_target_pairs={{8,0},{16,8},{24,16},{32,24},{40,32},{48,40},{56,48},{64,56},{72,6... | collective-permute-start | bytes 147464 | tf_op jit(solution)/shard_map/ppermute | solution.py:514

commit v7 on v6

--- a/solution.py
+++ b/solution.py
@@ -423,7 +423,7 @@
 
 
 def back_kernel(
-    query_mix, key_mix, value_mix, next_ref, filt_ref, out_ref, late, made, wide, sems
+    query_mix, key_mix, value_mix, filt_ref, out_ref, edge_ref, made, wide, sems
 ):
     mix = (query_mix, key_mix, value_mix)
     taps = filt_ref.shape[1]
@@ -431,7 +431,6 @@
     groups = channels // LANES
     steps = row_count // SUBS
     perm = step_major(row_count, True)
-    late[...] = next_ref[...].astype(F32)
     copies = []
     for part in range(3):
 
@@ -456,15 +455,40 @@
             window = [mix[part][group, step_rows(last + at), :] for at in range(CHUNK)]
             for step in range(taps - 1):
                 first = mix[part][group, step_rows(step), :]
-                row = late[part, pl.ds(step, 1), lanes]
                 window.append(
-                    jnp.where(sub_index() == SUBS - 1, spread(row), pltpu.roll(first, SUBS - 1, 0))
+                    jnp.where(sub_index() == SUBS - 1, 0.0, pltpu.roll(first, SUBS - 1, 0))
                 )
             back_rows(last, window)
+            edge = [
+                mix[part][group, pl.ds((steps - HALO + row) * SUBS + SUBS - 1, 1), :]
+                for row in range(HALO)
+            ]
+            edge_ref[part, :, lanes] = jnp.concatenate(edge, axis=0)
 
         each_group(groups, one_group)
         wide[part] = jnp.dot(perm, made[...], preferred_element_type=F32).astype(BF16)
         copies.append(pltpu.make_async_copy(wide.at[part], out_ref.at[part], sems.at[part]))
+        copies[-1].start()
+    wait_all(copies)
+
+
+def edge_kernel(out_in, edge_ref, next_ref, filt_ref, out_ref, rows, made, sems):
+    del out_in
+    taps = filt_ref.shape[1]
+    last = out_ref.shape[1] - HALO
+    copies = []
+    for part in range(3):
+        rows[part, pl.ds(0, HALO), :] = edge_ref[part]
+        rows[part, pl.ds(HALO, HALO), :] = next_ref[part].astype(F32)
+        terms = [
+            filt_ref[part, pl.ds(k, 1), :] * rows[part, pl.ds(k, HALO), :] for k in range(taps)
+        ]
+        made[part] = added(terms).astype(BF16)
+        copies.append(
+            pltpu.make_async_copy(
+                made.at[part], out_ref.at[part, pl.ds(last, HALO), :], sems.at[part]
+            )
+        )
         copies[-1].start()
     wait_all(copies)
 
@@ -700,18 +724,17 @@
         functools.partial(line_kernel, share, tp_count),
         in_specs=[at_vmem],
         out_specs=at_vmem,
-        out_shape=shaped(BF16, planes, tp_count * share, LANES),
+        out_shape=far(BF16, planes, tp_count * share, LANES),
         compiler_params=small,
         name="line",
     )(gathered)
     all_sums = exchange(own_sum, "ctx", line_members)
-    grad_inputs = pl.pallas_call(
+    grad_inputs, edge = pl.pallas_call(
         back_kernel,
-        in_specs=[at_vmem] * 5,
-        out_specs=at_hbm,
-        out_shape=far(BF16, 3, row_count, channels),
+        in_specs=[at_vmem] * 4,
+        out_specs=[at_hbm, at_vmem],
+        out_shape=[far(BF16, 3, row_count, channels), far(F32, 3, HALO, channels)],
         scratch_shapes=[
-            pltpu.VMEM((3, HALO, channels), F32),
             pltpu.VMEM((row_count, channels), BF16),
             pltpu.VMEM((3, row_count, channels), BF16),
             sems((3,)),
@@ -719,8 +742,8 @@
         compiler_params=params,
         cost_estimate=cost(work * 48, work * 12),
         name="back",
-    )(*from_near(*grad_mix), late, *from_near(filt))
-    all_sums, grad_inputs = lax.optimization_barrier((all_sums, grad_inputs))
+    )(*from_near(*grad_mix, filt))
+    all_sums, grad_inputs, late = lax.optimization_barrier((all_sums, grad_inputs, late))
     all_sums = pl.pallas_call(
         functools.partial(plane_kernel, share),
         in_specs=[at_vmem],
@@ -730,6 +753,22 @@
         name="plane",
     )(all_sums)
     all_sums = exchange(all_sums, ("ctx", "tp"), plane_members)
+    grad_inputs = pl.pallas_call(
+        edge_kernel,
+        in_specs=[at_hbm] + [at_vmem] * 3,
+        out_specs=at_hbm,
+        out_shape=far(BF16, 3, row_count, channels),
+        scratch_shapes=[
+            pltpu.VMEM((3, 2 * HALO, channels), F32),
+            pltpu.VMEM((3, HALO, channels), BF16),
+            sems((3,)),
+        ],
+        input_output_aliases={0: 0},
+        compiler_params=small,
+        cost_estimate=cost(work, work),
+        name="edge",
+    )(*from_far(grad_inputs), edge, late, *from_near(filt))
+    all_sums, grad_inputs = lax.optimization_barrier((all_sums, grad_inputs))
     clip_limit = math.sqrt(3 * channels * tp_count * taps)
     grad_short = pl.pallas_call(
         functools.partial(scale_kernel, clip_limit, share),

time: 125 us -> 126 us (level)
  blocking collectives: 31.4 us -> 17.5 us
  starting transfers between devices: 34.5 us -> 41.4 us
  waiting for transfers between devices: 25 us -> 29.9 us
  local copies, waits for them, and re-layouts: 0.81 us -> 2.35 us
  Pallas kernels: 31.7 us -> 33.2 us
    all_to_all x2 -> x1, blocking collectives: 31.4 us -> 17.5 us  [exchange(): lax.all_to_all(blocks, axis, split_axis=0, concat_axis=0, tiled=True, axi...]
    all_to_all x3 -> x4, waiting for transfers between devices: 16.1 us -> 25 us  [exchange(): lax.all_to_all(blocks, axis, split_axis=0, concat_axis=0, tiled=True, axi...]
    all_to_all x3 -> x4, starting transfers between devices: 28.9 us -> 35.7 us  [exchange(): lax.all_to_all(blocks, axis, split_axis=0, concat_axis=0, tiled=True, axi...]
    ppermute x2, waiting for transfers between devices: 8.88 us -> 4.84 us  [passed_along(): return lax.ppermute(shard, 'ctx', pairs)]
    unnamed x0 -> x4, local copies, waits for them, and re-layouts: none -> 1.54 us
    pallas_call x1 -> x2, Pallas kernels: 3.37 us -> 4.87 us  [the longest x1 4.03 us: per_device(): pl.pallas_call(back_kernel, in_specs=[at_vmem] * 4, out_specs=[at_hbm, at...]
  transfers between devices with their start and end apart: 5 -> 6, of which waited for: 3 -> 5; matrix products, arithmetic and copies ran while one was open for 0% -> 0% of each run, Pallas kernels for 14% -> 15%
where the time goes in v7:
time: 126 us; the launch traced here: 125 us
  starting transfers between devices  41.4 us (33%)
  Pallas kernels  33.2 us (26%)
  waiting for transfers between devices  29.9 us (24%)
  blocking collectives  17.5 us (14%)
  local copies, waits for them, and re-layouts  2.35 us (2%)
    all_to_all x4, starting transfers between devices, exchange(): lax.all_to_all(blocks, axis, split_axis=0, concat_axis=0, tiled=True, axi...  35.7 us
    all_to_all x4, waiting for transfers between devices, exchange(): lax.all_to_all(blocks, axis, split_axis=0, concat_axis=0, tiled=True, axi...  25 us
    all_to_all x1, blocking collectives, exchange(): lax.all_to_all(blocks, axis, split_axis=0, concat_axis=0, tiled=True, axi...  17.5 us
    pallas_call x2, Pallas kernels, local_sums(): pl.pallas_call(functools.partial(local_kernel, span, len(seg)), in_specs=...  7.11 us
    pallas_call x1, Pallas kernels, per_device(): pl.pallas_call(functools.partial(grad_kernel, share), in_specs=[at_hbm] *...  6.82 us
    ppermute x2, starting transfers between devices, passed_along(): return lax.ppermute(shard, 'ctx', pairs)  5.65 us
    pallas_call x1, Pallas kernels, per_device(): pl.pallas_call(mix_kernel, in_specs=[at_vmem] * 5, out_specs=[at_vmem] *...  4.89 us
    ppermute x2, waiting for transfers between devices, passed_along(): return lax.ppermute(shard, 'ctx', pairs)  4.84 us
  transfers between devices with their start and end apart: 6, of which 5 were waited for; matrix products, arithmetic and copies ran while one was open for 0% of the time, Pallas kernels for 15%

profile of v7, /device:TPU:1, one launch (start us, length us, event | category | flops | bytes accessed | tf_op | source)
XLA Modules:
  0.0 125.0 jit_solution(2173554566010707015)
XLA Ops:
  0.6 0.8 slice.3
  1.4 4.4 %collective-permute-start = (bf16[3,8,1024]{2,1,0:T(8,128)(2,1)S(1)}, bf16[3,8,1024]{2,1,0:T(8,128)(2,1)S(1)}, u32[]{:S(2)}, u32[]{:S(2)}) collective-permute-start(bf16[3,8,1024]{2,1,0:T(8,128)(2,1)S(1)} %slice.3), channel_id=1, source_target_pairs={{0,8},{8,16},{16,24},{24,32},{32,40},{40,48},{48,56},{56,64},{64,7... | collective-permute-start | bytes 147464 | tf_op jit(solution)/shard_map/ppermute | solution.py:538
  5.8 2.3 %load.1 = (f32[8,3,256,128]{3,2,1,0:T(8,128)S(1)}, f32[8,256,128]{2,1,0:T(8,128)S(1)}, f32[3,7,1024]{2,1,0:T(8,128)S(1)}, f32[16,1024]{1,0:T(8,128)S(1)}, f32[16,1024]{1,0:T(8,128)S(1)}) custom-call(bf16[3,256,1024]{2,1,0:T(8,128)(2,1)} %x_ref.3, bf16[256,1024]{1,0:T(8,128)(2,1)} %cot_ref.1, f32[3,7,1024]{2,1,0:T(8,128)} %filt_in.1, f32[16,1024]{1,0:T(8,128)} %rate_ref.1, ...), custom_call_target="tpu_custom_call" | custom-call | flops 524288000 | bytes 2097152 | tf_op jit(solution)/shard_map/load/pallas_call | solution.py:591
  8.1 0.0 collective-permute-done.prev_ref
  8.2 4.9 %mix.1 = (f32[8,256,128]{2,1,0:T(8,128)S(1)}, f32[8,256,128]{2,1,0:T(8,128)S(1)}, f32[32,8,128]{2,1,0:T(8,128)}) custom-call(f32[8,3,256,128]{3,2,1,0:T(8,128)S(1)} %get-tuple-element.41.held, bf16[3,8,1024]{2,1,0:T(8,128)(2,1)S(1)} %collective-permute-done.prev_ref, f32[8,256,128]{2,1,0:T(8,128)S(1)} %get-tuple-element.43.cot_ref.cot, ...), custom_call_target="tpu_custom_call" | custom-call | flops 28835840 | bytes 6291456 | tf_op jit(solution)/shard_map/mix/pallas_call | solution.py:609
  13.0 18.6 %all-to-all-start = ((f32[64,4,128]{2,1,0:T(4,128)}), f32[64,4,128]{2,1,0:T(4,128)S(1)}, u32[]{:S(2)}, u32[]{:S(2)}) async-start(f32[64,4,128]{2,1,0:T(4,128)} %bitcast.4), calls=%async_computation | async-start | bytes 262144 | tf_op jit(solution)/shard_map/all_to_all | solution.py:542
  31.6 1.4 %local.2 = (f32[8,256,128]{2,1,0:T(8,128)S(1)}, f32[8,256,128]{2,1,0:T(8,128)S(1)}, f32[8,2,16,8,128]{4,3,2,1,0:T(8,128)}) custom-call(f32[8,256,128]{2,1,0:T(8,128)S(1)} %get-tuple-element.49.gated, f32[8,256,128]{2,1,0:T(8,128)S(1)} %get-tuple-element.50.gradm, ...), custom_call_target="tpu_custom_call", output_to_operand_aliasing={{0}: (0, {}), {1}: (1, {})} | custom-call | flops 4194304 | bytes 4718592 | tf_op jit(solution)/shard_map/local/pallas_call | solution.py:646
  33.1 4.7 %stage.1 = (f32[8,3,304,128]{3,2,1,0:T(8,128)}, f32[8,2,256,128]{3,2,1,0:T(8,128)}) custom-call(bf16[3,256,1024]{2,1,0:T(8,128)(2,1)} %x_ref.3, f32[3,7,1024]{2,1,0:T(8,128)} %filt_in.1, bf16[3,8,1024]{2,1,0:T(8,128)(2,1)S(1)} %collective-permute-done.prev_ref), custom_call_target="tpu_custom_call" | custom-call | flops 524288000 | bytes 4718592 | tf_op jit(solution)/shard_map/stage/pallas_call | solution.py:625
  37.8 7.9 %all-to-all-done.arrived_ref = f32[64,4,128]{2,1,0:T(4,128)S(1)} async-done(((f32[64,4,128]{2,1,0:T(4,128)}), f32[64,4,128]{2,1,0:T(4,128)S(1)}, u32[]{:S(2)}, u32[]{:S(2)}) %all-to-all-start) | async-done | bytes 131104 | tf_op jit(solution)/shard_map/all_to_all | solution.py:542
  45.7 0.2 chain.1
  45.8 0.0 copy-start
  45.8 0.7 copy-done
  46.5 6.7 %all-to-all-start.1 = ((f32[64,4,128]{2,1,0:T(4,128)}), f32[64,4,128]{2,1,0:T(4,128)S(1)}, u32[]{:S(2)}, u32[]{:S(2)}) async-start(f32[64,4,128]{2,1,0:T(4,128)} %copy-done), calls=%async_computation.1 | async-start | bytes 262144 | tf_op jit(solution)/shard_map/all_to_all | solution.py:542
  53.2 5.7 %local.3 = (f32[8,256,128]{2,1,0:T(8,128)S(1)}, f32[8,256,128]{2,1,0:T(8,128)S(1)}, f32[8,2,16,8,128]{4,3,2,1,0:T(8,128)}) custom-call(f32[8,256,128]{2,1,0:T(8,128)S(1)} %get-tuple-element.56.gated, f32[8,256,128]{2,1,0:T(8,128)S(1)} %get-tuple-element.57.gradm, ...), custom_call_target="tpu_custom_call", output_to_operand_aliasing={{0}: (0, {}), {1}: (1, {}), {2}: (4, {})} | custom-call | flops 29360128 | bytes 4718592 | tf_op jit(solution)/shard_map/local/pallas_call | solution.py:646
  58.9 8.3 %all-to-all-done.1 = f32[64,4,128]{2,1,0:T(4,128)S(1)} async-done(((f32[64,4,128]{2,1,0:T(4,128)}), f32[64,4,128]{2,1,0:T(4,128)S(1)}, u32[]{:S(2)}, u32[]{:S(2)}) %all-to-all-start.1) | async-done | bytes 131104 | tf_op jit(solution)/shard_map/all_to_all | solution.py:542
  67.2 6.8 %grad.1 = (f32[8,256,128]{2,1,0:T(8,128)S(1)}, f32[8,256,128]{2,1,0:T(8,128)S(1)}, f32[8,256,128]{2,1,0:T(8,128)S(1)}, bf16[3,8,1024]{2,1,0:T(8,128)(2,1)S(1)}, f32[32,8,128]{2,1,0:T(8,128)}) custom-call(f32[8,3,304,128]{3,2,1,0:T(8,128)} %get-tuple-element.53.held_ref, ...), custom_call_target="tpu_custom_call", output_to_operand_aliasing={{0}: (3, {}), {1}: (4, {}), {2}: (5, {})} | custom-call | flops 28835840 | bytes 7864320 | tf_op jit(solution)/shard_map/grad/pallas_call | solution.py:695
  74.0 17.5 %all_to_all.25.part_ref = f32[32,8,128]{2,1,0:T(8,128)S(1)} all-to-all(f32[32,8,128]{2,1,0:T(8,128)} %get-tuple-element.64), channel_id=1, replica_groups={{0,1,2,3,4,5,6,7,128,129,130,131,132,133,134,135,256,257,258,259,260,26..., dimensions={0} | all-to-all | bytes 262144 | tf_op jit(solution)/shard_map/all_to_all | solution.py:542
  91.5 0.7 line.1
  92.2 3.5 %all-to-all-start.3 = ((bf16[16,48,128]{2,1,0:T(8,128)(2,1)}), bf16[16,48,128]{2,1,0:T(8,128)(2,1)S(1)}, u32[]{:S(2)}, u32[]{:S(2)}) async-start(bf16[16,48,128]{2,1,0:T(8,128)(2,1)} %line.1), calls=%async_computation.3 | async-start | bytes 393216 | tf_op jit(solution)/shard_map/all_to_all | solution.py:542
  95.7 1.3 %collective-permute-start.1 = (bf16[3,8,1024]{2,1,0:T(8,128)(2,1)S(1)}, bf16[3,8,1024]{2,1,0:T(8,128)(2,1)S(1)}, u32[]{:S(2)}, u32[]{:S(2)}) collective-permute-start(bf16[3,8,1024]{2,1,0:T(8,128)(2,1)S(1)} %get-tuple-element.69), channel_id=1, source_target_pairs={{8,0},{16,8},{24,16},{32,24},{40,32},{48,40},{56,48},{64,56},{72,6... | collective-permute-start | bytes 147464 | tf_op jit(solution)/shard_map/ppermute | solution.py:538
  97.0 4.0 %back.1 = (bf16[3,256,1024]{2,1,0:T(8,128)(2,1)}, f32[3,8,1024]{2,1,0:T(8,128)}) custom-call(f32[8,256,128]{2,1,0:T(8,128)S(1)} %get-tuple-element.65.query_mix, f32[8,256,128]{2,1,0:T(8,128)S(1)} %get-tuple-element.66.key_mix, f32[8,256,128]{2,1,0:T(8,128)S(1)} %get-tuple-element.67.value_mix, f32[3,7,1024]{2,1,0:T(8,128)S(1)} %get-tuple-element.44.filt_ref), custom_call_target="tpu_custom_call" | custom-call | flops 12582912 | bytes 3145728 | tf_op jit(solution)/shard_map/back/pallas_call | solution.py:732
  101.1 4.8 %collective-permute-done.1.next_ref = bf16[3,8,1024]{2,1,0:T(8,128)(2,1)S(1)} collective-permute-done((bf16[3,8,1024]{2,1,0:T(8,128)(2,1)S(1)}, bf16[3,8,1024]{2,1,0:T(8,128)(2,1)S(1)}, u32[]{:S(2)}, u32[]{:S(2)}) %collective-permute-start.1) | collective-permute-done | bytes 49184 | tf_op jit(solution)/shard_map/ppermute | solution.py:538
  105.9 3.0 %all-to-all-done.3.part_ref = bf16[16,48,128]{2,1,0:T(8,128)(2,1)S(1)} async-done(((bf16[16,48,128]{2,1,0:T(8,128)(2,1)}), bf16[16,48,128]{2,1,0:T(8,128)(2,1)S(1)}, u32[]{:S(2)}, u32[]{:S(2)}) %all-to-all-start.3) | async-done | bytes 196640 | tf_op jit(solution)/shard_map/all_to_all | solution.py:542
  108.9 0.8 plane.1
  109.8 6.9 %all-to-all-start.4 = ((f32[32,8,128]{2,1,0:T(8,128)}), f32[32,8,128]{2,1,0:T(8,128)S(1)}, u32[]{:S(2)}, u32[]{:S(2)}) async-start(f32[32,8,128]{2,1,0:T(8,128)} %plane.1), calls=%async_computation.4 | async-start | bytes 262144 | tf_op jit(solution)/shard_map/all_to_all | solution.py:542
  116.7 0.0 copy-start.1
  116.7 0.9 copy-done.1
  117.6 0.8 edge.1
  118.4 5.9 %all-to-all-done.4.sums_ref = f32[32,8,128]{2,1,0:T(8,128)S(1)} async-done(((f32[32,8,128]{2,1,0:T(8,128)}), f32[32,8,128]{2,1,0:T(8,128)S(1)}, u32[]{:S(2)}, u32[]{:S(2)}) %all-to-all-start.4) | async-done | bytes 131104 | tf_op jit(solution)/shard_map/all_to_all | solution.py:542
  124.3 0.7 scale.1
Async XLA Ops:
  1.4 6.7 %collective-permute-start = (bf16[3,8,1024]{2,1,0:T(8,128)(2,1)S(1)}, bf16[3,8,1024]{2,1,0:T(8,128)(2,1)S(1)}, u32[]{:S(2)}, u32[]{:S(2)}) collective-permute-start(bf16[3,8,1024]{2,1,0:T(8,128)(2,1)S(1)} %slice.3), channel_id=1, source_target_pairs={{0,8},{8,16},{16,24},{24,32},{32,40},{40,48},{48,56},{56,64},{64,7... | collective-permute-start | bytes 147464 | tf_op jit(solution)/shard_map/ppermute | solution.py:538
  13.0 32.6 %all-to-all-start = ((f32[64,4,128]{2,1,0:T(4,128)}), f32[64,4,128]{2,1,0:T(4,128)S(1)}, u32[]{:S(2)}, u32[]{:S(2)}) async-start(f32[64,4,128]{2,1,0:T(4,128)} %bitcast.4), calls=%async_computation | async-start | bytes 262144 | tf_op jit(solution)/shard_map/all_to_all | solution.py:542
  45.8 0.7 copy-start
  46.5 20.7 %all-to-all-start.1 = ((f32[64,4,128]{2,1,0:T(4,128)}), f32[64,4,128]{2,1,0:T(4,128)S(1)}, u32[]{:S(2)}, u32[]{:S(2)}) async-start(f32[64,4,128]{2,1,0:T(4,128)} %copy-done), calls=%async_computation.1 | async-start | bytes 262144 | tf_op jit(solution)/shard_map/all_to_all | solution.py:542
  92.2 16.7 %all-to-all-start.3 = ((bf16[16,48,128]{2,1,0:T(8,128)(2,1)}), bf16[16,48,128]{2,1,0:T(8,128)(2,1)S(1)}, u32[]{:S(2)}, u32[]{:S(2)}) async-start(bf16[16,48,128]{2,1,0:T(8,128)(2,1)} %line.1), calls=%async_computation.3 | async-start | bytes 393216 | tf_op jit(solution)/shard_map/all_to_all | solution.py:542
  95.7 10.2 %collective-permute-start.1 = (bf16[3,8,1024]{2,1,0:T(8,128)(2,1)S(1)}, bf16[3,8,1024]{2,1,0:T(8,128)(2,1)S(1)}, u32[]{:S(2)}, u32[]{:S(2)}) collective-permute-start(bf16[3,8,1024]{2,1,0:T(8,128)(2,1)S(1)} %get-tuple-element.69), channel_id=1, source_target_pairs={{8,0},{16,8},{24,16},{32,24},{40,32},{48,40},{56,48},{64,56},{72,6... | collective-permute-start | bytes 147464 | tf_op jit(solution)/shard_map/ppermute | solution.py:538
  109.8 14.5 %all-to-all-start.4 = ((f32[32,8,128]{2,1,0:T(8,128)}), f32[32,8,128]{2,1,0:T(8,128)S(1)}, u32[]{:S(2)}, u32[]{:S(2)}) async-start(f32[32,8,128]{2,1,0:T(8,128)} %plane.1), calls=%async_computation.4 | async-start | bytes 262144 | tf_op jit(solution)/shard_map/all_to_all | solution.py:542
  116.7 0.9 copy-start.1

commit v8 on v6

--- a/solution.py
+++ b/solution.py
@@ -704,6 +704,7 @@
         compiler_params=small,
         name="line",
     )(gathered)
+    own_sum, late = lax.optimization_barrier((own_sum, late))
     all_sums = exchange(own_sum, "ctx", line_members)
     grad_inputs = pl.pallas_call(
         back_kernel,

time: 125 us -> 127 us (1.016)
  blocking collectives: 31.4 us -> 16.2 us
  starting transfers between devices: 34.5 us -> 44.3 us
  waiting for transfers between devices: 25 us -> 32.3 us
    all_to_all x3 -> x4, waiting for transfers between devices: 16.1 us -> 32.3 us  [exchange(): lax.all_to_all(blocks, axis, split_axis=0, concat_axis=0, tiled=True, axi...]
    all_to_all x2 -> x1, blocking collectives: 31.4 us -> 16.2 us  [exchange(): lax.all_to_all(blocks, axis, split_axis=0, concat_axis=0, tiled=True, axi...]
    all_to_all x3 -> x4, starting transfers between devices: 28.9 us -> 38.7 us  [exchange(): lax.all_to_all(blocks, axis, split_axis=0, concat_axis=0, tiled=True, axi...]
    ppermute x2, waiting for transfers between devices: 8.88 us -> 0.01 us  [passed_along(): return lax.ppermute(shard, 'ctx', pairs)]
  transfers between devices with their start and end apart: 5 -> 6, of which waited for: 3 -> 4; matrix products, arithmetic and copies ran while one was open for 0% -> 0% of each run, Pallas kernels for 14% -> 14%
where the time goes in v8:
time: 127 us; the launch traced here: 126 us
  starting transfers between devices  44.3 us (35%)
  waiting for transfers between devices  32.3 us (25%)
  Pallas kernels  31.6 us (25%)
  blocking collectives  16.2 us (13%)
    all_to_all x4, starting transfers between devices, exchange(): lax.all_to_all(blocks, axis, split_axis=0, concat_axis=0, tiled=True, axi...  38.7 us
    all_to_all x4, waiting for transfers between devices, exchange(): lax.all_to_all(blocks, axis, split_axis=0, concat_axis=0, tiled=True, axi...  32.3 us
    all_to_all x1, blocking collectives, exchange(): lax.all_to_all(blocks, axis, split_axis=0, concat_axis=0, tiled=True, axi...  16.2 us
    pallas_call x2, Pallas kernels, local_sums(): pl.pallas_call(functools.partial(local_kernel, span, len(seg)), in_specs=...  7.11 us
    pallas_call x1, Pallas kernels, per_device(): pl.pallas_call(functools.partial(grad_kernel, share), in_specs=[at_hbm] *...  6.81 us
    ppermute x2, starting transfers between devices, passed_along(): return lax.ppermute(shard, 'ctx', pairs)  5.65 us
    pallas_call x1, Pallas kernels, per_device(): pl.pallas_call(mix_kernel, in_specs=[at_vmem] * 5, out_specs=[at_vmem] *...  4.88 us
    pallas_call x1, Pallas kernels, per_device(): pl.pallas_call(stage_kernel, in_specs=[at_hbm] * 2 + [at_vmem], out_specs...  4.74 us
  transfers between devices with their start and end apart: 6, of which 4 were waited for; matrix products, arithmetic and copies ran while one was open for 0% of the time, Pallas kernels for 14%

profile of v8, /device:TPU:1, one launch (start us, length us, event | category | flops | bytes accessed | tf_op | source)
XLA Modules:
  0.0 126.0 jit_solution(17606326615112948904)
XLA Ops:
  0.6 0.8 slice.3
  1.4 4.4 %collective-permute-start = (bf16[3,8,1024]{2,1,0:T(8,128)(2,1)S(1)}, bf16[3,8,1024]{2,1,0:T(8,128)(2,1)S(1)}, u32[]{:S(2)}, u32[]{:S(2)}) collective-permute-start(bf16[3,8,1024]{2,1,0:T(8,128)(2,1)S(1)} %slice.3), channel_id=1, source_target_pairs={{0,8},{8,16},{16,24},{24,32},{32,40},{40,48},{48,56},{56,64},{64,7... | collective-permute-start | bytes 147464 | tf_op jit(solution)/shard_map/ppermute | solution.py:514
  5.8 2.3 %load.1 = (f32[8,3,256,128]{3,2,1,0:T(8,128)S(1)}, f32[8,256,128]{2,1,0:T(8,128)S(1)}, f32[3,7,1024]{2,1,0:T(8,128)S(1)}, f32[16,1024]{1,0:T(8,128)S(1)}, f32[16,1024]{1,0:T(8,128)S(1)}) custom-call(bf16[3,256,1024]{2,1,0:T(8,128)(2,1)} %x_ref.3, bf16[256,1024]{1,0:T(8,128)(2,1)} %cot_ref.1, f32[3,7,1024]{2,1,0:T(8,128)} %filt_in.1, f32[16,1024]{1,0:T(8,128)} %rate_ref.1, ...), custom_call_target="tpu_custom_call" | custom-call | flops 524288000 | bytes 2097152 | tf_op jit(solution)/shard_map/load/pallas_call | solution.py:567
  8.1 0.0 collective-permute-done.prev_ref
  8.2 4.9 %mix.1 = (f32[8,256,128]{2,1,0:T(8,128)S(1)}, f32[8,256,128]{2,1,0:T(8,128)S(1)}, f32[32,8,128]{2,1,0:T(8,128)}) custom-call(f32[8,3,256,128]{3,2,1,0:T(8,128)S(1)} %get-tuple-element.38.held, bf16[3,8,1024]{2,1,0:T(8,128)(2,1)S(1)} %collective-permute-done.prev_ref, f32[8,256,128]{2,1,0:T(8,128)S(1)} %get-tuple-element.40.cot_ref.cot, ...), custom_call_target="tpu_custom_call" | custom-call | flops 28835840 | bytes 6291456 | tf_op jit(solution)/shard_map/mix/pallas_call | solution.py:585
  13.0 18.6 %all-to-all-start = ((f32[64,4,128]{2,1,0:T(4,128)}), f32[64,4,128]{2,1,0:T(4,128)S(1)}, u32[]{:S(2)}, u32[]{:S(2)}) async-start(f32[64,4,128]{2,1,0:T(4,128)} %bitcast.4), calls=%async_computation | async-start | bytes 262144 | tf_op jit(solution)/shard_map/all_to_all | solution.py:518
  31.6 1.4 %local.2 = (f32[8,256,128]{2,1,0:T(8,128)S(1)}, f32[8,256,128]{2,1,0:T(8,128)S(1)}, f32[8,2,16,8,128]{4,3,2,1,0:T(8,128)}) custom-call(f32[8,256,128]{2,1,0:T(8,128)S(1)} %get-tuple-element.46.gated, f32[8,256,128]{2,1,0:T(8,128)S(1)} %get-tuple-element.47.gradm, ...), custom_call_target="tpu_custom_call", output_to_operand_aliasing={{0}: (0, {}), {1}: (1, {})} | custom-call | flops 4194304 | bytes 4718592 | tf_op jit(solution)/shard_map/local/pallas_call | solution.py:622
  33.1 4.7 %stage.1 = (f32[8,3,304,128]{3,2,1,0:T(8,128)}, f32[8,2,256,128]{3,2,1,0:T(8,128)}) custom-call(bf16[3,256,1024]{2,1,0:T(8,128)(2,1)} %x_ref.3, f32[3,7,1024]{2,1,0:T(8,128)} %filt_in.1, bf16[3,8,1024]{2,1,0:T(8,128)(2,1)S(1)} %collective-permute-done.prev_ref), custom_call_target="tpu_custom_call" | custom-call | flops 524288000 | bytes 4718592 | tf_op jit(solution)/shard_map/stage/pallas_call | solution.py:601
  37.8 7.8 %all-to-all-done.arrived_ref = f32[64,4,128]{2,1,0:T(4,128)S(1)} async-done(((f32[64,4,128]{2,1,0:T(4,128)}), f32[64,4,128]{2,1,0:T(4,128)S(1)}, u32[]{:S(2)}, u32[]{:S(2)}) %all-to-all-start) | async-done | bytes 131104 | tf_op jit(solution)/shard_map/all_to_all | solution.py:518
  45.7 0.8 chain.1
  46.5 6.8 %all-to-all-start.1 = ((f32[64,4,128]{2,1,0:T(4,128)}), f32[64,4,128]{2,1,0:T(4,128)S(1)}, u32[]{:S(2)}, u32[]{:S(2)}) async-start(f32[64,4,128]{2,1,0:T(4,128)} %chain.1), calls=%async_computation.1 | async-start | bytes 262144 | tf_op jit(solution)/shard_map/all_to_all | solution.py:518
  53.2 5.7 %local.3 = (f32[8,256,128]{2,1,0:T(8,128)S(1)}, f32[8,256,128]{2,1,0:T(8,128)S(1)}, f32[8,2,16,8,128]{4,3,2,1,0:T(8,128)}) custom-call(f32[8,256,128]{2,1,0:T(8,128)S(1)} %get-tuple-element.53.gated, f32[8,256,128]{2,1,0:T(8,128)S(1)} %get-tuple-element.54.gradm, ...), custom_call_target="tpu_custom_call", output_to_operand_aliasing={{0}: (0, {}), {1}: (1, {}), {2}: (4, {})} | custom-call | flops 29360128 | bytes 4718592 | tf_op jit(solution)/shard_map/local/pallas_call | solution.py:622
  58.9 8.3 %all-to-all-done.1 = f32[64,4,128]{2,1,0:T(4,128)S(1)} async-done(((f32[64,4,128]{2,1,0:T(4,128)}), f32[64,4,128]{2,1,0:T(4,128)S(1)}, u32[]{:S(2)}, u32[]{:S(2)}) %all-to-all-start.1) | async-done | bytes 131104 | tf_op jit(solution)/shard_map/all_to_all | solution.py:518
  67.2 6.8 %grad.1 = (f32[8,256,128]{2,1,0:T(8,128)S(1)}, f32[8,256,128]{2,1,0:T(8,128)S(1)}, f32[8,256,128]{2,1,0:T(8,128)S(1)}, bf16[3,8,1024]{2,1,0:T(8,128)(2,1)S(1)}, f32[32,8,128]{2,1,0:T(8,128)}) custom-call(f32[8,3,304,128]{3,2,1,0:T(8,128)} %get-tuple-element.50.held_ref, ...), custom_call_target="tpu_custom_call", output_to_operand_aliasing={{0}: (3, {}), {1}: (4, {}), {2}: (5, {})} | custom-call | flops 28835840 | bytes 7864320 | tf_op jit(solution)/shard_map/grad/pallas_call | solution.py:671
  74.0 9.8 %all-to-all-start.2 = ((f32[32,8,128]{2,1,0:T(8,128)}), f32[32,8,128]{2,1,0:T(8,128)S(1)}, u32[]{:S(2)}, u32[]{:S(2)}) async-start(f32[32,8,128]{2,1,0:T(8,128)} %get-tuple-element.61), calls=%async_computation.2 | async-start | bytes 262144 | tf_op jit(solution)/shard_map/all_to_all | solution.py:518
  83.8 1.3 %collective-permute-start.1 = (bf16[3,8,1024]{2,1,0:T(8,128)(2,1)S(1)}, bf16[3,8,1024]{2,1,0:T(8,128)(2,1)S(1)}, u32[]{:S(2)}, u32[]{:S(2)}) collective-permute-start(bf16[3,8,1024]{2,1,0:T(8,128)(2,1)S(1)} %get-tuple-element.62), channel_id=1, source_target_pairs={{8,0},{16,8},{24,16},{32,24},{40,32},{48,40},{56,48},{64,56},{72,6... | collective-permute-start | bytes 147464 | tf_op jit(solution)/shard_map/ppermute | solution.py:514
  85.1 6.3 %all-to-all-done.2.part_ref = f32[32,8,128]{2,1,0:T(8,128)S(1)} async-done(((f32[32,8,128]{2,1,0:T(8,128)}), f32[32,8,128]{2,1,0:T(8,128)S(1)}, u32[]{:S(2)}, u32[]{:S(2)}) %all-to-all-start.2) | async-done | bytes 131104 | tf_op jit(solution)/shard_map/all_to_all | solution.py:518
  91.5 0.7 line.1
  92.2 0.0 collective-permute-done.1.next_ref
  92.2 3.5 %all-to-all-start.3 = ((bf16[16,48,128]{2,1,0:T(8,128)(2,1)}), bf16[16,48,128]{2,1,0:T(8,128)(2,1)S(1)}, u32[]{:S(2)}, u32[]{:S(2)}) async-start(bf16[16,48,128]{2,1,0:T(8,128)(2,1)} %line.1), calls=%async_computation.3 | async-start | bytes 393216 | tf_op jit(solution)/shard_map/all_to_all | solution.py:518
  95.7 3.4 %back.1 = bf16[3,256,1024]{2,1,0:T(8,128)(2,1)} custom-call(f32[8,256,128]{2,1,0:T(8,128)S(1)} %get-tuple-element.64.query_mix, f32[8,256,128]{2,1,0:T(8,128)S(1)} %get-tuple-element.65.key_mix, f32[8,256,128]{2,1,0:T(8,128)S(1)} %get-tuple-element.66.value_mix, bf16[3,8,1024]{2,1,0:T(8,128)(2,1)S(1)} %collective-permute-done.1.next_ref, ...), custom_call_target="tpu_custom_call" | custom-call | flops 12582912 | bytes 3145728 | tf_op jit(solution)/shard_map/back/pallas_call | solution.py:709
  99.1 9.8 %all-to-all-done.3.part_ref = bf16[16,48,128]{2,1,0:T(8,128)(2,1)S(1)} async-done(((bf16[16,48,128]{2,1,0:T(8,128)(2,1)}), bf16[16,48,128]{2,1,0:T(8,128)(2,1)S(1)}, u32[]{:S(2)}, u32[]{:S(2)}) %all-to-all-start.3) | async-done | bytes 196640 | tf_op jit(solution)/shard_map/all_to_all | solution.py:518
  108.9 0.2 plane.1
  109.1 16.2 %all_to_all.25.sums_ref = f32[32,8,128]{2,1,0:T(8,128)S(1)} all-to-all(f32[32,8,128]{2,1,0:T(8,128)S(1)} %plane.1), channel_id=1, replica_groups={{0,1,2,3,4,5,6,7,128,129,130,131,132,133,134,135,256,257,258,259,260,26..., dimensions={0} | all-to-all | bytes 262144 | tf_op jit(solution)/shard_map/all_to_all | solution.py:518
  125.3 0.7 scale.1
Async XLA Ops:
  1.4 6.7 %collective-permute-start = (bf16[3,8,1024]{2,1,0:T(8,128)(2,1)S(1)}, bf16[3,8,1024]{2,1,0:T(8,128)(2,1)S(1)}, u32[]{:S(2)}, u32[]{:S(2)}) collective-permute-start(bf16[3,8,1024]{2,1,0:T(8,128)(2,1)S(1)} %slice.3), channel_id=1, source_target_pairs={{0,8},{8,16},{16,24},{24,32},{32,40},{40,48},{48,56},{56,64},{64,7... | collective-permute-start | bytes 147464 | tf_op jit(solution)/shard_map/ppermute | solution.py:514
  13.0 32.6 %all-to-all-start = ((f32[64,4,128]{2,1,0:T(4,128)}), f32[64,4,128]{2,1,0:T(4,128)S(1)}, u32[]{:S(2)}, u32[]{:S(2)}) async-start(f32[64,4,128]{2,1,0:T(4,128)} %bitcast.4), calls=%async_computation | async-start | bytes 262144 | tf_op jit(solution)/shard_map/all_to_all | solution.py:518
  46.5 20.7 %all-to-all-start.1 = ((f32[64,4,128]{2,1,0:T(4,128)}), f32[64,4,128]{2,1,0:T(4,128)S(1)}, u32[]{:S(2)}, u32[]{:S(2)}) async-start(f32[64,4,128]{2,1,0:T(4,128)} %chain.1), calls=%async_computation.1 | async-start | bytes 262144 | tf_op jit(solution)/shard_map/all_to_all | solution.py:518
  74.0 17.4 %all-to-all-start.2 = ((f32[32,8,128]{2,1,0:T(8,128)}), f32[32,8,128]{2,1,0:T(8,128)S(1)}, u32[]{:S(2)}, u32[]{:S(2)}) async-start(f32[32,8,128]{2,1,0:T(8,128)} %get-tuple-element.61), calls=%async_computation.2 | async-start | bytes 262144 | tf_op jit(solution)/shard_map/all_to_all | solution.py:518
  83.8 8.3 %collective-permute-start.1 = (bf16[3,8,1024]{2,1,0:T(8,128)(2,1)S(1)}, bf16[3,8,1024]{2,1,0:T(8,128)(2,1)S(1)}, u32[]{:S(2)}, u32[]{:S(2)}) collective-permute-start(bf16[3,8,1024]{2,1,0:T(8,128)(2,1)S(1)} %get-tuple-element.62), channel_id=1, source_target_pairs={{8,0},{16,8},{24,16},{32,24},{40,32},{48,40},{56,48},{64,56},{72,6... | collective-permute-start | bytes 147464 | tf_op jit(solution)/shard_map/ppermute | solution.py:514
  92.2 16.7 %all-to-all-start.3 = ((bf16[16,48,128]{2,1,0:T(8,128)(2,1)}), bf16[16,48,128]{2,1,0:T(8,128)(2,1)S(1)}, u32[]{:S(2)}, u32[]{:S(2)}) async-start(bf16[16,48,128]{2,1,0:T(8,128)(2,1)} %line.1), calls=%async_computation.3 | async-start | bytes 393216 | tf_op jit(solution)/shard_map/all_to_all | solution.py:518
